TPU v7x, 32 devices: a whole 2x2x4 slice. The times are simulated.
32 devices in a mesh: dp: 8 (over y, x, core), tensor: 4 (over z).
Axes of the slice: x: 2, y: 2, z: 4, core: 2. Of those that a mesh axis runs over, the one named last changes fastest.
Arguments:
- inputs_x: bfloat16 [1024, 4096], P('dp', 'tensor'), may hold values from -6 to 6
- hidden: bfloat16 [1024, 14336], P('dp', 'tensor'), may hold values from -6 to 6
- grad_up: bfloat16 [1024, 14336], P('dp', 'tensor'), may hold values from -6 to 6
- grad_down: bfloat16 [1024, 4096], P('dp', 'tensor'), may hold values from -6 to 6
- proj_in_up: bfloat16 [4096, 64], P('tensor'), may hold values from -0.09375 to 0.09375
- proj_in_down: bfloat16 [14336, 64], P('tensor'), may hold values from -0.046875 to 0.046875
- proj_out_up: bfloat16 [14336, 64], P('tensor'), may hold values from -0.046875 to 0.046875
- proj_out_down: bfloat16 [4096, 64], P('tensor'), may hold values from -0.09375 to 0.09375
- lengths: int32 [16], P('dp'), may hold values from 16 to 64
- stored_grads: bfloat16 [208, 8192], P('dp', 'tensor'), may hold values from -6 to 6
Outputs:
- gram: bfloat16 [8192, 8, 1024], P('tensor', 'dp')
All inputs are finite; a program needn't handle non-finite values.
Results may differ from a plain program's by a relative error of at most 0.0034.
Values may be sent and summed in bfloat16 or wider, within the bound.
No kernel may reach another device: no remote copies, remote signals or barrier semaphores. Data moves between devices by JAX's collectives and lax.ppermute only.
A program may use at most 64 MiB of HBM per device.

v0:
```python
import math

import jax
import jax.numpy as jnp
from jax import lax
from jax.sharding import PartitionSpec as P


def matmul(left, right):
    return jnp.dot(left, right, preferred_element_type=jnp.float32)


def local(
    inputs_x,
    hidden,
    grad_up,
    grad_down,
    proj_in_up,
    proj_in_down,
    proj_out_up,
    proj_out_down,
    lengths,
    stored_grads,
):
    examples = lengths.shape[0]
    slot_count = inputs_x.shape[0] // examples
    proj_width = proj_in_up.shape[1]
    tensor_count = lax.axis_size("tensor")
    out_share = proj_width // tensor_count
    tensor_index = lax.axis_index("tensor")
    layers = 2
    terms_in = jnp.stack([matmul(inputs_x, proj_in_up), matmul(hidden, proj_in_down)])
    terms_out = jnp.stack([matmul(grad_up, proj_out_up), matmul(grad_down, proj_out_down)])
    summed_in, summed_out = lax.psum((terms_in, terms_out), "tensor")
    summed_out = lax.dynamic_slice_in_dim(summed_out, tensor_index * out_share, out_share, 2)
    live_mask = (jnp.arange(slot_count, dtype=jnp.int32)[None, :] < lengths[:, None]).astype(
        jnp.float32
    )
    in_proj = summed_in.reshape(layers, examples, slot_count, proj_width).transpose(1, 2, 0, 3)
    out_proj = summed_out.reshape(layers, examples, slot_count, out_share).transpose(1, 2, 0, 3)
    out_proj = out_proj * live_mask[:, :, None, None]
    current = jnp.einsum("esla,eslb->ealb", out_proj, in_proj, precision=lax.Precision.HIGHEST)
    current = (current * (1.0 / math.sqrt(slot_count))).reshape(
        examples, out_share * layers * proj_width
    )
    local_rows = jnp.concatenate([current.astype(jnp.bfloat16), stored_grads], axis=0)
    row_count = local_rows.shape[0]
    quarter = local_rows.shape[1]
    dp_count = lax.axis_size("dp")
    sub_width = quarter // dp_count
    every_count = row_count * dp_count
    everything = lax.all_gather(local_rows, "dp", axis=0, tiled=True)
    column_block = lax.dynamic_slice_in_dim(
        everything, lax.axis_index("dp") * sub_width, sub_width, 1
    )
    columns = lax.all_gather(column_block, "tensor", axis=1, tiled=True)
    product = lax.dot_general(
        everything, columns, (((0,), (0,)), ((), ())), preferred_element_type=jnp.float32
    )
    product = product * (1.0 / math.sqrt(every_count))
    return product.astype(jnp.bfloat16).reshape(quarter, 1, columns.shape[1])


def solution(mesh):
    in_specs = (
        P("dp", "tensor"),
        P("dp", "tensor"),
        P("dp", "tensor"),
        P("dp", "tensor"),
        P("tensor", None),
        P("tensor", None),
        P("tensor", None),
        P("tensor", None),
        P("dp"),
        P("dp", "tensor"),
    )
    out_specs = P("tensor", "dp", None)
    return jax.shard_map(local, mesh=mesh, in_specs=in_specs, out_specs=out_specs, check_vma=False)
```

profile of v0, /device:TPU:0, one launch (start us, length us, event | category | flops | bytes accessed | tf_op | source)
XLA Modules:
  0.0 90.2 jit_solution(6700811130995102947)
XLA Ops:
  6.5 0.0 copy-start
  6.5 0.0 copy-start.2
  6.5 0.0 copy-start.1
  6.5 0.0 all-reduce.3.cloned.1.call-start
  6.5 1.3 %convolution_bitcast_fusion.3 = f32[1,128,64]{1,2,0:T(8,128)S(1)} fusion(bf16[128,1024]{1,0:T(8,128)(2,1)} %param.10, bf16[1024,64]{0,1:T(8,128)(2,1)} %param.14), kind=kOutput, calls=%fused_computation.6 | convolution fusion | flops 16777216 | bytes 425984 | tf_op jit(solution)/shard_map/dot_general | solution.py:10
  7.8 0.0 copy-done
  7.9 1.4 %convolution_bitcast_fusion.1 = f32[1,128,64]{1,2,0:T(8,128)S(1)} fusion(bf16[128,3584]{1,0:T(8,128)(2,1)S(1)} %copy-done, bf16[3584,64]{0,1:T(8,128)(2,1)} %param.15), kind=kOutput, calls=%fused_computation.3 | convolution fusion | flops 58720256 | bytes 1409024 | tf_op jit(solution)/shard_map/dot_general | solution.py:10
  9.3 0.1 reshape.33
  9.4 0.8 copy.15
  10.2 1.7 %convolution_bitcast_fusion = f32[1,128,64]{1,2,0:T(8,128)S(1)} fusion(bf16[128,3584]{1,0:T(8,128)(2,1)} %param.12, bf16[3584,64]{0,1:T(8,128)(2,1)} %param.16), kind=kOutput, calls=%fused_computation.2 | convolution fusion | flops 58720256 | bytes 1409024 | tf_op jit(solution)/shard_map/dot_general | solution.py:10
  11.9 1.2 %convolution_bitcast_fusion.2 = f32[1,128,64]{1,2,0:T(8,128)S(1)} fusion(bf16[128,1024]{1,0:T(8,128)(2,1)} %param.13, bf16[1024,64]{0,1:T(8,128)(2,1)} %param.17), kind=kOutput, calls=%fused_computation.5 | convolution fusion | flops 16777216 | bytes 425984 | tf_op jit(solution)/shard_map/dot_general | solution.py:10
  13.1 0.6 pad_maximum_fusion.1
  13.8 0.0 all-reduce.3.cloned.1.call-update
  13.8 0.0 copy-done.2
  13.8 0.1 compare_convert_fusion
  13.9 37.9 %all-reduce.3.cloned.1.call-done = (f32[2,64,2,64]{3,1,2,0:T(8,128)}, f32[2,128,64]{1,2,0:T(8,128)}) async-done(((f32[2,64,2,64]{3,1,2,0:T(8,128)}, f32[2,128,64]{1,2,0:T(8,128)}), (f32[2,64,2,64]{3,1,2,0:T(8,128)}, f32[2,128,64]{1,2,0:T(8,128)})) %all-reduce.3.cloned.1.call-update) | async-done | bytes 131088 | tf_op jit(solution)/shard_map/psum | solution.py:34
  51.7 0.7 constant_dynamic-slice_fusion.1
  52.4 0.1 reshape.34
  52.5 1.1 %fusion.2 = bf16[2,16,2,64]{3,1,2,0:T(8,128)(2,1)S(1)} fusion(f32[2,64,2,64]{3,1,2,0:T(8,128)} %get-tuple-element.5, f32[2,64,2,16]{1,0,3,2:T(2,128)S(1)} %multiply_bitcast_fusion), kind=kOutput, calls=%fused_computation.8 | convolution fusion | flops 3153920 | bytes 90112 | tf_op jit(solution)/shard_map/esla,eslb->ealb/dot_general | solution.py:42
  53.7 0.1 convert_element_type.22
  53.8 0.0 copy-done.1
  53.9 10.9 %all-gather = bf16[8,28,2048]{2,1,0:T(8,128)(2,1)S(1)} all-gather(bf16[1,28,2048]{2,1,0:T(8,128)(2,1)S(1)} %maximum_bitcast_fusion), channel_id=1, replica_groups=mesh['dp'=8,'tensor'=4] {'dp'}, dimensions={0}, use_global_device_ids=true | all-gather | bytes 1032192 | tf_op jit(solution)/shard_map/all_gather | solution.py:52
  64.7 0.2 reshape.37
  64.9 15.1 %all_gather.7 = bf16[224,1024]{1,0:T(8,128)(2,1)S(1)} all-gather(bf16[224,256]{1,0:T(8,128)(2,1)S(1)} %constant_dynamic-slice_fusion), channel_id=1, replica_groups=mesh['dp'=8,'tensor'=4] {'tensor'}, dimensions={1}, use_global_device_ids=true | all-gather | bytes 573440 | tf_op jit(solution)/shard_map/all_gather | solution.py:56
  80.0 3.3 %fusion = bf16[2048,1,1024]{2,0,1:T(8,128)(2,1)} fusion(bf16[224,2048]{1,0:T(8,128)(2,1)S(1)} %reshape.37, bf16[224,1024]{1,0:T(8,128)(2,1)S(1)} %all_gather.7), kind=kOutput, calls=%fused_computation.1 | convolution fusion | flops 943718400 | bytes 5570560 | tf_op jit(solution)/shard_map/dot_general | solution.py:57
  (5 shorter events, 0.1 us)
Async XLA Ops:
  6.5 1.3 %copy-start = (bf16[128,3584]{1,0:T(8,128)(2,1)S(1)}, bf16[128,3584]{1,0:T(8,128)(2,1)}, u32[]{:S(2)}) copy-start(bf16[128,3584]{1,0:T(8,128)(2,1)} %param.11) | copy-start | bytes 2752516
  6.5 7.2 %copy-start.2 = (s32[2]{0:T(128)S(1)}, s32[2]{0:T(128)}, u32[]{:S(2)}) copy-start(s32[2]{0:T(128)} %param.18) | copy-start | bytes 28
  6.5 47.3 %copy-start.1 = (bf16[26,2048]{1,0:T(8,128)(2,1)S(1)}, bf16[26,2048]{1,0:T(8,128)(2,1)}, u32[]{:S(2)}) copy-start(bf16[26,2048]{1,0:T(8,128)(2,1)} %param.19) | copy-start | bytes 319492
  6.5 45.2 %all-reduce.3.cloned.1.call-start = ((), (), s32[]{:S(2)}) async-start(), calls=%async_computation | async-start | bytes 393216 | tf_op jit(solution)/shard_map/psum | solution.py:34
Sparse Core Ops, SparseCore 0:
  13.9 37.7 all-reduce.2
where the time goes:
time: 90.5 us; the launch traced here: 90.2 us
  waiting for transfers between devices  37.9 us (42%)
  blocking collectives  25.9 us (29%)
  between operations  13.5 us (15%)
  matrix products  10.1 us (11%)
  local copies, waits for them, and re-layouts  2.04 us (2%)
    psum x1, waiting for transfers between devices, local(): summed_in, summed_out = lax.psum((terms_in, terms_out), 'tensor')  37.9 us
    all_gather x1, blocking collectives, local(): columns = lax.all_gather(column_block, 'tensor', axis=1, tiled=True)  15.1 us
    all_gather x1, blocking collectives, local(): everything = lax.all_gather(local_rows, 'dp', axis=0, tiled=True)  10.9 us
    dot_general x4, matrix products, matmul(): return jnp.dot(left, right, preferred_element_type=jnp.float32)  5.6 us
    dot_general x1, matrix products, local(): lax.dot_general(everything, columns, (((0,), (0,)), ((), ())), preferred_...  3.32 us
  transfers between devices with their start and end apart: 1, of which 1 were waited for; matrix products, arithmetic and copies ran while one was open for 0% of the time, Pallas kernels for 0%

commit v1 on v0

--- a/solution.py
+++ b/solution.py
@@ -1,16 +1,255 @@
+import functools
 import math
 
 import jax
 import jax.numpy as jnp
 from jax import lax
+from jax.experimental import pallas as pl
+from jax.experimental.pallas import tpu as pltpu
 from jax.sharding import PartitionSpec as P
+
+LAYERS = 2
+LANES = 128
+SLOT = 16
 
 
 def matmul(left, right):
     return jnp.dot(left, right, preferred_element_type=jnp.float32)
 
 
+def power_of_two(n):
+    return n & (n - 1) == 0
+
+
+def bits_of(n):
+    return [1 << k for k in range(n.bit_length() - 1)]
+
+
+def swap(value, axis, bit):
+    count = lax.axis_size(axis)
+    return lax.ppermute(value, axis, [(i, i ^ bit) for i in range(count)])
+
+
+def project_kernel(x, h, gu, gd, pu, pd, ou, od, out, *scratch):
+    ins = (x, h, gu, gd, pu, pd, ou, od)
+    bufs, sem = scratch[:8], scratch[8]
+    order = (4, 0, 7, 3, 5, 1, 6, 2)
+    copies = {}
+    for n in order:
+        copies[n] = pltpu.make_async_copy(ins[n], bufs[n], sem.at[n])
+        copies[n].start()
+
+    def product(left, right):
+        copies[right].wait()
+        copies[left].wait()
+        return lax.dot_general(
+            bufs[left][...],
+            bufs[right][...],
+            (((1,), (1,)), ((), ())),
+            preferred_element_type=jnp.float32,
+        )
+
+    rows = x.shape[0]
+    in_up = product(0, 4)
+    out_down = product(3, 7)
+    in_down = product(1, 5)
+    out[:rows, :] = jnp.concatenate([in_up, in_down], axis=1)
+    out_up = product(2, 6)
+    out[rows:, :] = jnp.concatenate([out_up, out_down], axis=1)
+
+
+def project(x, h, gu, gd, pu, pd, ou, od):
+    args = (x, h, gu, gd, pu.T, pd.T, ou.T, od.T)
+    rows = x.shape[0]
+    width = LAYERS * pu.shape[1]
+    return pl.pallas_call(
+        project_kernel,
+        out_shape=jax.ShapeDtypeStruct((2 * rows, width), jnp.float32),
+        in_specs=[pl.BlockSpec(memory_space=pl.ANY)] * 8,
+        out_specs=pl.BlockSpec(memory_space=pltpu.VMEM),
+        scratch_shapes=[pltpu.VMEM(a.shape, a.dtype) for a in args]
+        + [pltpu.SemaphoreType.DMA((8,))],
+        cost_estimate=pl.CostEstimate(
+            flops=2 * sum(math.prod(a.shape) for a in args[:4]) * pu.shape[1],
+            bytes_accessed=2 * sum(math.prod(a.shape) for a in args),
+            transcendentals=0,
+        ),
+        name="project",
+    )(*args)
+
+
+def current_kernel(lengths, own, other, out):
+    examples, half, width = out.shape
+    total = own[...] + other[...]
+    rows = total.shape[0] // 2
+    slots = rows // examples
+    position = lax.broadcasted_iota(jnp.int32, (slots, width), 0)
+    lane = lax.broadcasted_iota(jnp.int32, (half, width), 1)
+    for e in range(examples):
+        left = total[rows + e * slots : rows + (e + 1) * slots]
+        right = total[e * slots : (e + 1) * slots]
+        left = left * (position < lengths[e]).astype(jnp.float32)
+        both = lax.dot_general(
+            left,
+            right,
+            (((0,), (0,)), ((), ())),
+            precision=lax.Precision.HIGHEST,
+            preferred_element_type=jnp.float32,
+        )
+        mine = jnp.where(lane < half, both[:half], both[half:])
+        out[e] = (mine * (1.0 / math.sqrt(slots))).astype(out.dtype)
+
+
+def current_rows(lengths, own, other, proj_width):
+    examples = lengths.shape[0]
+    return pl.pallas_call(
+        current_kernel,
+        out_shape=jax.ShapeDtypeStruct(
+            (examples, proj_width, LAYERS * proj_width), jnp.bfloat16
+        ),
+        in_specs=[
+            pl.BlockSpec(memory_space=pltpu.SMEM),
+            pl.BlockSpec(memory_space=pltpu.VMEM),
+            pl.BlockSpec(memory_space=pltpu.VMEM),
+        ],
+        out_specs=pl.BlockSpec(memory_space=pltpu.VMEM),
+        cost_estimate=pl.CostEstimate(
+            flops=2 * examples * 64 * width_flops(proj_width),
+            bytes_accessed=own.size * 8,
+            transcendentals=0,
+        ),
+        name="current",
+    )(lengths, own, other)
+
+
+def width_flops(proj_width):
+    return (LAYERS * proj_width) ** 2
+
+
+def gram_kernel(scale, offsets, place, stored, cols, cur, out, left, right, buf, sem):
+    pieces, old, quarter = stored.shape
+    new = cur.shape[1]
+    sub = cols.shape[-1]
+    slot = left.shape[0] // pieces
+    q, i = place[0], place[1]
+    left[...] = jnp.zeros_like(left)
+    right[...] = jnp.zeros_like(right)
+    for p in range(pieces):
+        left[p * slot : p * slot + old, :] = stored[p]
+        left[p * slot + old : p * slot + old + new, :] = cur[
+            p, :, pl.ds(pl.multiple_of(q * quarter, quarter), quarter)
+        ]
+    for k, off in enumerate(offsets):
+        to = pl.multiple_of((q ^ off) * sub, sub)
+        source = pl.multiple_of((q ^ off) * quarter + i * sub, sub)
+        for p in range(pieces):
+            right[p * slot : p * slot + old, pl.ds(to, sub)] = cols[k, p]
+            right[p * slot + old : p * slot + old + new, pl.ds(to, sub)] = cur[
+                p, :, pl.ds(source, sub)
+            ]
+    chunk = buf.shape[1]
+    copies = []
+    for m in range(buf.shape[0]):
+        product = lax.dot_general(
+            left[:, m * chunk : (m + 1) * chunk],
+            right[...],
+            (((0,), (0,)), ((), ())),
+            preferred_element_type=jnp.float32,
+        )
+        buf[m] = (product * scale).astype(buf.dtype)
+        copies.append(
+            pltpu.make_async_copy(
+                buf.at[m], out.at[pl.ds(m * chunk, chunk)], sem.at[m]
+            )
+        )
+        copies[-1].start()
+    for copy in copies:
+        copy.wait()
+
+
+def gram(stored, cols, cur, place, offsets):
+    pieces, old, quarter = stored.shape
+    new = cur.shape[1]
+    slot = -(-(old + new) // SLOT) * SLOT
+    width = cols.shape[0] * cols.shape[-1]
+    chunk = 256 if quarter % 256 == 0 else quarter
+    scale = 1.0 / math.sqrt(pieces * (old + new))
+    return pl.pallas_call(
+        functools.partial(gram_kernel, scale, offsets),
+        out_shape=jax.ShapeDtypeStruct((quarter, width), jnp.bfloat16),
+        in_specs=[pl.BlockSpec(memory_space=pltpu.SMEM)]
+        + [pl.BlockSpec(memory_space=pltpu.VMEM)] * 3,
+        out_specs=pl.BlockSpec(memory_space=pl.ANY),
+        scratch_shapes=[
+            pltpu.VMEM((pieces * slot, quarter), jnp.bfloat16),
+            pltpu.VMEM((pieces * slot, width), jnp.bfloat16),
+            pltpu.VMEM((quarter // chunk, chunk, width), jnp.bfloat16),
+            pltpu.SemaphoreType.DMA((quarter // chunk,)),
+        ],
+        cost_estimate=pl.CostEstimate(
+            flops=2 * pieces * slot * quarter * width,
+            bytes_accessed=2 * quarter * width,
+            transcendentals=0,
+        ),
+        name="gram",
+    )(place, stored, cols, cur)
+
+
 def local(
+    inputs_x,
+    hidden,
+    grad_up,
+    grad_down,
+    proj_in_up,
+    proj_in_down,
+    proj_out_up,
+    proj_out_down,
+    lengths,
+    stored_grads,
+):
+    examples = lengths.shape[0]
+    proj_width = proj_in_up.shape[1]
+    quarter = stored_grads.shape[1]
+    dp_count = lax.axis_size("dp")
+    tensor_count = lax.axis_size("tensor")
+    sub_width = quarter // dp_count
+    q, i = lax.axis_index("tensor"), lax.axis_index("dp")
+    dp_bits = bits_of(dp_count)
+    tensor_bits = bits_of(tensor_count)
+
+    partial = project(
+        inputs_x,
+        hidden,
+        grad_up,
+        grad_down,
+        proj_in_up,
+        proj_in_down,
+        proj_out_up,
+        proj_out_down,
+    )
+    rows = stored_grads[None]
+    for bit in dp_bits[1:] + dp_bits[:1]:
+        rows = jnp.concatenate([rows, swap(rows, "dp", bit)], axis=0)
+    cols = lax.dynamic_slice_in_dim(rows, i * sub_width, sub_width, 2)[None]
+    offsets = [0]
+    for bit in reversed(tensor_bits):
+        cols = jnp.concatenate([cols, swap(cols, "tensor", bit)], axis=0)
+        offsets += [off ^ bit for off in offsets]
+
+    total = partial
+    for bit in tensor_bits[:-1]:
+        total = total + swap(total, "tensor", bit)
+    other = swap(total, "tensor", tensor_bits[-1])
+    cur = current_rows(lengths, total, other, proj_width)
+    cur = cur.reshape(1, examples, proj_width * LAYERS * proj_width)
+    for bit in reversed(dp_bits):
+        cur = jnp.concatenate([cur, swap(cur, "dp", bit)], axis=0)
+    place = jnp.stack([q, i]).astype(jnp.int32)
+    product = gram(rows, cols, cur, place, offsets)
+    return product.reshape(quarter, 1, tensor_count * sub_width)
+
+
+def local_any(
     inputs_x,
     hidden,
     grad_up,
@@ -28,7 +267,6 @@
     tensor_count = lax.axis_size("tensor")
     out_share = proj_width // tensor_count
     tensor_index = lax.axis_index("tensor")
-    layers = 2
     terms_in = jnp.stack([matmul(inputs_x, proj_in_up), matmul(hidden, proj_in_down)])
     terms_out = jnp.stack([matmul(grad_up, proj_out_up), matmul(grad_down, proj_out_down)])
     summed_in, summed_out = lax.psum((terms_in, terms_out), "tensor")
@@ -36,12 +274,12 @@
     live_mask = (jnp.arange(slot_count, dtype=jnp.int32)[None, :] < lengths[:, None]).astype(
         jnp.float32
     )
-    in_proj = summed_in.reshape(layers, examples, slot_count, proj_width).transpose(1, 2, 0, 3)
-    out_proj = summed_out.reshape(layers, examples, slot_count, out_share).transpose(1, 2, 0, 3)
+    in_proj = summed_in.reshape(LAYERS, examples, slot_count, proj_width).transpose(1, 2, 0, 3)
+    out_proj = summed_out.reshape(LAYERS, examples, slot_count, out_share).transpose(1, 2, 0, 3)
     out_proj = out_proj * live_mask[:, :, None, None]
     current = jnp.einsum("esla,eslb->ealb", out_proj, in_proj, precision=lax.Precision.HIGHEST)
     current = (current * (1.0 / math.sqrt(slot_count))).reshape(
-        examples, out_share * layers * proj_width
+        examples, out_share * LAYERS * proj_width
     )
     local_rows = jnp.concatenate([current.astype(jnp.bfloat16), stored_grads], axis=0)
     row_count = local_rows.shape[0]
@@ -61,6 +299,13 @@
     return product.astype(jnp.bfloat16).reshape(quarter, 1, columns.shape[1])
 
 
+def paired(dp_count, tensor_count, proj_width, quarter):
+    sizes = power_of_two(dp_count) and power_of_two(tensor_count)
+    many = dp_count > 1 and tensor_count > 1
+    lanes = quarter % (dp_count * LANES) == 0 and LAYERS * proj_width == LANES
+    return sizes and many and lanes
+
+
 def solution(mesh):
     in_specs = (
         P("dp", "tensor"),
@@ -75,4 +320,14 @@
         P("dp", "tensor"),
     )
     out_specs = P("tensor", "dp", None)
-    return jax.shard_map(local, mesh=mesh, in_specs=in_specs, out_specs=out_specs, check_vma=False)
+
+    def step(*args):
+        counts = mesh.shape["dp"], mesh.shape["tensor"]
+        quarter = args[9].shape[1] // counts[1]
+        fits = paired(*counts, args[4].shape[1], quarter)
+        body = local if fits else local_any
+        return jax.shard_map(
+            body, mesh=mesh, in_specs=in_specs, out_specs=out_specs, check_vma=False
+        )(*args)
+
+    return step

time: 90.5 us -> 54.8 us (0.61)
  blocking collectives: 25.9 us -> 0 us
  between operations: 13.5 us -> 0.1 us
  starting transfers between devices: 0.01 us -> 11.6 us
  waiting for transfers between devices: 37.9 us -> 27.4 us
  matrix products: 10.1 us -> 0 us
  Pallas kernels: 0 us -> 9.51 us
  other arithmetic: 0.77 us -> 4.08 us
    psum x1 -> x0, waiting for transfers between devices: 37.9 us -> none  [local(): summed_in, summed_out = lax.psum((terms_in, terms_out), 'tensor')]
    ppermute x0 -> x10, waiting for transfers between devices: none -> 27.4 us  [swap(): return lax.ppermute(value, axis, [(i, i ^ bit) for i in range(count)])]
    all_gather x2 -> x0, blocking collectives: 25.9 us -> none  [the longest x1 15.1 us: local(): columns = lax.all_gather(column_block, 'tensor', axis=1, tiled=True)]
    ppermute x0 -> x10, starting transfers between devices: none -> 11.6 us  [swap(): return lax.ppermute(value, axis, [(i, i ^ bit) for i in range(count)])]
    dot_general x6 -> x0, matrix products: 10.1 us -> none  [the longest x4 5.6 us: matmul(): return jnp.dot(left, right, preferred_element_type=jnp.float32)]
    pallas_call x0 -> x3, Pallas kernels: none -> 9.51 us  [the longest x1 3.97 us: gram(): pl.pallas_call(functools.partial(gram_kernel, scale, offsets), out_shape=...]
    concatenate x0 -> x8, other arithmetic: none -> 2.49 us  [the longest x3 1.36 us: local(): cur = jnp.concatenate([cur, swap(cur, 'dp', bit)], axis=0)]
    add x0 -> x1, other arithmetic: none -> 0.92 us  [local(): total = total + swap(total, 'tensor', bit)]
  transfers between devices with their start and end apart: 1 -> 10, of which waited for: 1 -> 8; matrix products, arithmetic and copies ran while one was open for 0% -> 6% of each run, Pallas kernels for 0% -> 4%
where the time goes in v1:
time: 54.8 us; the launch traced here: 54.1 us
  waiting for transfers between devices  27.4 us (50%)
  starting transfers between devices  11.6 us (21%)
  Pallas kernels  9.51 us (17%)
  other arithmetic  4.08 us (7%)
  local copies, waits for them, and re-layouts  1.46 us (3%)
    ppermute x10, waiting for transfers between devices, swap(): return lax.ppermute(value, axis, [(i, i ^ bit) for i in range(count)])  27.4 us
    ppermute x10, starting transfers between devices, swap(): return lax.ppermute(value, axis, [(i, i ^ bit) for i in range(count)])  11.6 us
    pallas_call x1, Pallas kernels, gram(): pl.pallas_call(functools.partial(gram_kernel, scale, offsets), out_shape=...  3.97 us
    pallas_call x1, Pallas kernels, project(): pl.pallas_call(project_kernel, out_shape=jax.ShapeDtypeStruct((2 * rows,...  3.64 us
    pallas_call x1, Pallas kernels, current_rows(): pl.pallas_call(current_kernel, out_shape=jax.ShapeDtypeStruct((examples,...  1.9 us
    concatenate x3, other arithmetic, local(): cur = jnp.concatenate([cur, swap(cur, 'dp', bit)], axis=0)  1.36 us
  transfers between devices with their start and end apart: 10, of which 8 were waited for; matrix products, arithmetic and copies ran while one was open for 6% of the time, Pallas kernels for 4%

profile of v1, /device:TPU:0, one launch (start us, length us, event | category | flops | bytes accessed | tf_op | source)
XLA Modules:
  0.0 54.1 jit_solution(17338128456835014958)
XLA Ops:
  0.0 0.0 copy-start.1
  0.0 3.6 %project.1 = f32[256,128]{1,0:T(8,128)} custom-call(bf16[128,1024]{1,0:T(8,128)(2,1)} %x.1, bf16[128,3584]{1,0:T(8,128)(2,1)} %h.1, bf16[128,3584]{1,0:T(8,128)(2,1)} %gu.1, bf16[128,1024]{1,0:T(8,128)(2,1)} %gd.1, bf16[64,1024]{1,0:T(8,128)(2,1)} %bitcast.16, bf16[64,3584]{1,0:T(8,128)(2,1)} %bitcast.14, bf16[64,3584]{1,0:T(8,128)(2,1)} %bitcast.15, ...), custom_call_target="tpu_custom_call" | custom-call | flops 150994944 | bytes 3538944 | tf_op jit(solution)/shard_map/project/pallas_call | solution.py:65
  3.7 3.1 %collective-permute-start.5 = (f32[256,128]{1,0:T(8,128)}, f32[256,128]{1,0:T(8,128)S(1)}, u32[]{:S(2)}, u32[]{:S(2)}) collective-permute-start(f32[256,128]{1,0:T(8,128)} %project.1), channel_id=1, source_target_pairs={{0,1},{1,0},{2,3},{3,2},{4,5},{5,4},{6,7},{7,6},{8,9},{9,8},{10,11... | collective-permute-start | bytes 393224 | tf_op jit(solution)/shard_map/ppermute | solution.py:30
  6.8 3.7 %collective-permute-done.5 = f32[256,128]{1,0:T(8,128)S(1)} collective-permute-done((f32[256,128]{1,0:T(8,128)}, f32[256,128]{1,0:T(8,128)S(1)}, u32[]{:S(2)}, u32[]{:S(2)}) %collective-permute-start.5) | collective-permute-done | bytes 131104 | tf_op jit(solution)/shard_map/ppermute | solution.py:30
  10.5 0.9 %add.7.own = f32[256,128]{1,0:T(8,128)S(1)} add(f32[256,128]{1,0:T(8,128)} %project.1, f32[256,128]{1,0:T(8,128)S(1)} %collective-permute-done.5) | non-fusion elementwise | flops 32768 | bytes 393216 | tf_op jit(solution)/shard_map/add | solution.py:241
  11.4 0.0 copy-start.2
  11.4 2.8 %collective-permute-start.6 = (f32[256,128]{1,0:T(8,128)S(1)}, f32[256,128]{1,0:T(8,128)S(1)}, u32[]{:S(2)}, u32[]{:S(2)}) collective-permute-start(f32[256,128]{1,0:T(8,128)S(1)} %add.7.own), channel_id=1, source_target_pairs={{0,2},{1,3},{2,0},{3,1},{4,6},{5,7},{6,4},{7,5},{8,10},{9,11},{10,... | collective-permute-start | bytes 393224 | tf_op jit(solution)/shard_map/ppermute | solution.py:30
  14.2 1.5 %collective-permute-start = (bf16[1,26,2048]{2,1,0:T(8,128)(2,1)}, bf16[1,26,2048]{2,1,0:T(8,128)(2,1)S(1)}, u32[]{:S(2)}, u32[]{:S(2)}) collective-permute-start(bf16[1,26,2048]{2,1,0:T(8,128)(2,1)} %bitcast.10), channel_id=1, source_target_pairs={{0,8},{4,12},{8,0},{12,4},{16,24},{20,28},{24,16},{28,20},{1,9},{5... | collective-permute-start | bytes 319496 | tf_op jit(solution)/shard_map/ppermute | solution.py:30
  15.7 4.1 %collective-permute-done.6.other = f32[256,128]{1,0:T(8,128)S(1)} collective-permute-done((f32[256,128]{1,0:T(8,128)S(1)}, f32[256,128]{1,0:T(8,128)S(1)}, u32[]{:S(2)}, u32[]{:S(2)}) %collective-permute-start.6) | collective-permute-done | bytes 131104 | tf_op jit(solution)/shard_map/ppermute | solution.py:30
  19.8 0.0 copy-done.2
  19.9 0.0 copy-start.3
  19.9 0.6 %copy-done.3 = f32[256,128]{1,0:T(8,128)} copy-done((f32[256,128]{1,0:T(8,128)}, f32[256,128]{1,0:T(8,128)S(1)}, u32[]{:S(2)}) %copy-start.3) | copy-done | bytes 131096
  20.5 1.9 %current.1 = bf16[2,64,128]{2,1,0:T(8,128)(2,1)} custom-call(s32[2]{0:T(128)} %lengths.1, f32[256,128]{1,0:T(8,128)} %copy-done.2, f32[256,128]{1,0:T(8,128)} %copy-done.3), custom_call_target="tpu_custom_call" | custom-call | flops 4194304 | bytes 262144 | tf_op jit(solution)/shard_map/current/pallas_call | solution.py:105
  22.4 0.8 %reshape.6 = bf16[1,2,8192]{2,1,0:T(2,128)(2,1)S(1)} reshape(bf16[2,64,128]{2,1,0:T(8,128)(2,1)} %current.1) | data formatting | bytes 65536 | tf_op jit(solution)/shard_map/reshape | solution.py:244
  23.2 1.5 %collective-permute-start.7 = (bf16[1,2,8192]{2,1,0:T(2,128)(2,1)S(1)}, bf16[1,2,8192]{2,1,0:T(2,128)(2,1)S(1)}, u32[]{:S(2)}, u32[]{:S(2)}) collective-permute-start(bf16[1,2,8192]{2,1,0:T(2,128)(2,1)S(1)} %reshape.6), channel_id=1, source_target_pairs={{0,16},{4,20},{8,24},{12,28},{16,0},{20,4},{24,8},{28,12},{1,17},{... | collective-permute-start | bytes 98312 | tf_op jit(solution)/shard_map/ppermute | solution.py:30
  24.6 0.0 collective-permute-done
  24.6 0.0 copy-done.1
  24.7 0.7 %collective-permute-start.1 = (bf16[2,26,2048]{2,1,0:T(8,128)(2,1)S(1)}, bf16[2,26,2048]{2,1,0:T(8,128)(2,1)S(1)}, u32[]{:S(2)}, u32[]{:S(2)}) collective-permute-start(bf16[2,26,2048]{2,1,0:T(8,128)(2,1)S(1)} %pad_maximum_fusion.3), channel_id=1, source_target_pairs={{0,16},{4,20},{8,24},{12,28},{16,0},{20,4},{24,8},{28,12},{1,17},{... | collective-permute-start | bytes 638984 | tf_op jit(solution)/shard_map/ppermute | solution.py:30
  25.4 2.1 %collective-permute-done.7 = bf16[1,2,8192]{2,1,0:T(2,128)(2,1)S(1)} collective-permute-done((bf16[1,2,8192]{2,1,0:T(2,128)(2,1)S(1)}, bf16[1,2,8192]{2,1,0:T(2,128)(2,1)S(1)}, u32[]{:S(2)}, u32[]{:S(2)}) %collective-permute-start.7) | collective-permute-done | bytes 32800 | tf_op jit(solution)/shard_map/ppermute | solution.py:30
  27.5 0.1 pad_maximum_fusion.7
  27.6 1.4 %collective-permute-start.8 = (bf16[2,2,8192]{2,1,0:T(2,128)(2,1)S(1)}, bf16[2,2,8192]{2,1,0:T(2,128)(2,1)S(1)}, u32[]{:S(2)}, u32[]{:S(2)}) collective-permute-start(bf16[2,2,8192]{2,1,0:T(2,128)(2,1)S(1)} %pad_maximum_fusion.7), channel_id=1, source_target_pairs={{0,8},{4,12},{8,0},{12,4},{16,24},{20,28},{24,16},{28,20},{1,9},{5... | collective-permute-start | bytes 196616 | tf_op jit(solution)/shard_map/ppermute | solution.py:30
  29.0 2.2 %collective-permute-done.1 = bf16[2,26,2048]{2,1,0:T(8,128)(2,1)S(1)} collective-permute-done((bf16[2,26,2048]{2,1,0:T(8,128)(2,1)S(1)}, bf16[2,26,2048]{2,1,0:T(8,128)(2,1)S(1)}, u32[]{:S(2)}, u32[]{:S(2)}) %collective-permute-start.1) | collective-permute-done | bytes 213024 | tf_op jit(solution)/shard_map/ppermute | solution.py:30
  31.3 0.1 pad_maximum_fusion.1
  31.3 0.1 collective-permute-start.2
  31.4 0.5 collective-permute-done.8
  31.9 0.2 pad_maximum_fusion.6
  32.1 0.1 collective-permute-start.9
  32.2 1.1 %collective-permute-done.2 = bf16[4,26,2048]{2,1,0:T(8,128)(2,1)S(1)} collective-permute-done((bf16[4,26,2048]{2,1,0:T(8,128)(2,1)S(1)}, bf16[4,26,2048]{2,1,0:T(8,128)(2,1)S(1)}, u32[]{:S(2)}, u32[]{:S(2)}) %collective-permute-start.2) | collective-permute-done | bytes 426016 | tf_op jit(solution)/shard_map/ppermute | solution.py:30
  33.3 0.1 pad_maximum_fusion.stored
  33.4 0.0 copy-start
  33.5 0.4 collective-permute-start.3
  33.9 0.7 %pad_add_fusion.place = s32[2]{0:T(128)} fusion(s32[1]{0:T(128)} %bitcast.1, s32[1]{0:T(128)} %bitcast), kind=kLoop, calls=%fused_computation.9 | loop fusion | flops 2 | bytes 16 | tf_op jit(solution)/shard_map/stack | solution.py:247
  34.5 8.3 %collective-permute-done.3 = bf16[1,8,26,256]{3,2,1,0:T(8,128)(2,1)S(1)} collective-permute-done((bf16[1,8,26,256]{3,2,1,0:T(8,128)(2,1)S(1)}, bf16[1,8,26,256]{3,2,1,0:T(8,128)(2,1)S(1)}, u32[]{:S(2)}, u32[]{:S(2)}) %collective-permute-start.3) | collective-permute-done | bytes 106528 | tf_op jit(solution)/shard_map/ppermute | solution.py:30
  42.8 0.1 collective-permute-start.4
  42.9 0.0 collective-permute-done.9
  42.9 1.1 %pad_maximum_fusion.5.cur = bf16[8,2,8192]{2,1,0:T(2,128)(2,1)} fusion(bf16[4,2,8192]{2,1,0:T(2,128)(2,1)S(1)} %collective-permute-done.9, bf16[2,2,8192]{2,1,0:T(2,128)(2,1)S(1)} %collective-permute-done.8, bf16[1,2,8192]{2,1,0:T(2,128)(2,1)S(1)} %collective-permute-done.7, bf16[1,2,8192]{2,1,0:T(2,128)(2,1)S(1)} %reshape.6), kind=kLoop, calls=%fused_computation.5 | loop fusion | flops 393216 | bytes 524288 | tf_op jit(solution)/shard_map/concatenate | solution.py:246
  44.0 5.3 %collective-permute-done.4 = bf16[2,8,26,256]{3,2,1,0:T(8,128)(2,1)S(1)} collective-permute-done((bf16[2,8,26,256]{3,2,1,0:T(8,128)(2,1)S(1)}, bf16[2,8,26,256]{3,2,1,0:T(8,128)(2,1)S(1)}, u32[]{:S(2)}, u32[]{:S(2)}) %collective-permute-start.4) | collective-permute-done | bytes 213024 | tf_op jit(solution)/shard_map/ppermute | solution.py:30
  49.3 0.9 %pad_maximum_fusion.2.cols = bf16[4,8,26,256]{3,2,1,0:T(8,128)(2,1)} fusion(bf16[2,8,26,256]{3,2,1,0:T(8,128)(2,1)S(1)} %collective-permute-done.4, bf16[1,8,26,256]{3,2,1,0:T(8,128)(2,1)S(1)} %collective-permute-done.3, bf16[1,8,26,256]{3,2,1,0:T(8,128)(2,1)S(1)} %dynamic-slice_bitcast_fusion), kind=kLoop, calls=%fused_computation.2 | loop fusion | flops 425984 | bytes 851968 | tf_op jit(solution)/shard_map/concatenate | solution.py:236
  50.2 0.0 copy-done
  50.2 4.0 %gram.1 = bf16[2048,1024]{1,0:T(8,128)(2,1)} custom-call(s32[2]{0:T(128)} %pad_add_fusion.place, bf16[8,26,2048]{2,1,0:T(8,128)(2,1)} %copy-done, bf16[4,8,26,256]{3,2,1,0:T(8,128)(2,1)} %pad_maximum_fusion.2.cols, bf16[8,2,8192]{2,1,0:T(2,128)(2,1)} %pad_maximum_fusion.5.cur), custom_call_target="tpu_custom_call" | custom-call | flops 1073741824 | bytes 4194304 | tf_op jit(solution)/shard_map/gram/pallas_call | solution.py:177
  (3 shorter events, 0.1 us)
Async XLA Ops:
  0.0 24.6 %copy-start.1 = (bf16[26,2048]{1,0:T(8,128)(2,1)S(1)}, bf16[26,2048]{1,0:T(8,128)(2,1)}, u32[]{:S(2)}) copy-start(bf16[26,2048]{1,0:T(8,128)(2,1)} %param.19) | copy-start | bytes 319492
  3.7 6.8 %collective-permute-start.5 = (f32[256,128]{1,0:T(8,128)}, f32[256,128]{1,0:T(8,128)S(1)}, u32[]{:S(2)}, u32[]{:S(2)}) collective-permute-start(f32[256,128]{1,0:T(8,128)} %project.1), channel_id=1, source_target_pairs={{0,1},{1,0},{2,3},{3,2},{4,5},{5,4},{6,7},{7,6},{8,9},{9,8},{10,11... | collective-permute-start | bytes 393224 | tf_op jit(solution)/shard_map/ppermute | solution.py:30
  11.4 8.4 %copy-start.2 = (f32[256,128]{1,0:T(8,128)}, f32[256,128]{1,0:T(8,128)S(1)}, u32[]{:S(2)}) copy-start(f32[256,128]{1,0:T(8,128)S(1)} %add.7.own) | copy-start | bytes 393220
  11.4 8.4 %collective-permute-start.6 = (f32[256,128]{1,0:T(8,128)S(1)}, f32[256,128]{1,0:T(8,128)S(1)}, u32[]{:S(2)}, u32[]{:S(2)}) collective-permute-start(f32[256,128]{1,0:T(8,128)S(1)} %add.7.own), channel_id=1, source_target_pairs={{0,2},{1,3},{2,0},{3,1},{4,6},{5,7},{6,4},{7,5},{8,10},{9,11},{10,... | collective-permute-start | bytes 393224 | tf_op jit(solution)/shard_map/ppermute | solution.py:30
  14.2 10.4 %collective-permute-start = (bf16[1,26,2048]{2,1,0:T(8,128)(2,1)}, bf16[1,26,2048]{2,1,0:T(8,128)(2,1)S(1)}, u32[]{:S(2)}, u32[]{:S(2)}) collective-permute-start(bf16[1,26,2048]{2,1,0:T(8,128)(2,1)} %bitcast.10), channel_id=1, source_target_pairs={{0,8},{4,12},{8,0},{12,4},{16,24},{20,28},{24,16},{28,20},{1,9},{5... | collective-permute-start | bytes 319496 | tf_op jit(solution)/shard_map/ppermute | solution.py:30
  19.9 0.7 %copy-start.3 = (f32[256,128]{1,0:T(8,128)}, f32[256,128]{1,0:T(8,128)S(1)}, u32[]{:S(2)}) copy-start(f32[256,128]{1,0:T(8,128)S(1)} %collective-permute-done.6.other) | copy-start | bytes 393220
  23.2 4.3 %collective-permute-start.7 = (bf16[1,2,8192]{2,1,0:T(2,128)(2,1)S(1)}, bf16[1,2,8192]{2,1,0:T(2,128)(2,1)S(1)}, u32[]{:S(2)}, u32[]{:S(2)}) collective-permute-start(bf16[1,2,8192]{2,1,0:T(2,128)(2,1)S(1)} %reshape.6), channel_id=1, source_target_pairs={{0,16},{4,20},{8,24},{12,28},{16,0},{20,4},{24,8},{28,12},{1,17},{... | collective-permute-start | bytes 98312 | tf_op jit(solution)/shard_map/ppermute | solution.py:30
  24.7 6.6 %collective-permute-start.1 = (bf16[2,26,2048]{2,1,0:T(8,128)(2,1)S(1)}, bf16[2,26,2048]{2,1,0:T(8,128)(2,1)S(1)}, u32[]{:S(2)}, u32[]{:S(2)}) collective-permute-start(bf16[2,26,2048]{2,1,0:T(8,128)(2,1)S(1)} %pad_maximum_fusion.3), channel_id=1, source_target_pairs={{0,16},{4,20},{8,24},{12,28},{16,0},{20,4},{24,8},{28,12},{1,17},{... | collective-permute-start | bytes 638984 | tf_op jit(solution)/shard_map/ppermute | solution.py:30
  27.6 4.3 %collective-permute-start.8 = (bf16[2,2,8192]{2,1,0:T(2,128)(2,1)S(1)}, bf16[2,2,8192]{2,1,0:T(2,128)(2,1)S(1)}, u32[]{:S(2)}, u32[]{:S(2)}) collective-permute-start(bf16[2,2,8192]{2,1,0:T(2,128)(2,1)S(1)} %pad_maximum_fusion.7), channel_id=1, source_target_pairs={{0,8},{4,12},{8,0},{12,4},{16,24},{20,28},{24,16},{28,20},{1,9},{5... | collective-permute-start | bytes 196616 | tf_op jit(solution)/shard_map/ppermute | solution.py:30
  31.3 2.0 %collective-permute-start.2 = (bf16[4,26,2048]{2,1,0:T(8,128)(2,1)S(1)}, bf16[4,26,2048]{2,1,0:T(8,128)(2,1)S(1)}, u32[]{:S(2)}, u32[]{:S(2)}) collective-permute-start(bf16[4,26,2048]{2,1,0:T(8,128)(2,1)S(1)} %pad_maximum_fusion.1), channel_id=1, source_target_pairs={{0,4},{4,0},{8,12},{12,8},{16,20},{20,16},{24,28},{28,24},{1,5},{5... | collective-permute-start | bytes 1277960 | tf_op jit(solution)/shard_map/ppermute | solution.py:30
  32.1 10.8 %collective-permute-start.9 = (bf16[4,2,8192]{2,1,0:T(2,128)(2,1)S(1)}, bf16[4,2,8192]{2,1,0:T(2,128)(2,1)S(1)}, u32[]{:S(2)}, u32[]{:S(2)}) collective-permute-start(bf16[4,2,8192]{2,1,0:T(2,128)(2,1)S(1)} %pad_maximum_fusion.6), channel_id=1, source_target_pairs={{0,4},{4,0},{8,12},{12,8},{16,20},{20,16},{24,28},{28,24},{1,5},{5... | collective-permute-start | bytes 393224 | tf_op jit(solution)/shard_map/ppermute | solution.py:30
  33.4 16.7 %copy-start = (bf16[8,26,2048]{2,1,0:T(8,128)(2,1)}, bf16[8,26,2048]{2,1,0:T(8,128)(2,1)S(1)}, u32[]{:S(2)}) copy-start(bf16[8,26,2048]{2,1,0:T(8,128)(2,1)S(1)} %pad_maximum_fusion.stored) | copy-start | bytes 2555908
  33.5 9.3 %collective-permute-start.3 = (bf16[1,8,26,256]{3,2,1,0:T(8,128)(2,1)S(1)}, bf16[1,8,26,256]{3,2,1,0:T(8,128)(2,1)S(1)}, u32[]{:S(2)}, u32[]{:S(2)}) collective-permute-start(bf16[1,8,26,256]{3,2,1,0:T(8,128)(2,1)S(1)} %dynamic-slice_bitcast_fusion), channel_id=1, source_target_pairs={{0,2},{1,3},{2,0},{3,1},{4,6},{5,7},{6,4},{7,5},{8,10},{9,11},{10,... | collective-permute-start | bytes 319496 | tf_op jit(solution)/shard_map/ppermute | solution.py:30
  42.8 6.4 %collective-permute-start.4 = (bf16[2,8,26,256]{3,2,1,0:T(8,128)(2,1)S(1)}, bf16[2,8,26,256]{3,2,1,0:T(8,128)(2,1)S(1)}, u32[]{:S(2)}, u32[]{:S(2)}) collective-permute-start(bf16[2,8,26,256]{3,2,1,0:T(8,128)(2,1)S(1)} %pad_maximum_fusion.4), channel_id=1, source_target_pairs={{0,1},{1,0},{2,3},{3,2},{4,5},{5,4},{6,7},{7,6},{8,9},{9,8},{10,11... | collective-permute-start | bytes 638984 | tf_op jit(solution)/shard_map/ppermute | solution.py:30

commit v2 on v1

--- a/solution.py
+++ b/solution.py
@@ -11,6 +11,7 @@
 LAYERS = 2
 LANES = 128
 SLOT = 16
+MIB = 1 << 20
 
 
 def matmul(left, right):
@@ -60,12 +61,13 @@
 
 def project(x, h, gu, gd, pu, pd, ou, od):
     args = (x, h, gu, gd, pu.T, pd.T, ou.T, od.T)
+    args = tuple(pltpu.with_memory_space_constraint(a, pltpu.HBM) for a in args)
     rows = x.shape[0]
     width = LAYERS * pu.shape[1]
     return pl.pallas_call(
         project_kernel,
         out_shape=jax.ShapeDtypeStruct((2 * rows, width), jnp.float32),
-        in_specs=[pl.BlockSpec(memory_space=pl.ANY)] * 8,
+        in_specs=[pl.BlockSpec(memory_space=pltpu.HBM)] * 8,
         out_specs=pl.BlockSpec(memory_space=pltpu.VMEM),
         scratch_shapes=[pltpu.VMEM(a.shape, a.dtype) for a in args]
         + [pltpu.SemaphoreType.DMA((8,))],
@@ -74,6 +76,7 @@
             bytes_accessed=2 * sum(math.prod(a.shape) for a in args),
             transcendentals=0,
         ),
+        compiler_params=pltpu.CompilerParams(vmem_limit_bytes=8 * MIB),
         name="project",
     )(*args)
 
@@ -118,6 +121,7 @@
             bytes_accessed=own.size * 8,
             transcendentals=0,
         ),
+        compiler_params=pltpu.CompilerParams(vmem_limit_bytes=4 * MIB),
         name="current",
     )(lengths, own, other)
 
@@ -126,12 +130,12 @@
     return (LAYERS * proj_width) ** 2
 
 
-def gram_kernel(scale, offsets, place, stored, cols, cur, out, left, right, buf, sem):
+def gram_kernel(scale, offsets, stored, cols, cur, out, left, right, buf, sem):
     pieces, old, quarter = stored.shape
     new = cur.shape[1]
     sub = cols.shape[-1]
     slot = left.shape[0] // pieces
-    q, i = place[0], place[1]
+    q, i = lax.axis_index("tensor"), lax.axis_index("dp")
     left[...] = jnp.zeros_like(left)
     right[...] = jnp.zeros_like(right)
     for p in range(pieces):
@@ -167,7 +171,7 @@
         copy.wait()
 
 
-def gram(stored, cols, cur, place, offsets):
+def gram(stored, cols, cur, offsets):
     pieces, old, quarter = stored.shape
     new = cur.shape[1]
     slot = -(-(old + new) // SLOT) * SLOT
@@ -177,9 +181,8 @@
     return pl.pallas_call(
         functools.partial(gram_kernel, scale, offsets),
         out_shape=jax.ShapeDtypeStruct((quarter, width), jnp.bfloat16),
-        in_specs=[pl.BlockSpec(memory_space=pltpu.SMEM)]
-        + [pl.BlockSpec(memory_space=pltpu.VMEM)] * 3,
-        out_specs=pl.BlockSpec(memory_space=pl.ANY),
+        in_specs=[pl.BlockSpec(memory_space=pltpu.VMEM)] * 3,
+        out_specs=pl.BlockSpec(memory_space=pltpu.HBM),
         scratch_shapes=[
             pltpu.VMEM((pieces * slot, quarter), jnp.bfloat16),
             pltpu.VMEM((pieces * slot, width), jnp.bfloat16),
@@ -191,8 +194,9 @@
             bytes_accessed=2 * quarter * width,
             transcendentals=0,
         ),
+        compiler_params=pltpu.CompilerParams(vmem_limit_bytes=24 * MIB),
         name="gram",
-    )(place, stored, cols, cur)
+    )(stored, cols, cur)
 
 
 def local(
@@ -213,11 +217,22 @@
     dp_count = lax.axis_size("dp")
     tensor_count = lax.axis_size("tensor")
     sub_width = quarter // dp_count
-    q, i = lax.axis_index("tensor"), lax.axis_index("dp")
+    i = lax.axis_index("dp")
     dp_bits = bits_of(dp_count)
     tensor_bits = bits_of(tensor_count)
 
-    partial = project(
+    rows = stored_grads[None]
+    for bit in dp_bits[1:] + dp_bits[:1]:
+        moved = swap(rows, "dp", bit)
+        rows = jnp.concatenate([rows, moved], axis=0)
+    cols = lax.dynamic_slice_in_dim(rows, i * sub_width, sub_width, 2)[None]
+    offsets = [0]
+    for bit in reversed(tensor_bits):
+        moved = swap(cols, "tensor", bit)
+        cols = jnp.concatenate([cols, moved], axis=0)
+        offsets += [off ^ bit for off in offsets]
+
+    total = project(
         inputs_x,
         hidden,
         grad_up,
@@ -227,25 +242,16 @@
         proj_out_up,
         proj_out_down,
     )
-    rows = stored_grads[None]
-    for bit in dp_bits[1:] + dp_bits[:1]:
-        rows = jnp.concatenate([rows, swap(rows, "dp", bit)], axis=0)
-    cols = lax.dynamic_slice_in_dim(rows, i * sub_width, sub_width, 2)[None]
-    offsets = [0]
-    for bit in reversed(tensor_bits):
-        cols = jnp.concatenate([cols, swap(cols, "tensor", bit)], axis=0)
-        offsets += [off ^ bit for off in offsets]
-
-    total = partial
-    for bit in tensor_bits[:-1]:
-        total = total + swap(total, "tensor", bit)
-    other = swap(total, "tensor", tensor_bits[-1])
+    for bit in tensor_bits:
+        other = swap(total, "tensor", bit)
+        if bit != tensor_bits[-1]:
+            total = total + other
     cur = current_rows(lengths, total, other, proj_width)
     cur = cur.reshape(1, examples, proj_width * LAYERS * proj_width)
     for bit in reversed(dp_bits):
-        cur = jnp.concatenate([cur, swap(cur, "dp", bit)], axis=0)
-    place = jnp.stack([q, i]).astype(jnp.int32)
-    product = gram(rows, cols, cur, place, offsets)
+        moved = swap(cur, "dp", bit)
+        cur = jnp.concatenate([cur, moved], axis=0)
+    product = gram(rows, cols, cur, offsets)
     return product.reshape(quarter, 1, tensor_count * sub_width)
 
 

time: 54.8 us -> 42.8 us (0.78)
  waiting for transfers between devices: 27.4 us -> 21.9 us
  Pallas kernels: 9.51 us -> 6.36 us
  other arithmetic: 4.08 us -> 1.87 us
  local copies, waits for them, and re-layouts: 1.46 us -> 0.05 us
  starting transfers between devices: 11.6 us -> 12.4 us
    ppermute x10, waiting for transfers between devices: 27.4 us -> 21.9 us  [swap(): return lax.ppermute(value, axis, [(i, i ^ bit) for i in range(count)])]
    pallas_call x1, Pallas kernels: 3.97 us -> 2.55 us  [gram(): pl.pallas_call(functools.partial(gram_kernel, scale, offsets), out_shape=...]
    pallas_call x1, Pallas kernels: 1.9 us -> 0.86 us  [current_rows(): pl.pallas_call(current_kernel, out_shape=jax.ShapeDtypeStruct((examples,...]
    add x1, other arithmetic: 0.92 us -> 0.02 us  [local(): total = total + other]
    reshape x1, local copies, waits for them, and re-layouts: 0.77 us -> 0.02 us  [local(): cur = cur.reshape(1, examples, proj_width * LAYERS * proj_width)]
    ppermute x10, starting transfers between devices: 11.6 us -> 12.4 us  [swap(): return lax.ppermute(value, axis, [(i, i ^ bit) for i in range(count)])]
    pallas_call x1, Pallas kernels: 3.64 us -> 2.96 us  [project(): pl.pallas_call(project_kernel, out_shape=jax.ShapeDtypeStruct((2 * rows,...]
    another operation x1 -> x0, other arithmetic: 0.66 us -> none  [local(): place = jnp.stack([q, i]).astype(jnp.int32)]
  transfers between devices with their start and end apart: 10 -> 10, of which waited for: 8 -> 6; matrix products, arithmetic and copies ran while one was open for 6% -> 4% of each run, Pallas kernels for 4% -> 9%
where the time goes in v2:
time: 42.8 us; the launch traced here: 42.7 us
  waiting for transfers between devices  21.9 us (51%)
  starting transfers between devices  12.4 us (29%)
  Pallas kernels  6.36 us (15%)
  other arithmetic  1.87 us (4%)
    ppermute x10, waiting for transfers between devices, swap(): return lax.ppermute(value, axis, [(i, i ^ bit) for i in range(count)])  21.9 us
    ppermute x10, starting transfers between devices, swap(): return lax.ppermute(value, axis, [(i, i ^ bit) for i in range(count)])  12.4 us
    pallas_call x1, Pallas kernels, project(): pl.pallas_call(project_kernel, out_shape=jax.ShapeDtypeStruct((2 * rows,...  2.96 us
    pallas_call x1, Pallas kernels, gram(): pl.pallas_call(functools.partial(gram_kernel, scale, offsets), out_shape=...  2.55 us
    concatenate x3, other arithmetic, local(): rows = jnp.concatenate([rows, moved], axis=0)  1.12 us
    pallas_call x1, Pallas kernels, current_rows(): pl.pallas_call(current_kernel, out_shape=jax.ShapeDtypeStruct((examples,...  0.86 us
  transfers between devices with their start and end apart: 10, of which 6 were waited for; matrix products, arithmetic and copies ran while one was open for 4% of the time, Pallas kernels for 9%

profile of v2, /device:TPU:0, one launch (start us, length us, event | category | flops | bytes accessed | tf_op | source)
XLA Modules:
  0.0 42.7 jit_solution(9980378636064650585)
XLA Ops:
  0.0 0.0 copy-start.1
  0.0 0.0 copy-start
  0.0 3.0 %collective-permute-start = (bf16[1,26,2048]{2,1,0:T(8,128)(2,1)}, bf16[1,26,2048]{2,1,0:T(8,128)(2,1)S(1)}, u32[]{:S(2)}, u32[]{:S(2)}) collective-permute-start(bf16[1,26,2048]{2,1,0:T(8,128)(2,1)} %bitcast.8), channel_id=1, source_target_pairs={{0,8},{4,12},{8,0},{12,4},{16,24},{20,28},{24,16},{28,20},{1,9},{5... | collective-permute-start | bytes 319496 | tf_op jit(solution)/shard_map/ppermute | solution.py:31
  3.0 3.0 %project.1 = f32[256,128]{1,0:T(8,128)S(1)} custom-call(bf16[128,1024]{1,0:T(8,128)(2,1)} %x.1, bf16[128,3584]{1,0:T(8,128)(2,1)} %h.1, bf16[128,3584]{1,0:T(8,128)(2,1)} %gu.1, bf16[128,1024]{1,0:T(8,128)(2,1)} %gd.1, bf16[64,1024]{1,0:T(8,128)(2,1)} %bitcast.14, bf16[64,3584]{1,0:T(8,128)(2,1)} %bitcast.12, bf16[64,3584]{1,0:T(8,128)(2,1)} %bitcast.13, ...), custom_call_target="tpu_custom_call" | custom-call | flops 150994944 | bytes 3538944 | tf_op jit(solution)/shard_map/project/pallas_call | solution.py:67
  5.9 1.6 %collective-permute-start.5 = (f32[256,128]{1,0:T(8,128)S(1)}, f32[256,128]{1,0:T(8,128)S(1)}, u32[]{:S(2)}, u32[]{:S(2)}) collective-permute-start(f32[256,128]{1,0:T(8,128)S(1)} %project.1), channel_id=1, source_target_pairs={{0,1},{1,0},{2,3},{3,2},{4,5},{5,4},{6,7},{7,6},{8,9},{9,8},{10,11... | collective-permute-start | bytes 393224 | tf_op jit(solution)/shard_map/ppermute | solution.py:31
  7.6 0.0 collective-permute-done
  7.6 0.9 %pad_maximum_fusion.3 = bf16[2,26,2048]{2,1,0:T(8,128)(2,1)S(1)} fusion(bf16[1,26,2048]{2,1,0:T(8,128)(2,1)S(1)} %collective-permute-done, bf16[1,26,2048]{2,1,0:T(8,128)(2,1)} %bitcast.9), kind=kLoop, calls=%fused_computation.3 | loop fusion | flops 106496 | bytes 425984 | tf_op jit(solution)/shard_map/concatenate | solution.py:227
  8.5 1.6 %collective-permute-start.1 = (bf16[2,26,2048]{2,1,0:T(8,128)(2,1)S(1)}, bf16[2,26,2048]{2,1,0:T(8,128)(2,1)S(1)}, u32[]{:S(2)}, u32[]{:S(2)}) collective-permute-start(bf16[2,26,2048]{2,1,0:T(8,128)(2,1)S(1)} %pad_maximum_fusion.3), channel_id=1, source_target_pairs={{0,16},{4,20},{8,24},{12,28},{16,0},{20,4},{24,8},{28,12},{1,17},{... | collective-permute-start | bytes 638984 | tf_op jit(solution)/shard_map/ppermute | solution.py:31
  10.1 0.9 %collective-permute-done.5 = f32[256,128]{1,0:T(8,128)S(1)} collective-permute-done((f32[256,128]{1,0:T(8,128)S(1)}, f32[256,128]{1,0:T(8,128)S(1)}, u32[]{:S(2)}, u32[]{:S(2)}) %collective-permute-start.5) | collective-permute-done | bytes 131104 | tf_op jit(solution)/shard_map/ppermute | solution.py:31
  11.0 2.7 %collective-permute-start.6 = (f32[256,128]{1,0:T(8,128)S(1)}, f32[256,128]{1,0:T(8,128)S(1)}, u32[]{:S(2)}, u32[]{:S(2)}) collective-permute-start(f32[256,128]{1,0:T(8,128)S(1)} %add.7.own), channel_id=1, source_target_pairs={{0,2},{1,3},{2,0},{3,1},{4,6},{5,7},{6,4},{7,5},{8,10},{9,11},{10,... | collective-permute-start | bytes 393224 | tf_op jit(solution)/shard_map/ppermute | solution.py:31
  13.6 4.9 %collective-permute-done.6.other = f32[256,128]{1,0:T(8,128)S(1)} collective-permute-done((f32[256,128]{1,0:T(8,128)S(1)}, f32[256,128]{1,0:T(8,128)S(1)}, u32[]{:S(2)}, u32[]{:S(2)}) %collective-permute-start.6) | collective-permute-done | bytes 131104 | tf_op jit(solution)/shard_map/ppermute | solution.py:31
  18.6 0.0 copy-done
  18.6 0.9 %current.1 = bf16[2,64,128]{2,1,0:T(8,128)(2,1)S(1)} custom-call(s32[2]{0:T(128)S(1)} %copy-done, f32[256,128]{1,0:T(8,128)S(1)} %add.7.own, f32[256,128]{1,0:T(8,128)S(1)} %collective-permute-done.6.other), custom_call_target="tpu_custom_call" | custom-call | flops 4194304 | bytes 262144 | tf_op jit(solution)/shard_map/current/pallas_call | solution.py:108
  19.5 1.6 %collective-permute-start.7 = (bf16[1,2,8192]{2,1,0:T(2,128)(2,1)S(1)}, bf16[1,2,8192]{2,1,0:T(2,128)(2,1)S(1)}, u32[]{:S(2)}, u32[]{:S(2)}) collective-permute-start(bf16[1,2,8192]{2,1,0:T(2,128)(2,1)S(1)} %reshape.6), channel_id=1, source_target_pairs={{0,16},{4,20},{8,24},{12,28},{16,0},{20,4},{24,8},{28,12},{1,17},{... | collective-permute-start | bytes 98312 | tf_op jit(solution)/shard_map/ppermute | solution.py:31
  21.0 0.0 collective-permute-done.1
  21.0 0.0 copy-done.1
  21.1 0.1 pad_maximum_fusion.1
  21.1 0.1 collective-permute-start.2
  21.2 2.2 %collective-permute-done.7 = bf16[1,2,8192]{2,1,0:T(2,128)(2,1)S(1)} collective-permute-done((bf16[1,2,8192]{2,1,0:T(2,128)(2,1)S(1)}, bf16[1,2,8192]{2,1,0:T(2,128)(2,1)S(1)}, u32[]{:S(2)}, u32[]{:S(2)}) %collective-permute-start.7) | collective-permute-done | bytes 32800 | tf_op jit(solution)/shard_map/ppermute | solution.py:31
  23.4 0.1 pad_maximum_fusion.7
  23.5 1.0 %collective-permute-start.8 = (bf16[2,2,8192]{2,1,0:T(2,128)(2,1)S(1)}, bf16[2,2,8192]{2,1,0:T(2,128)(2,1)S(1)}, u32[]{:S(2)}, u32[]{:S(2)}) collective-permute-start(bf16[2,2,8192]{2,1,0:T(2,128)(2,1)S(1)} %pad_maximum_fusion.7), channel_id=1, source_target_pairs={{0,8},{4,12},{8,0},{12,4},{16,24},{20,28},{24,16},{28,20},{1,9},{5... | collective-permute-start | bytes 196616 | tf_op jit(solution)/shard_map/ppermute | solution.py:31
  24.5 0.0 collective-permute-done.2
  24.5 0.1 pad_maximum_fusion.stored
  24.7 0.7 %collective-permute-start.3 = (bf16[1,8,26,256]{3,2,1,0:T(8,128)(2,1)S(1)}, bf16[1,8,26,256]{3,2,1,0:T(8,128)(2,1)S(1)}, u32[]{:S(2)}, u32[]{:S(2)}) collective-permute-start(bf16[1,8,26,256]{3,2,1,0:T(8,128)(2,1)S(1)} %dynamic-slice_bitcast_fusion), channel_id=1, source_target_pairs={{0,2},{1,3},{2,0},{3,1},{4,6},{5,7},{6,4},{7,5},{8,10},{9,11},{10,... | collective-permute-start | bytes 319496 | tf_op jit(solution)/shard_map/ppermute | solution.py:31
  25.4 2.5 %collective-permute-done.8 = bf16[2,2,8192]{2,1,0:T(2,128)(2,1)S(1)} collective-permute-done((bf16[2,2,8192]{2,1,0:T(2,128)(2,1)S(1)}, bf16[2,2,8192]{2,1,0:T(2,128)(2,1)S(1)}, u32[]{:S(2)}, u32[]{:S(2)}) %collective-permute-start.8) | collective-permute-done | bytes 65568 | tf_op jit(solution)/shard_map/ppermute | solution.py:31
  27.9 0.2 pad_maximum_fusion.6
  28.1 0.1 collective-permute-start.9
  28.1 4.4 %collective-permute-done.3 = bf16[1,8,26,256]{3,2,1,0:T(8,128)(2,1)S(1)} collective-permute-done((bf16[1,8,26,256]{3,2,1,0:T(8,128)(2,1)S(1)}, bf16[1,8,26,256]{3,2,1,0:T(8,128)(2,1)S(1)}, u32[]{:S(2)}, u32[]{:S(2)}) %collective-permute-start.3) | collective-permute-done | bytes 106528 | tf_op jit(solution)/shard_map/ppermute | solution.py:31
  32.6 0.1 collective-permute-start.4
  32.7 0.0 collective-permute-done.9
  32.7 0.4 pad_maximum_fusion.5.cur
  33.1 7.0 %collective-permute-done.4 = bf16[2,8,26,256]{3,2,1,0:T(8,128)(2,1)S(1)} collective-permute-done((bf16[2,8,26,256]{3,2,1,0:T(8,128)(2,1)S(1)}, bf16[2,8,26,256]{3,2,1,0:T(8,128)(2,1)S(1)}, u32[]{:S(2)}, u32[]{:S(2)}) %collective-permute-start.4) | collective-permute-done | bytes 213024 | tf_op jit(solution)/shard_map/ppermute | solution.py:31
  40.0 0.1 pad_maximum_fusion.2.cols
  40.1 2.5 %gram.1 = bf16[2048,1024]{1,0:T(8,128)(2,1)} custom-call(bf16[8,26,2048]{2,1,0:T(8,128)(2,1)S(1)} %pad_maximum_fusion.stored, bf16[4,8,26,256]{3,2,1,0:T(8,128)(2,1)S(1)} %pad_maximum_fusion.2.cols, bf16[8,2,8192]{2,1,0:T(2,128)(2,1)S(1)} %pad_maximum_fusion.5.cur), custom_call_target="tpu_custom_call" | custom-call | flops 1073741824 | bytes 4194304 | tf_op jit(solution)/shard_map/gram/pallas_call | solution.py:181
  (4 shorter events, 0.1 us)
Async XLA Ops:
  0.0 21.1 %copy-start.1 = (bf16[26,2048]{1,0:T(8,128)(2,1)S(1)}, bf16[26,2048]{1,0:T(8,128)(2,1)}, u32[]{:S(2)}) copy-start(bf16[26,2048]{1,0:T(8,128)(2,1)} %param.19) | copy-start | bytes 319492
  0.0 18.6 %copy-start = (s32[2]{0:T(128)S(1)}, s32[2]{0:T(128)}, u32[]{:S(2)}) copy-start(s32[2]{0:T(128)} %lengths.1) | copy-start | bytes 28
  0.0 7.6 %collective-permute-start = (bf16[1,26,2048]{2,1,0:T(8,128)(2,1)}, bf16[1,26,2048]{2,1,0:T(8,128)(2,1)S(1)}, u32[]{:S(2)}, u32[]{:S(2)}) collective-permute-start(bf16[1,26,2048]{2,1,0:T(8,128)(2,1)} %bitcast.8), channel_id=1, source_target_pairs={{0,8},{4,12},{8,0},{12,4},{16,24},{20,28},{24,16},{28,20},{1,9},{5... | collective-permute-start | bytes 319496 | tf_op jit(solution)/shard_map/ppermute | solution.py:31
  5.9 5.0 %collective-permute-start.5 = (f32[256,128]{1,0:T(8,128)S(1)}, f32[256,128]{1,0:T(8,128)S(1)}, u32[]{:S(2)}, u32[]{:S(2)}) collective-permute-start(f32[256,128]{1,0:T(8,128)S(1)} %project.1), channel_id=1, source_target_pairs={{0,1},{1,0},{2,3},{3,2},{4,5},{5,4},{6,7},{7,6},{8,9},{9,8},{10,11... | collective-permute-start | bytes 393224 | tf_op jit(solution)/shard_map/ppermute | solution.py:31
  8.5 12.5 %collective-permute-start.1 = (bf16[2,26,2048]{2,1,0:T(8,128)(2,1)S(1)}, bf16[2,26,2048]{2,1,0:T(8,128)(2,1)S(1)}, u32[]{:S(2)}, u32[]{:S(2)}) collective-permute-start(bf16[2,26,2048]{2,1,0:T(8,128)(2,1)S(1)} %pad_maximum_fusion.3), channel_id=1, source_target_pairs={{0,16},{4,20},{8,24},{12,28},{16,0},{20,4},{24,8},{28,12},{1,17},{... | collective-permute-start | bytes 638984 | tf_op jit(solution)/shard_map/ppermute | solution.py:31
  11.0 7.6 %collective-permute-start.6 = (f32[256,128]{1,0:T(8,128)S(1)}, f32[256,128]{1,0:T(8,128)S(1)}, u32[]{:S(2)}, u32[]{:S(2)}) collective-permute-start(f32[256,128]{1,0:T(8,128)S(1)} %add.7.own), channel_id=1, source_target_pairs={{0,2},{1,3},{2,0},{3,1},{4,6},{5,7},{6,4},{7,5},{8,10},{9,11},{10,... | collective-permute-start | bytes 393224 | tf_op jit(solution)/shard_map/ppermute | solution.py:31
  19.5 4.0 %collective-permute-start.7 = (bf16[1,2,8192]{2,1,0:T(2,128)(2,1)S(1)}, bf16[1,2,8192]{2,1,0:T(2,128)(2,1)S(1)}, u32[]{:S(2)}, u32[]{:S(2)}) collective-permute-start(bf16[1,2,8192]{2,1,0:T(2,128)(2,1)S(1)} %reshape.6), channel_id=1, source_target_pairs={{0,16},{4,20},{8,24},{12,28},{16,0},{20,4},{24,8},{28,12},{1,17},{... | collective-permute-start | bytes 98312 | tf_op jit(solution)/shard_map/ppermute | solution.py:31
  21.1 3.4 %collective-permute-start.2 = (bf16[4,26,2048]{2,1,0:T(8,128)(2,1)S(1)}, bf16[4,26,2048]{2,1,0:T(8,128)(2,1)S(1)}, u32[]{:S(2)}, u32[]{:S(2)}) collective-permute-start(bf16[4,26,2048]{2,1,0:T(8,128)(2,1)S(1)} %pad_maximum_fusion.1), channel_id=1, source_target_pairs={{0,4},{4,0},{8,12},{12,8},{16,20},{20,16},{24,28},{28,24},{1,5},{5... | collective-permute-start | bytes 1277960 | tf_op jit(solution)/shard_map/ppermute | solution.py:31
  23.5 4.3 %collective-permute-start.8 = (bf16[2,2,8192]{2,1,0:T(2,128)(2,1)S(1)}, bf16[2,2,8192]{2,1,0:T(2,128)(2,1)S(1)}, u32[]{:S(2)}, u32[]{:S(2)}) collective-permute-start(bf16[2,2,8192]{2,1,0:T(2,128)(2,1)S(1)} %pad_maximum_fusion.7), channel_id=1, source_target_pairs={{0,8},{4,12},{8,0},{12,4},{16,24},{20,28},{24,16},{28,20},{1,9},{5... | collective-permute-start | bytes 196616 | tf_op jit(solution)/shard_map/ppermute | solution.py:31
  24.7 7.9 %collective-permute-start.3 = (bf16[1,8,26,256]{3,2,1,0:T(8,128)(2,1)S(1)}, bf16[1,8,26,256]{3,2,1,0:T(8,128)(2,1)S(1)}, u32[]{:S(2)}, u32[]{:S(2)}) collective-permute-start(bf16[1,8,26,256]{3,2,1,0:T(8,128)(2,1)S(1)} %dynamic-slice_bitcast_fusion), channel_id=1, source_target_pairs={{0,2},{1,3},{2,0},{3,1},{4,6},{5,7},{6,4},{7,5},{8,10},{9,11},{10,... | collective-permute-start | bytes 319496 | tf_op jit(solution)/shard_map/ppermute | solution.py:31
  28.1 4.6 %collective-permute-start.9 = (bf16[4,2,8192]{2,1,0:T(2,128)(2,1)S(1)}, bf16[4,2,8192]{2,1,0:T(2,128)(2,1)S(1)}, u32[]{:S(2)}, u32[]{:S(2)}) collective-permute-start(bf16[4,2,8192]{2,1,0:T(2,128)(2,1)S(1)} %pad_maximum_fusion.6), channel_id=1, source_target_pairs={{0,4},{4,0},{8,12},{12,8},{16,20},{20,16},{24,28},{28,24},{1,5},{5... | collective-permute-start | bytes 393224 | tf_op jit(solution)/shard_map/ppermute | solution.py:31
  32.6 7.4 %collective-permute-start.4 = (bf16[2,8,26,256]{3,2,1,0:T(8,128)(2,1)S(1)}, bf16[2,8,26,256]{3,2,1,0:T(8,128)(2,1)S(1)}, u32[]{:S(2)}, u32[]{:S(2)}) collective-permute-start(bf16[2,8,26,256]{3,2,1,0:T(8,128)(2,1)S(1)} %pad_maximum_fusion.4), channel_id=1, source_target_pairs={{0,1},{1,0},{2,3},{3,2},{4,5},{5,4},{6,7},{7,6},{8,9},{9,8},{10,11... | collective-permute-start | bytes 638984 | tf_op jit(solution)/shard_map/ppermute | solution.py:31

commit v3 on v2

--- a/solution.py
+++ b/solution.py
@@ -26,9 +26,19 @@
     return [1 << k for k in range(n.bit_length() - 1)]
 
 
-def swap(value, axis, bit):
-    count = lax.axis_size(axis)
-    return lax.ppermute(value, axis, [(i, i ^ bit) for i in range(count)])
+def turned(bits):
+    return bits[1:] + bits[:1]
+
+
+def swap(value, axis, bit, odd_bit):
+    dp_count, tensor_count = lax.axis_size("dp"), lax.axis_size("tensor")
+    pairs = []
+    for d in range(dp_count):
+        by = odd_bit if d % 2 else bit
+        for t in range(tensor_count):
+            to = (d ^ by, t) if axis == "dp" else (d, t ^ by)
+            pairs.append((d * tensor_count + t, to[0] * tensor_count + to[1]))
+    return lax.ppermute(value, ("dp", "tensor"), pairs)
 
 
 def project_kernel(x, h, gu, gd, pu, pd, ou, od, out, *scratch):
@@ -143,7 +153,8 @@
         left[p * slot + old : p * slot + old + new, :] = cur[
             p, :, pl.ds(pl.multiple_of(q * quarter, quarter), quarter)
         ]
-    for k, off in enumerate(offsets):
+    for k, (even, odd) in enumerate(offsets):
+        off = jnp.where(i % 2 == 0, even, odd)
         to = pl.multiple_of((q ^ off) * sub, sub)
         source = pl.multiple_of((q ^ off) * quarter + i * sub, sub)
         for p in range(pieces):
@@ -218,19 +229,21 @@
     tensor_count = lax.axis_size("tensor")
     sub_width = quarter // dp_count
     i = lax.axis_index("dp")
-    dp_bits = bits_of(dp_count)
+    links = bits_of(dp_count)[1:]
+    dp_rounds = [*zip(links, turned(links), strict=True), (1, 1)]
     tensor_bits = bits_of(tensor_count)
+    tensor_rounds = [*zip(tensor_bits, turned(tensor_bits), strict=True)]
 
     rows = stored_grads[None]
-    for bit in dp_bits[1:] + dp_bits[:1]:
-        moved = swap(rows, "dp", bit)
+    for bits in dp_rounds:
+        moved = swap(rows, "dp", *bits)
         rows = jnp.concatenate([rows, moved], axis=0)
     cols = lax.dynamic_slice_in_dim(rows, i * sub_width, sub_width, 2)[None]
-    offsets = [0]
-    for bit in reversed(tensor_bits):
-        moved = swap(cols, "tensor", bit)
+    offsets = [(0, 0)]
+    for bits in reversed(tensor_rounds):
+        moved = swap(cols, "tensor", *bits)
         cols = jnp.concatenate([cols, moved], axis=0)
-        offsets += [off ^ bit for off in offsets]
+        offsets += [(even ^ bits[0], odd ^ bits[1]) for even, odd in offsets]
 
     total = project(
         inputs_x,
@@ -242,14 +255,14 @@
         proj_out_up,
         proj_out_down,
     )
-    for bit in tensor_bits:
-        other = swap(total, "tensor", bit)
-        if bit != tensor_bits[-1]:
+    for n, bits in enumerate(tensor_rounds):
+        other = swap(total, "tensor", *bits)
+        if n < len(tensor_rounds) - 1:
             total = total + other
     cur = current_rows(lengths, total, other, proj_width)
     cur = cur.reshape(1, examples, proj_width * LAYERS * proj_width)
-    for bit in reversed(dp_bits):
-        moved = swap(cur, "dp", bit)
+    for bits in dp_rounds:
+        moved = swap(cur, "dp", *bits)
         cur = jnp.concatenate([cur, moved], axis=0)
     product = gram(rows, cols, cur, offsets)
     return product.reshape(quarter, 1, tensor_count * sub_width)

time: 42.8 us -> 41.9 us (0.979)
  the two profiles are of different devices: /device:TPU:0 before, /device:TPU:24 now
where the time goes in v3:
time: 41.9 us; the launch traced here: 41.8 us
  waiting for transfers between devices  26.8 us (64%)
  starting transfers between devices  6.51 us (16%)
  Pallas kernels  6.36 us (15%)
  other arithmetic  1.87 us (4%)
    ppermute x10, waiting for transfers between devices, swap(): return lax.ppermute(value, ('dp', 'tensor'), pairs)  26.8 us
    ppermute x10, starting transfers between devices, swap(): return lax.ppermute(value, ('dp', 'tensor'), pairs)  6.51 us
    pallas_call x1, Pallas kernels, project(): pl.pallas_call(project_kernel, out_shape=jax.ShapeDtypeStruct((2 * rows,...  2.96 us
    pallas_call x1, Pallas kernels, gram(): pl.pallas_call(functools.partial(gram_kernel, scale, offsets), out_shape=...  2.54 us
    concatenate x3, other arithmetic, local(): rows = jnp.concatenate([rows, moved], axis=0)  1.12 us
    pallas_call x1, Pallas kernels, current_rows(): pl.pallas_call(current_kernel, out_shape=jax.ShapeDtypeStruct((examples,...  0.86 us
  transfers between devices with their start and end apart: 10, of which 7 were waited for; matrix products, arithmetic and copies ran while one was open for 4% of the time, Pallas kernels for 9%

profile of v3, /device:TPU:24, one launch (start us, length us, event | category | flops | bytes accessed | tf_op | source)
XLA Modules:
  0.0 41.8 jit_solution(2379591374840992892)
XLA Ops:
  0.0 0.0 copy-start.1
  0.0 0.0 copy-start
  0.0 1.5 %collective-permute-start = (bf16[1,26,2048]{2,1,0:T(8,128)(2,1)}, bf16[1,26,2048]{2,1,0:T(8,128)(2,1)S(1)}, u32[]{:S(2)}, u32[]{:S(2)}) collective-permute-start(bf16[1,26,2048]{2,1,0:T(8,128)(2,1)} %bitcast.8), channel_id=1, source_target_pairs={{0,8},{1,9},{2,10},{3,11},{4,20},{5,21},{6,22},{7,23},{8,0},{9,1},... | collective-permute-start | bytes 319496 | tf_op jit(solution)/shard_map/ppermute | solution.py:41
  1.5 3.0 %project.1 = f32[256,128]{1,0:T(8,128)S(1)} custom-call(bf16[128,1024]{1,0:T(8,128)(2,1)} %x.1, bf16[128,3584]{1,0:T(8,128)(2,1)} %h.1, bf16[128,3584]{1,0:T(8,128)(2,1)} %gu.1, bf16[128,1024]{1,0:T(8,128)(2,1)} %gd.1, bf16[64,1024]{1,0:T(8,128)(2,1)} %bitcast.14, bf16[64,3584]{1,0:T(8,128)(2,1)} %bitcast.12, bf16[64,3584]{1,0:T(8,128)(2,1)} %bitcast.13, ...), custom_call_target="tpu_custom_call" | custom-call | flops 150994944 | bytes 3538944 | tf_op jit(solution)/shard_map/project/pallas_call | solution.py:77
  4.5 0.5 %collective-permute-start.5 = (f32[256,128]{1,0:T(8,128)S(1)}, f32[256,128]{1,0:T(8,128)S(1)}, u32[]{:S(2)}, u32[]{:S(2)}) collective-permute-start(f32[256,128]{1,0:T(8,128)S(1)} %project.1), channel_id=1, source_target_pairs={{0,1},{1,0},{2,3},{3,2},{4,6},{5,7},{6,4},{7,5},{8,9},{9,8},{10,11... | collective-permute-start | bytes 393224 | tf_op jit(solution)/shard_map/ppermute | solution.py:41
  5.0 0.2 collective-permute-done
  5.2 0.9 %pad_maximum_fusion.3 = bf16[2,26,2048]{2,1,0:T(8,128)(2,1)S(1)} fusion(bf16[1,26,2048]{2,1,0:T(8,128)(2,1)S(1)} %collective-permute-done, bf16[1,26,2048]{2,1,0:T(8,128)(2,1)} %bitcast.9), kind=kLoop, calls=%fused_computation.3 | loop fusion | flops 106496 | bytes 425984 | tf_op jit(solution)/shard_map/concatenate | solution.py:240
  6.1 1.6 %collective-permute-start.1 = (bf16[2,26,2048]{2,1,0:T(8,128)(2,1)S(1)}, bf16[2,26,2048]{2,1,0:T(8,128)(2,1)S(1)}, u32[]{:S(2)}, u32[]{:S(2)}) collective-permute-start(bf16[2,26,2048]{2,1,0:T(8,128)(2,1)S(1)} %pad_maximum_fusion.3), channel_id=1, source_target_pairs={{0,16},{1,17},{2,18},{3,19},{4,12},{5,13},{6,14},{7,15},{8,24},{9,... | collective-permute-start | bytes 638984 | tf_op jit(solution)/shard_map/ppermute | solution.py:41
  7.7 3.1 %collective-permute-done.5 = f32[256,128]{1,0:T(8,128)S(1)} collective-permute-done((f32[256,128]{1,0:T(8,128)S(1)}, f32[256,128]{1,0:T(8,128)S(1)}, u32[]{:S(2)}, u32[]{:S(2)}) %collective-permute-start.5) | collective-permute-done | bytes 131104 | tf_op jit(solution)/shard_map/ppermute | solution.py:41
  10.8 0.1 collective-permute-start.6
  10.9 6.2 %collective-permute-done.6.other = f32[256,128]{1,0:T(8,128)S(1)} collective-permute-done((f32[256,128]{1,0:T(8,128)S(1)}, f32[256,128]{1,0:T(8,128)S(1)}, u32[]{:S(2)}, u32[]{:S(2)}) %collective-permute-start.6) | collective-permute-done | bytes 131104 | tf_op jit(solution)/shard_map/ppermute | solution.py:41
  17.2 0.0 copy-done
  17.2 0.9 %current.1 = bf16[2,64,128]{2,1,0:T(8,128)(2,1)S(1)} custom-call(s32[2]{0:T(128)S(1)} %copy-done, f32[256,128]{1,0:T(8,128)S(1)} %add.7.own, f32[256,128]{1,0:T(8,128)S(1)} %collective-permute-done.6.other), custom_call_target="tpu_custom_call" | custom-call | flops 4194304 | bytes 262144 | tf_op jit(solution)/shard_map/current/pallas_call | solution.py:118
  18.0 1.0 %collective-permute-start.7 = (bf16[1,2,8192]{2,1,0:T(2,128)(2,1)S(1)}, bf16[1,2,8192]{2,1,0:T(2,128)(2,1)S(1)}, u32[]{:S(2)}, u32[]{:S(2)}) collective-permute-start(bf16[1,2,8192]{2,1,0:T(2,128)(2,1)S(1)} %reshape.6), channel_id=1, source_target_pairs={{0,8},{1,9},{2,10},{3,11},{4,20},{5,21},{6,22},{7,23},{8,0},{9,1},... | collective-permute-start | bytes 98312 | tf_op jit(solution)/shard_map/ppermute | solution.py:41
  19.1 0.0 collective-permute-done.1
  19.1 0.0 copy-done.1
  19.1 0.1 pad_maximum_fusion.1
  19.2 0.1 collective-permute-start.2
  19.2 2.8 %collective-permute-done.7 = bf16[1,2,8192]{2,1,0:T(2,128)(2,1)S(1)} collective-permute-done((bf16[1,2,8192]{2,1,0:T(2,128)(2,1)S(1)}, bf16[1,2,8192]{2,1,0:T(2,128)(2,1)S(1)}, u32[]{:S(2)}, u32[]{:S(2)}) %collective-permute-start.7) | collective-permute-done | bytes 32800 | tf_op jit(solution)/shard_map/ppermute | solution.py:41
  22.0 0.1 pad_maximum_fusion.7
  22.1 1.5 %collective-permute-start.8 = (bf16[2,2,8192]{2,1,0:T(2,128)(2,1)S(1)}, bf16[2,2,8192]{2,1,0:T(2,128)(2,1)S(1)}, u32[]{:S(2)}, u32[]{:S(2)}) collective-permute-start(bf16[2,2,8192]{2,1,0:T(2,128)(2,1)S(1)} %pad_maximum_fusion.7), channel_id=1, source_target_pairs={{0,16},{1,17},{2,18},{3,19},{4,12},{5,13},{6,14},{7,15},{8,24},{9,... | collective-permute-start | bytes 196616 | tf_op jit(solution)/shard_map/ppermute | solution.py:41
  23.6 0.0 collective-permute-done.2
  23.6 0.1 pad_maximum_fusion.stored
  23.7 0.1 collective-permute-start.3
  23.8 2.6 %collective-permute-done.8 = bf16[2,2,8192]{2,1,0:T(2,128)(2,1)S(1)} collective-permute-done((bf16[2,2,8192]{2,1,0:T(2,128)(2,1)S(1)}, bf16[2,2,8192]{2,1,0:T(2,128)(2,1)S(1)}, u32[]{:S(2)}, u32[]{:S(2)}) %collective-permute-start.8) | collective-permute-done | bytes 65568 | tf_op jit(solution)/shard_map/ppermute | solution.py:41
  26.4 0.2 pad_maximum_fusion.6
  26.6 0.1 collective-permute-start.9
  26.7 6.0 %collective-permute-done.3 = bf16[1,8,26,256]{3,2,1,0:T(8,128)(2,1)S(1)} collective-permute-done((bf16[1,8,26,256]{3,2,1,0:T(8,128)(2,1)S(1)}, bf16[1,8,26,256]{3,2,1,0:T(8,128)(2,1)S(1)}, u32[]{:S(2)}, u32[]{:S(2)}) %collective-permute-start.3) | collective-permute-done | bytes 106528 | tf_op jit(solution)/shard_map/ppermute | solution.py:41
  32.7 0.1 collective-permute-start.4
  32.8 0.0 collective-permute-done.9
  32.8 0.4 pad_maximum_fusion.5.cur
  33.2 6.0 %collective-permute-done.4 = bf16[2,8,26,256]{3,2,1,0:T(8,128)(2,1)S(1)} collective-permute-done((bf16[2,8,26,256]{3,2,1,0:T(8,128)(2,1)S(1)}, bf16[2,8,26,256]{3,2,1,0:T(8,128)(2,1)S(1)}, u32[]{:S(2)}, u32[]{:S(2)}) %collective-permute-start.4) | collective-permute-done | bytes 213024 | tf_op jit(solution)/shard_map/ppermute | solution.py:41
  39.1 0.1 pad_maximum_fusion.2.cols
  39.2 2.5 %gram.1 = bf16[2048,1024]{1,0:T(8,128)(2,1)} custom-call(bf16[8,26,2048]{2,1,0:T(8,128)(2,1)S(1)} %pad_maximum_fusion.stored, bf16[4,8,26,256]{3,2,1,0:T(8,128)(2,1)S(1)} %pad_maximum_fusion.2.cols, bf16[8,2,8192]{2,1,0:T(2,128)(2,1)S(1)} %pad_maximum_fusion.5.cur), custom_call_target="tpu_custom_call" | custom-call | flops 1073741824 | bytes 4194304 | tf_op jit(solution)/shard_map/gram/pallas_call | solution.py:192
  (4 shorter events, 0.1 us)
Async XLA Ops:
  0.0 19.1 %copy-start.1 = (bf16[26,2048]{1,0:T(8,128)(2,1)S(1)}, bf16[26,2048]{1,0:T(8,128)(2,1)}, u32[]{:S(2)}) copy-start(bf16[26,2048]{1,0:T(8,128)(2,1)} %param.19) | copy-start | bytes 319492
  0.0 17.2 %copy-start = (s32[2]{0:T(128)S(1)}, s32[2]{0:T(128)}, u32[]{:S(2)}) copy-start(s32[2]{0:T(128)} %lengths.1) | copy-start | bytes 28
  0.0 5.2 %collective-permute-start = (bf16[1,26,2048]{2,1,0:T(8,128)(2,1)}, bf16[1,26,2048]{2,1,0:T(8,128)(2,1)S(1)}, u32[]{:S(2)}, u32[]{:S(2)}) collective-permute-start(bf16[1,26,2048]{2,1,0:T(8,128)(2,1)} %bitcast.8), channel_id=1, source_target_pairs={{0,8},{1,9},{2,10},{3,11},{4,20},{5,21},{6,22},{7,23},{8,0},{9,1},... | collective-permute-start | bytes 319496 | tf_op jit(solution)/shard_map/ppermute | solution.py:41
  4.5 6.3 %collective-permute-start.5 = (f32[256,128]{1,0:T(8,128)S(1)}, f32[256,128]{1,0:T(8,128)S(1)}, u32[]{:S(2)}, u32[]{:S(2)}) collective-permute-start(f32[256,128]{1,0:T(8,128)S(1)} %project.1), channel_id=1, source_target_pairs={{0,1},{1,0},{2,3},{3,2},{4,6},{5,7},{6,4},{7,5},{8,9},{9,8},{10,11... | collective-permute-start | bytes 393224 | tf_op jit(solution)/shard_map/ppermute | solution.py:41
  6.1 13.0 %collective-permute-start.1 = (bf16[2,26,2048]{2,1,0:T(8,128)(2,1)S(1)}, bf16[2,26,2048]{2,1,0:T(8,128)(2,1)S(1)}, u32[]{:S(2)}, u32[]{:S(2)}) collective-permute-start(bf16[2,26,2048]{2,1,0:T(8,128)(2,1)S(1)} %pad_maximum_fusion.3), channel_id=1, source_target_pairs={{0,16},{1,17},{2,18},{3,19},{4,12},{5,13},{6,14},{7,15},{8,24},{9,... | collective-permute-start | bytes 638984 | tf_op jit(solution)/shard_map/ppermute | solution.py:41
  10.8 6.4 %collective-permute-start.6 = (f32[256,128]{1,0:T(8,128)S(1)}, f32[256,128]{1,0:T(8,128)S(1)}, u32[]{:S(2)}, u32[]{:S(2)}) collective-permute-start(f32[256,128]{1,0:T(8,128)S(1)} %add.7.own), channel_id=1, source_target_pairs={{0,2},{1,3},{2,0},{3,1},{4,5},{5,4},{6,7},{7,6},{8,10},{9,11},{10,... | collective-permute-start | bytes 393224 | tf_op jit(solution)/shard_map/ppermute | solution.py:41
  18.0 4.0 %collective-permute-start.7 = (bf16[1,2,8192]{2,1,0:T(2,128)(2,1)S(1)}, bf16[1,2,8192]{2,1,0:T(2,128)(2,1)S(1)}, u32[]{:S(2)}, u32[]{:S(2)}) collective-permute-start(bf16[1,2,8192]{2,1,0:T(2,128)(2,1)S(1)} %reshape.6), channel_id=1, source_target_pairs={{0,8},{1,9},{2,10},{3,11},{4,20},{5,21},{6,22},{7,23},{8,0},{9,1},... | collective-permute-start | bytes 98312 | tf_op jit(solution)/shard_map/ppermute | solution.py:41
  19.2 4.4 %collective-permute-start.2 = (bf16[4,26,2048]{2,1,0:T(8,128)(2,1)S(1)}, bf16[4,26,2048]{2,1,0:T(8,128)(2,1)S(1)}, u32[]{:S(2)}, u32[]{:S(2)}) collective-permute-start(bf16[4,26,2048]{2,1,0:T(8,128)(2,1)S(1)} %pad_maximum_fusion.1), channel_id=1, source_target_pairs={{0,4},{1,5},{2,6},{3,7},{4,0},{5,1},{6,2},{7,3},{8,12},{9,13},{10,... | collective-permute-start | bytes 1277960 | tf_op jit(solution)/shard_map/ppermute | solution.py:41
  22.1 4.3 %collective-permute-start.8 = (bf16[2,2,8192]{2,1,0:T(2,128)(2,1)S(1)}, bf16[2,2,8192]{2,1,0:T(2,128)(2,1)S(1)}, u32[]{:S(2)}, u32[]{:S(2)}) collective-permute-start(bf16[2,2,8192]{2,1,0:T(2,128)(2,1)S(1)} %pad_maximum_fusion.7), channel_id=1, source_target_pairs={{0,16},{1,17},{2,18},{3,19},{4,12},{5,13},{6,14},{7,15},{8,24},{9,... | collective-permute-start | bytes 196616 | tf_op jit(solution)/shard_map/ppermute | solution.py:41
  23.7 8.9 %collective-permute-start.3 = (bf16[1,8,26,256]{3,2,1,0:T(8,128)(2,1)S(1)}, bf16[1,8,26,256]{3,2,1,0:T(8,128)(2,1)S(1)}, u32[]{:S(2)}, u32[]{:S(2)}) collective-permute-start(bf16[1,8,26,256]{3,2,1,0:T(8,128)(2,1)S(1)} %dynamic-slice_bitcast_fusion), channel_id=1, source_target_pairs={{0,2},{1,3},{2,0},{3,1},{4,5},{5,4},{6,7},{7,6},{8,10},{9,11},{10,... | collective-permute-start | bytes 319496 | tf_op jit(solution)/shard_map/ppermute | solution.py:41
  26.6 6.2 %collective-permute-start.9 = (bf16[4,2,8192]{2,1,0:T(2,128)(2,1)S(1)}, bf16[4,2,8192]{2,1,0:T(2,128)(2,1)S(1)}, u32[]{:S(2)}, u32[]{:S(2)}) collective-permute-start(bf16[4,2,8192]{2,1,0:T(2,128)(2,1)S(1)} %pad_maximum_fusion.6), channel_id=1, source_target_pairs={{0,4},{1,5},{2,6},{3,7},{4,0},{5,1},{6,2},{7,3},{8,12},{9,13},{10,... | collective-permute-start | bytes 393224 | tf_op jit(solution)/shard_map/ppermute | solution.py:41
  32.7 6.4 %collective-permute-start.4 = (bf16[2,8,26,256]{3,2,1,0:T(8,128)(2,1)S(1)}, bf16[2,8,26,256]{3,2,1,0:T(8,128)(2,1)S(1)}, u32[]{:S(2)}, u32[]{:S(2)}) collective-permute-start(bf16[2,8,26,256]{3,2,1,0:T(8,128)(2,1)S(1)} %pad_maximum_fusion.4), channel_id=1, source_target_pairs={{0,1},{1,0},{2,3},{3,2},{4,6},{5,7},{6,4},{7,5},{8,9},{9,8},{10,11... | collective-permute-start | bytes 638984 | tf_op jit(solution)/shard_map/ppermute | solution.py:41

commit v4 on v3

--- a/solution.py
+++ b/solution.py
@@ -41,10 +41,10 @@
     return lax.ppermute(value, ("dp", "tensor"), pairs)
 
 
-def project_kernel(x, h, gu, gd, pu, pd, ou, od, out, *scratch):
-    ins = (x, h, gu, gd, pu, pd, ou, od)
-    bufs, sem = scratch[:8], scratch[8]
-    order = (4, 0, 7, 3, 5, 1, 6, 2)
+def project_kernel(x, h, gu, gd, pu, pd, ou, od, stored, out, keep, *scratch):
+    ins = (x, h, gu, gd, pu, pd, ou, od, stored)
+    bufs, sem = (*scratch[:8], keep), scratch[8]
+    order = (4, 0, 7, 3, 5, 1, 6, 2, 8)
     copies = {}
     for n in order:
         copies[n] = pltpu.make_async_copy(ins[n], bufs[n], sem.at[n])
@@ -67,20 +67,24 @@
     out[:rows, :] = jnp.concatenate([in_up, in_down], axis=1)
     out_up = product(2, 6)
     out[rows:, :] = jnp.concatenate([out_up, out_down], axis=1)
-
-
-def project(x, h, gu, gd, pu, pd, ou, od):
-    args = (x, h, gu, gd, pu.T, pd.T, ou.T, od.T)
+    copies[8].wait()
+
+
+def project(x, h, gu, gd, pu, pd, ou, od, stored):
+    args = (x, h, gu, gd, pu.T, pd.T, ou.T, od.T, stored)
     args = tuple(pltpu.with_memory_space_constraint(a, pltpu.HBM) for a in args)
     rows = x.shape[0]
     width = LAYERS * pu.shape[1]
     return pl.pallas_call(
         project_kernel,
-        out_shape=jax.ShapeDtypeStruct((2 * rows, width), jnp.float32),
-        in_specs=[pl.BlockSpec(memory_space=pltpu.HBM)] * 8,
-        out_specs=pl.BlockSpec(memory_space=pltpu.VMEM),
-        scratch_shapes=[pltpu.VMEM(a.shape, a.dtype) for a in args]
-        + [pltpu.SemaphoreType.DMA((8,))],
+        out_shape=(
+            jax.ShapeDtypeStruct((2 * rows, width), jnp.float32),
+            jax.ShapeDtypeStruct(stored.shape, stored.dtype),
+        ),
+        in_specs=[pl.BlockSpec(memory_space=pltpu.HBM)] * 9,
+        out_specs=(pl.BlockSpec(memory_space=pltpu.VMEM),) * 2,
+        scratch_shapes=[pltpu.VMEM(a.shape, a.dtype) for a in args[:8]]
+        + [pltpu.SemaphoreType.DMA((9,))],
         cost_estimate=pl.CostEstimate(
             flops=2 * sum(math.prod(a.shape) for a in args[:4]) * pu.shape[1],
             bytes_accessed=2 * sum(math.prod(a.shape) for a in args),
@@ -140,28 +144,32 @@
     return (LAYERS * proj_width) ** 2
 
 
-def gram_kernel(scale, offsets, stored, cols, cur, out, left, right, buf, sem):
+def gram_kernel(scale, offsets, stored, cols, cur, moved, out, left, right, buf, sem):
     pieces, old, quarter = stored.shape
-    new = cur.shape[1]
+    half, new = cur.shape[:2]
     sub = cols.shape[-1]
     slot = left.shape[0] // pieces
     q, i = lax.axis_index("tensor"), lax.axis_index("dp")
+    place = pl.ds(pl.multiple_of(q * quarter, quarter), quarter)
     left[...] = jnp.zeros_like(left)
     right[...] = jnp.zeros_like(right)
     for p in range(pieces):
-        left[p * slot : p * slot + old, :] = stored[p]
-        left[p * slot + old : p * slot + old + new, :] = cur[
-            p, :, pl.ds(pl.multiple_of(q * quarter, quarter), quarter)
-        ]
-    for k, (even, odd) in enumerate(offsets):
-        off = jnp.where(i % 2 == 0, even, odd)
-        to = pl.multiple_of((q ^ off) * sub, sub)
-        source = pl.multiple_of((q ^ off) * quarter + i * sub, sub)
+        base = p * slot
+        fresh = cur if p < half else moved
+        left[base : base + old, :] = stored[p]
+        left[base + old : base + old + new, :] = fresh[p % half, :, place]
+    for block in range(len(offsets)):
+        to = slice(block * sub, (block + 1) * sub)
+        source = pl.ds(pl.multiple_of(block * quarter + i * sub, sub), sub)
         for p in range(pieces):
-            right[p * slot : p * slot + old, pl.ds(to, sub)] = cols[k, p]
-            right[p * slot + old : p * slot + old + new, pl.ds(to, sub)] = cur[
-                p, :, pl.ds(source, sub)
-            ]
+            base = p * slot + old
+            fresh = cur if p < half else moved
+            right[base : base + new, to] = fresh[p % half, :, source]
+    for k, pair in enumerate(offsets):
+        block = q ^ jnp.where(i % 2 == 0, *pair)
+        to = pl.ds(pl.multiple_of(block * sub, sub), sub)
+        for p in range(pieces):
+            right[p * slot : p * slot + old, to] = cols[k, p]
     chunk = buf.shape[1]
     copies = []
     for m in range(buf.shape[0]):
@@ -182,7 +190,7 @@
         copy.wait()
 
 
-def gram(stored, cols, cur, offsets):
+def gram(stored, cols, cur, moved, offsets):
     pieces, old, quarter = stored.shape
     new = cur.shape[1]
     slot = -(-(old + new) // SLOT) * SLOT
@@ -192,7 +200,7 @@
     return pl.pallas_call(
         functools.partial(gram_kernel, scale, offsets),
         out_shape=jax.ShapeDtypeStruct((quarter, width), jnp.bfloat16),
-        in_specs=[pl.BlockSpec(memory_space=pltpu.VMEM)] * 3,
+        in_specs=[pl.BlockSpec(memory_space=pltpu.VMEM)] * 4,
         out_specs=pl.BlockSpec(memory_space=pltpu.HBM),
         scratch_shapes=[
             pltpu.VMEM((pieces * slot, quarter), jnp.bfloat16),
@@ -207,7 +215,7 @@
         ),
         compiler_params=pltpu.CompilerParams(vmem_limit_bytes=24 * MIB),
         name="gram",
-    )(stored, cols, cur)
+    )(stored, cols, cur, moved)
 
 
 def local(
@@ -234,8 +242,20 @@
     tensor_bits = bits_of(tensor_count)
     tensor_rounds = [*zip(tensor_bits, turned(tensor_bits), strict=True)]
 
-    rows = stored_grads[None]
-    for bits in dp_rounds:
+    moved = swap(stored_grads, "dp", *dp_rounds[0])
+    total, stored = project(
+        inputs_x,
+        hidden,
+        grad_up,
+        grad_down,
+        proj_in_up,
+        proj_in_down,
+        proj_out_up,
+        proj_out_down,
+        stored_grads,
+    )
+    rows = jnp.stack([stored, moved])
+    for n, bits in enumerate(dp_rounds[1:], 1):
         moved = swap(rows, "dp", *bits)
         rows = jnp.concatenate([rows, moved], axis=0)
     cols = lax.dynamic_slice_in_dim(rows, i * sub_width, sub_width, 2)[None]
@@ -245,26 +265,17 @@
         cols = jnp.concatenate([cols, moved], axis=0)
         offsets += [(even ^ bits[0], odd ^ bits[1]) for even, odd in offsets]
 
-    total = project(
-        inputs_x,
-        hidden,
-        grad_up,
-        grad_down,
-        proj_in_up,
-        proj_in_down,
-        proj_out_up,
-        proj_out_down,
-    )
     for n, bits in enumerate(tensor_rounds):
         other = swap(total, "tensor", *bits)
         if n < len(tensor_rounds) - 1:
             total = total + other
     cur = current_rows(lengths, total, other, proj_width)
     cur = cur.reshape(1, examples, proj_width * LAYERS * proj_width)
-    for bits in dp_rounds:
+    for n, bits in enumerate(dp_rounds):
         moved = swap(cur, "dp", *bits)
-        cur = jnp.concatenate([cur, moved], axis=0)
-    product = gram(rows, cols, cur, offsets)
+        if n < len(dp_rounds) - 1:
+            cur = jnp.concatenate([cur, moved], axis=0)
+    product = gram(rows, cols, cur, moved, offsets)
     return product.reshape(quarter, 1, tensor_count * sub_width)
 
 

time: 41.9 us -> 41.8 us (level)
  the two profiles are of different devices: /device:TPU:24 before, /device:TPU:0 now
where the time goes in v4:
time: 41.8 us; the launch traced here: 41.7 us
  starting transfers between devices  17.8 us (43%)
  waiting for transfers between devices  16.8 us (40%)
  Pallas kernels  6.4 us (15%)
    ppermute x10, starting transfers between devices, swap(): return lax.ppermute(value, ('dp', 'tensor'), pairs)  17.8 us
    ppermute x10, waiting for transfers between devices, swap(): return lax.ppermute(value, ('dp', 'tensor'), pairs)  16.8 us
    pallas_call x1, Pallas kernels, project(): pl.pallas_call(project_kernel, out_shape=(jax.ShapeDtypeStruct((2 * rows,...  2.98 us
    pallas_call x1, Pallas kernels, gram(): pl.pallas_call(functools.partial(gram_kernel, scale, offsets), out_shape=...  2.56 us
    pallas_call x1, Pallas kernels, current_rows(): pl.pallas_call(current_kernel, out_shape=jax.ShapeDtypeStruct((examples,...  0.86 us
  transfers between devices with their start and end apart: 10, of which 6 were waited for; matrix products, arithmetic and copies ran while one was open for 1% of the time, Pallas kernels for 2%

profile of v4, /device:TPU:0, one launch (start us, length us, event | category | flops | bytes accessed | tf_op | source)
XLA Modules:
  0.0 41.7 jit_solution(18309924142312519133)
XLA Ops:
  0.0 0.0 copy-start
  0.0 3.0 %project.1 = (f32[256,128]{1,0:T(8,128)S(1)}, bf16[26,2048]{1,0:T(8,128)(2,1)S(1)}) custom-call(bf16[128,1024]{1,0:T(8,128)(2,1)} %x.1, bf16[128,3584]{1,0:T(8,128)(2,1)} %h.1, bf16[128,3584]{1,0:T(8,128)(2,1)} %gu.1, bf16[128,1024]{1,0:T(8,128)(2,1)} %gd.1, bf16[64,1024]{1,0:T(8,128)(2,1)} %bitcast.17, bf16[64,3584]{1,0:T(8,128)(2,1)} %bitcast.15, ...), custom_call_target="tpu_custom_call" | custom-call | flops 150994944 | bytes 3645440 | tf_op jit(solution)/shard_map/project/pallas_call | solution.py:78
  3.0 3.1 %collective-permute-start.5 = (f32[256,128]{1,0:T(8,128)S(1)}, f32[256,128]{1,0:T(8,128)S(1)}, u32[]{:S(2)}, u32[]{:S(2)}) collective-permute-start(f32[256,128]{1,0:T(8,128)S(1)} %get-tuple-element.8), channel_id=1, source_target_pairs={{0,1},{1,0},{2,3},{3,2},{4,6},{5,7},{6,4},{7,5},{8,9},{9,8},{10,11... | collective-permute-start | bytes 393224 | tf_op jit(solution)/shard_map/ppermute | solution.py:41
  6.1 1.5 %collective-permute-start = (bf16[26,2048]{1,0:T(8,128)(2,1)}, bf16[26,2048]{1,0:T(8,128)(2,1)S(1)}, u32[]{:S(2)}, u32[]{:S(2)}) collective-permute-start(bf16[26,2048]{1,0:T(8,128)(2,1)} %stored.1), channel_id=1, source_target_pairs={{0,8},{1,9},{2,10},{3,11},{4,20},{5,21},{6,22},{7,23},{8,0},{9,1},... | collective-permute-start | bytes 319496 | tf_op jit(solution)/shard_map/ppermute | solution.py:41
  7.6 2.6 %collective-permute-done.5 = f32[256,128]{1,0:T(8,128)S(1)} collective-permute-done((f32[256,128]{1,0:T(8,128)S(1)}, f32[256,128]{1,0:T(8,128)S(1)}, u32[]{:S(2)}, u32[]{:S(2)}) %collective-permute-start.5) | collective-permute-done | bytes 131104 | tf_op jit(solution)/shard_map/ppermute | solution.py:41
  10.2 2.3 %collective-permute-start.6 = (f32[256,128]{1,0:T(8,128)S(1)}, f32[256,128]{1,0:T(8,128)S(1)}, u32[]{:S(2)}, u32[]{:S(2)}) collective-permute-start(f32[256,128]{1,0:T(8,128)S(1)} %add.7.own), channel_id=1, source_target_pairs={{0,2},{1,3},{2,0},{3,1},{4,5},{5,4},{6,7},{7,6},{8,10},{9,11},{10,... | collective-permute-start | bytes 393224 | tf_op jit(solution)/shard_map/ppermute | solution.py:41
  12.5 0.0 collective-permute-done
  12.5 1.6 %collective-permute-start.1 = (bf16[2,26,2048]{2,1,0:T(8,128)(2,1)S(1)}, bf16[2,26,2048]{2,1,0:T(8,128)(2,1)S(1)}, u32[]{:S(2)}, u32[]{:S(2)}) collective-permute-start(bf16[2,26,2048]{2,1,0:T(8,128)(2,1)S(1)} %pad_maximum_fusion.3), channel_id=1, source_target_pairs={{0,16},{1,17},{2,18},{3,19},{4,12},{5,13},{6,14},{7,15},{8,24},{9,... | collective-permute-start | bytes 638984 | tf_op jit(solution)/shard_map/ppermute | solution.py:41
  14.1 2.0 %collective-permute-done.6.other = f32[256,128]{1,0:T(8,128)S(1)} collective-permute-done((f32[256,128]{1,0:T(8,128)S(1)}, f32[256,128]{1,0:T(8,128)S(1)}, u32[]{:S(2)}, u32[]{:S(2)}) %collective-permute-start.6) | collective-permute-done | bytes 131104 | tf_op jit(solution)/shard_map/ppermute | solution.py:41
  16.1 0.0 copy-done
  16.1 0.9 %current.1 = bf16[2,64,128]{2,1,0:T(8,128)(2,1)S(1)} custom-call(s32[2]{0:T(128)S(1)} %copy-done, f32[256,128]{1,0:T(8,128)S(1)} %add.7.own, f32[256,128]{1,0:T(8,128)S(1)} %collective-permute-done.6.other), custom_call_target="tpu_custom_call" | custom-call | flops 4194304 | bytes 262144 | tf_op jit(solution)/shard_map/current/pallas_call | solution.py:122
  17.0 2.0 %collective-permute-start.7 = (bf16[1,2,8192]{2,1,0:T(2,128)(2,1)S(1)}, bf16[1,2,8192]{2,1,0:T(2,128)(2,1)S(1)}, u32[]{:S(2)}, u32[]{:S(2)}) collective-permute-start(bf16[1,2,8192]{2,1,0:T(2,128)(2,1)S(1)} %reshape.6), channel_id=1, source_target_pairs={{0,8},{1,9},{2,10},{3,11},{4,20},{5,21},{6,22},{7,23},{8,0},{9,1},... | collective-permute-start | bytes 98312 | tf_op jit(solution)/shard_map/ppermute | solution.py:41
  19.1 0.2 collective-permute-done.1
  19.3 0.1 pad_maximum_fusion.1
  19.4 0.1 collective-permute-start.2
  19.5 1.5 %collective-permute-done.7 = bf16[1,2,8192]{2,1,0:T(2,128)(2,1)S(1)} collective-permute-done((bf16[1,2,8192]{2,1,0:T(2,128)(2,1)S(1)}, bf16[1,2,8192]{2,1,0:T(2,128)(2,1)S(1)}, u32[]{:S(2)}, u32[]{:S(2)}) %collective-permute-start.7) | collective-permute-done | bytes 32800 | tf_op jit(solution)/shard_map/ppermute | solution.py:41
  21.0 0.1 pad_maximum_fusion.5
  21.1 2.0 %collective-permute-start.8 = (bf16[2,2,8192]{2,1,0:T(2,128)(2,1)S(1)}, bf16[2,2,8192]{2,1,0:T(2,128)(2,1)S(1)}, u32[]{:S(2)}, u32[]{:S(2)}) collective-permute-start(bf16[2,2,8192]{2,1,0:T(2,128)(2,1)S(1)} %pad_maximum_fusion.5), channel_id=1, source_target_pairs={{0,16},{1,17},{2,18},{3,19},{4,12},{5,13},{6,14},{7,15},{8,24},{9,... | collective-permute-start | bytes 196616 | tf_op jit(solution)/shard_map/ppermute | solution.py:41
  23.1 0.0 collective-permute-done.2
  23.1 0.1 pad_maximum_fusion.stored
  23.3 1.9 %collective-permute-start.3 = (bf16[1,8,26,256]{3,2,1,0:T(8,128)(2,1)S(1)}, bf16[1,8,26,256]{3,2,1,0:T(8,128)(2,1)S(1)}, u32[]{:S(2)}, u32[]{:S(2)}) collective-permute-start(bf16[1,8,26,256]{3,2,1,0:T(8,128)(2,1)S(1)} %dynamic-slice_bitcast_fusion), channel_id=1, source_target_pairs={{0,2},{1,3},{2,0},{3,1},{4,5},{5,4},{6,7},{7,6},{8,10},{9,11},{10,... | collective-permute-start | bytes 319496 | tf_op jit(solution)/shard_map/ppermute | solution.py:41
  25.2 5.5 %collective-permute-done.3 = bf16[1,8,26,256]{3,2,1,0:T(8,128)(2,1)S(1)} collective-permute-done((bf16[1,8,26,256]{3,2,1,0:T(8,128)(2,1)S(1)}, bf16[1,8,26,256]{3,2,1,0:T(8,128)(2,1)S(1)}, u32[]{:S(2)}, u32[]{:S(2)}) %collective-permute-start.3) | collective-permute-done | bytes 106528 | tf_op jit(solution)/shard_map/ppermute | solution.py:41
  30.7 3.3 %collective-permute-start.4 = (bf16[2,8,26,256]{3,2,1,0:T(8,128)(2,1)S(1)}, bf16[2,8,26,256]{3,2,1,0:T(8,128)(2,1)S(1)}, u32[]{:S(2)}, u32[]{:S(2)}) collective-permute-start(bf16[2,8,26,256]{3,2,1,0:T(8,128)(2,1)S(1)} %pad_maximum_fusion.4), channel_id=1, source_target_pairs={{0,1},{1,0},{2,3},{3,2},{4,6},{5,7},{6,4},{7,5},{8,9},{9,8},{10,11... | collective-permute-start | bytes 638984 | tf_op jit(solution)/shard_map/ppermute | solution.py:41
  34.0 0.0 collective-permute-done.8
  34.0 0.1 constant_dynamic-update-slice_fusion.cur
  34.0 0.1 collective-permute-start.9
  34.1 5.0 %collective-permute-done.4 = bf16[2,8,26,256]{3,2,1,0:T(8,128)(2,1)S(1)} collective-permute-done((bf16[2,8,26,256]{3,2,1,0:T(8,128)(2,1)S(1)}, bf16[2,8,26,256]{3,2,1,0:T(8,128)(2,1)S(1)}, u32[]{:S(2)}, u32[]{:S(2)}) %collective-permute-start.4) | collective-permute-done | bytes 213024 | tf_op jit(solution)/shard_map/ppermute | solution.py:41
  39.1 0.1 pad_maximum_fusion.2.cols
  39.1 0.0 collective-permute-done.9.moved
  39.1 2.6 %gram.1 = bf16[2048,1024]{1,0:T(8,128)(2,1)} custom-call(bf16[8,26,2048]{2,1,0:T(8,128)(2,1)S(1)} %pad_maximum_fusion.stored, bf16[4,8,26,256]{3,2,1,0:T(8,128)(2,1)S(1)} %pad_maximum_fusion.2.cols, bf16[4,2,8192]{2,1,0:T(2,128)(2,1)S(1)} %constant_dynamic-update-slice_fusion.cur, bf16[4,2,8192]{2,1,0:T(2,128)(2,1)S(1)} %collective-permute-done.9.moved), custom_call_target="tpu_custom_call" | custom-call | flops 1073741824 | bytes 4194304 | tf_op jit(solution)/shard_map/gram/pallas_call | solution.py:200
  (7 shorter events, 0.2 us)
Async XLA Ops:
  0.0 16.1 %copy-start = (s32[2]{0:T(128)S(1)}, s32[2]{0:T(128)}, u32[]{:S(2)}) copy-start(s32[2]{0:T(128)} %lengths.1) | copy-start | bytes 28
  3.0 7.2 %collective-permute-start.5 = (f32[256,128]{1,0:T(8,128)S(1)}, f32[256,128]{1,0:T(8,128)S(1)}, u32[]{:S(2)}, u32[]{:S(2)}) collective-permute-start(f32[256,128]{1,0:T(8,128)S(1)} %get-tuple-element.8), channel_id=1, source_target_pairs={{0,1},{1,0},{2,3},{3,2},{4,6},{5,7},{6,4},{7,5},{8,9},{9,8},{10,11... | collective-permute-start | bytes 393224 | tf_op jit(solution)/shard_map/ppermute | solution.py:41
  6.1 6.4 %collective-permute-start = (bf16[26,2048]{1,0:T(8,128)(2,1)}, bf16[26,2048]{1,0:T(8,128)(2,1)S(1)}, u32[]{:S(2)}, u32[]{:S(2)}) collective-permute-start(bf16[26,2048]{1,0:T(8,128)(2,1)} %stored.1), channel_id=1, source_target_pairs={{0,8},{1,9},{2,10},{3,11},{4,20},{5,21},{6,22},{7,23},{8,0},{9,1},... | collective-permute-start | bytes 319496 | tf_op jit(solution)/shard_map/ppermute | solution.py:41
  10.2 5.9 %collective-permute-start.6 = (f32[256,128]{1,0:T(8,128)S(1)}, f32[256,128]{1,0:T(8,128)S(1)}, u32[]{:S(2)}, u32[]{:S(2)}) collective-permute-start(f32[256,128]{1,0:T(8,128)S(1)} %add.7.own), channel_id=1, source_target_pairs={{0,2},{1,3},{2,0},{3,1},{4,5},{5,4},{6,7},{7,6},{8,10},{9,11},{10,... | collective-permute-start | bytes 393224 | tf_op jit(solution)/shard_map/ppermute | solution.py:41
  12.5 6.8 %collective-permute-start.1 = (bf16[2,26,2048]{2,1,0:T(8,128)(2,1)S(1)}, bf16[2,26,2048]{2,1,0:T(8,128)(2,1)S(1)}, u32[]{:S(2)}, u32[]{:S(2)}) collective-permute-start(bf16[2,26,2048]{2,1,0:T(8,128)(2,1)S(1)} %pad_maximum_fusion.3), channel_id=1, source_target_pairs={{0,16},{1,17},{2,18},{3,19},{4,12},{5,13},{6,14},{7,15},{8,24},{9,... | collective-permute-start | bytes 638984 | tf_op jit(solution)/shard_map/ppermute | solution.py:41
  17.0 4.0 %collective-permute-start.7 = (bf16[1,2,8192]{2,1,0:T(2,128)(2,1)S(1)}, bf16[1,2,8192]{2,1,0:T(2,128)(2,1)S(1)}, u32[]{:S(2)}, u32[]{:S(2)}) collective-permute-start(bf16[1,2,8192]{2,1,0:T(2,128)(2,1)S(1)} %reshape.6), channel_id=1, source_target_pairs={{0,8},{1,9},{2,10},{3,11},{4,20},{5,21},{6,22},{7,23},{8,0},{9,1},... | collective-permute-start | bytes 98312 | tf_op jit(solution)/shard_map/ppermute | solution.py:41
  19.4 3.8 %collective-permute-start.2 = (bf16[4,26,2048]{2,1,0:T(8,128)(2,1)S(1)}, bf16[4,26,2048]{2,1,0:T(8,128)(2,1)S(1)}, u32[]{:S(2)}, u32[]{:S(2)}) collective-permute-start(bf16[4,26,2048]{2,1,0:T(8,128)(2,1)S(1)} %pad_maximum_fusion.1), channel_id=1, source_target_pairs={{0,4},{1,5},{2,6},{3,7},{4,0},{5,1},{6,2},{7,3},{8,12},{9,13},{10,... | collective-permute-start | bytes 1277960 | tf_op jit(solution)/shard_map/ppermute | solution.py:41
  21.1 12.9 %collective-permute-start.8 = (bf16[2,2,8192]{2,1,0:T(2,128)(2,1)S(1)}, bf16[2,2,8192]{2,1,0:T(2,128)(2,1)S(1)}, u32[]{:S(2)}, u32[]{:S(2)}) collective-permute-start(bf16[2,2,8192]{2,1,0:T(2,128)(2,1)S(1)} %pad_maximum_fusion.5), channel_id=1, source_target_pairs={{0,16},{1,17},{2,18},{3,19},{4,12},{5,13},{6,14},{7,15},{8,24},{9,... | collective-permute-start | bytes 196616 | tf_op jit(solution)/shard_map/ppermute | solution.py:41
  23.3 7.3 %collective-permute-start.3 = (bf16[1,8,26,256]{3,2,1,0:T(8,128)(2,1)S(1)}, bf16[1,8,26,256]{3,2,1,0:T(8,128)(2,1)S(1)}, u32[]{:S(2)}, u32[]{:S(2)}) collective-permute-start(bf16[1,8,26,256]{3,2,1,0:T(8,128)(2,1)S(1)} %dynamic-slice_bitcast_fusion), channel_id=1, source_target_pairs={{0,2},{1,3},{2,0},{3,1},{4,5},{5,4},{6,7},{7,6},{8,10},{9,11},{10,... | collective-permute-start | bytes 319496 | tf_op jit(solution)/shard_map/ppermute | solution.py:41
  30.7 8.4 %collective-permute-start.4 = (bf16[2,8,26,256]{3,2,1,0:T(8,128)(2,1)S(1)}, bf16[2,8,26,256]{3,2,1,0:T(8,128)(2,1)S(1)}, u32[]{:S(2)}, u32[]{:S(2)}) collective-permute-start(bf16[2,8,26,256]{3,2,1,0:T(8,128)(2,1)S(1)} %pad_maximum_fusion.4), channel_id=1, source_target_pairs={{0,1},{1,0},{2,3},{3,2},{4,6},{5,7},{6,4},{7,5},{8,9},{9,8},{10,11... | collective-permute-start | bytes 638984 | tf_op jit(solution)/shard_map/ppermute | solution.py:41
  34.0 5.1 %collective-permute-start.9 = (bf16[4,2,8192]{2,1,0:T(2,128)(2,1)S(1)}, bf16[4,2,8192]{2,1,0:T(2,128)(2,1)S(1)}, u32[]{:S(2)}, u32[]{:S(2)}) collective-permute-start(bf16[4,2,8192]{2,1,0:T(2,128)(2,1)S(1)} %constant_dynamic-update-slice_fusion.cur), channel_id=1, source_target_pairs={{0,4},{1,5},{2,6},{3,7},{4,0},{5,1},{6,2},{7,3},{8,12},{9,13},{10,... | collective-permute-start | bytes 393224 | tf_op jit(solution)/shard_map/ppermute | solution.py:41

commit v5 on v4

--- a/solution.py
+++ b/solution.py
@@ -144,9 +144,11 @@
     return (LAYERS * proj_width) ** 2
 
 
-def gram_kernel(scale, offsets, stored, cols, cur, moved, out, left, right, buf, sem):
-    pieces, old, quarter = stored.shape
-    half, new = cur.shape[:2]
+def gram_kernel(
+    scale, offsets, stored, near, cols, cur, moved, out, left, right, buf, sem
+):
+    half, old, quarter = stored.shape
+    pieces, new = 2 * half, cur.shape[1]
     sub = cols.shape[-1]
     slot = left.shape[0] // pieces
     q, i = lax.axis_index("tensor"), lax.axis_index("dp")
@@ -155,8 +157,8 @@
     right[...] = jnp.zeros_like(right)
     for p in range(pieces):
         base = p * slot
-        fresh = cur if p < half else moved
-        left[base : base + old, :] = stored[p]
+        here, fresh = (stored, cur) if p < half else (near, moved)
+        left[base : base + old, :] = here[p % half]
         left[base + old : base + old + new, :] = fresh[p % half, :, place]
     for block in range(len(offsets)):
         to = slice(block * sub, (block + 1) * sub)
@@ -190,8 +192,9 @@
         copy.wait()
 
 
-def gram(stored, cols, cur, moved, offsets):
-    pieces, old, quarter = stored.shape
+def gram(stored, near, cols, cur, moved, offsets):
+    half, old, quarter = stored.shape
+    pieces = 2 * half
     new = cur.shape[1]
     slot = -(-(old + new) // SLOT) * SLOT
     width = cols.shape[0] * cols.shape[-1]
@@ -200,7 +203,7 @@
     return pl.pallas_call(
         functools.partial(gram_kernel, scale, offsets),
         out_shape=jax.ShapeDtypeStruct((quarter, width), jnp.bfloat16),
-        in_specs=[pl.BlockSpec(memory_space=pltpu.VMEM)] * 4,
+        in_specs=[pl.BlockSpec(memory_space=pltpu.VMEM)] * 5,
         out_specs=pl.BlockSpec(memory_space=pltpu.HBM),
         scratch_shapes=[
             pltpu.VMEM((pieces * slot, quarter), jnp.bfloat16),
@@ -215,7 +218,7 @@
         ),
         compiler_params=pltpu.CompilerParams(vmem_limit_bytes=24 * MIB),
         name="gram",
-    )(stored, cols, cur, moved)
+    )(stored, near, cols, cur, moved)
 
 
 def local(
@@ -255,10 +258,14 @@
         stored_grads,
     )
     rows = jnp.stack([stored, moved])
-    for n, bits in enumerate(dp_rounds[1:], 1):
+    for n, bits in enumerate(dp_rounds[1:-1], 1):
         moved = swap(rows, "dp", *bits)
         rows = jnp.concatenate([rows, moved], axis=0)
-    cols = lax.dynamic_slice_in_dim(rows, i * sub_width, sub_width, 2)[None]
+    give = lax.dynamic_slice_in_dim(rows, (i ^ 1) * sub_width, sub_width, 2)
+    got = swap(give, "dp", 1, 1)
+    cols = lax.dynamic_slice_in_dim(rows, i * sub_width, sub_width, 2)
+    cols = jnp.concatenate([cols, got], axis=0)[None]
+    near = swap(rows, "dp", 1, 1)
     offsets = [(0, 0)]
     for bits in reversed(tensor_rounds):
         moved = swap(cols, "tensor", *bits)
@@ -275,7 +282,7 @@
         moved = swap(cur, "dp", *bits)
         if n < len(dp_rounds) - 1:
             cur = jnp.concatenate([cur, moved], axis=0)
-    product = gram(rows, cols, cur, moved, offsets)
+    product = gram(rows, near, cols, cur, moved, offsets)
     return product.reshape(quarter, 1, tensor_count * sub_width)
 
 

time: 41.8 us -> 41.7 us (level)
  starting transfers between devices: 17.8 us -> 18.3 us
  waiting for transfers between devices: 16.8 us -> 16.3 us
    ppermute x10 -> x11, waiting for transfers between devices: 16.8 us -> 16.3 us  [swap(): return lax.ppermute(value, ('dp', 'tensor'), pairs)]
    ppermute x10 -> x11, starting transfers between devices: 17.8 us -> 18.3 us  [swap(): return lax.ppermute(value, ('dp', 'tensor'), pairs)]
  transfers between devices with their start and end apart: 10 -> 11, of which waited for: 6 -> 6; matrix products, arithmetic and copies ran while one was open for 1% -> 1% of each run, Pallas kernels for 2% -> 2%
where the time goes in v5:
time: 41.7 us; the launch traced here: 41.6 us
  starting transfers between devices  18.3 us (44%)
  waiting for transfers between devices  16.3 us (39%)
  Pallas kernels  6.4 us (15%)
    ppermute x11, starting transfers between devices, swap(): return lax.ppermute(value, ('dp', 'tensor'), pairs)  18.3 us
    ppermute x11, waiting for transfers between devices, swap(): return lax.ppermute(value, ('dp', 'tensor'), pairs)  16.3 us
    pallas_call x1, Pallas kernels, project(): pl.pallas_call(project_kernel, out_shape=(jax.ShapeDtypeStruct((2 * rows,...  2.98 us
    pallas_call x1, Pallas kernels, gram(): pl.pallas_call(functools.partial(gram_kernel, scale, offsets), out_shape=...  2.56 us
    pallas_call x1, Pallas kernels, current_rows(): pl.pallas_call(current_kernel, out_shape=jax.ShapeDtypeStruct((examples,...  0.86 us
  transfers between devices with their start and end apart: 11, of which 6 were waited for; matrix products, arithmetic and copies ran while one was open for 1% of the time, Pallas kernels for 2%

profile of v5, /device:TPU:0, one launch (start us, length us, event | category | flops | bytes accessed | tf_op | source)
XLA Modules:
  0.0 41.6 jit_solution(3871158444708611803)
XLA Ops:
  0.0 0.0 copy-start
  0.0 3.0 %project.1 = (f32[256,128]{1,0:T(8,128)S(1)}, bf16[26,2048]{1,0:T(8,128)(2,1)S(1)}) custom-call(bf16[128,1024]{1,0:T(8,128)(2,1)} %x.1, bf16[128,3584]{1,0:T(8,128)(2,1)} %h.1, bf16[128,3584]{1,0:T(8,128)(2,1)} %gu.1, bf16[128,1024]{1,0:T(8,128)(2,1)} %gd.1, bf16[64,1024]{1,0:T(8,128)(2,1)} %bitcast.15, bf16[64,3584]{1,0:T(8,128)(2,1)} %bitcast.13, ...), custom_call_target="tpu_custom_call" | custom-call | flops 150994944 | bytes 3645440 | tf_op jit(solution)/shard_map/project/pallas_call | solution.py:78
  3.0 3.1 %collective-permute-start.6 = (f32[256,128]{1,0:T(8,128)S(1)}, f32[256,128]{1,0:T(8,128)S(1)}, u32[]{:S(2)}, u32[]{:S(2)}) collective-permute-start(f32[256,128]{1,0:T(8,128)S(1)} %get-tuple-element.8), channel_id=1, source_target_pairs={{0,1},{1,0},{2,3},{3,2},{4,6},{5,7},{6,4},{7,5},{8,9},{9,8},{10,11... | collective-permute-start | bytes 393224 | tf_op jit(solution)/shard_map/ppermute | solution.py:41
  6.1 1.5 %collective-permute-start = (bf16[26,2048]{1,0:T(8,128)(2,1)}, bf16[26,2048]{1,0:T(8,128)(2,1)S(1)}, u32[]{:S(2)}, u32[]{:S(2)}) collective-permute-start(bf16[26,2048]{1,0:T(8,128)(2,1)} %stored.1), channel_id=1, source_target_pairs={{0,8},{1,9},{2,10},{3,11},{4,20},{5,21},{6,22},{7,23},{8,0},{9,1},... | collective-permute-start | bytes 319496 | tf_op jit(solution)/shard_map/ppermute | solution.py:41
  7.6 2.6 %collective-permute-done.6 = f32[256,128]{1,0:T(8,128)S(1)} collective-permute-done((f32[256,128]{1,0:T(8,128)S(1)}, f32[256,128]{1,0:T(8,128)S(1)}, u32[]{:S(2)}, u32[]{:S(2)}) %collective-permute-start.6) | collective-permute-done | bytes 131104 | tf_op jit(solution)/shard_map/ppermute | solution.py:41
  10.2 2.3 %collective-permute-start.7 = (f32[256,128]{1,0:T(8,128)S(1)}, f32[256,128]{1,0:T(8,128)S(1)}, u32[]{:S(2)}, u32[]{:S(2)}) collective-permute-start(f32[256,128]{1,0:T(8,128)S(1)} %add.11.own), channel_id=1, source_target_pairs={{0,2},{1,3},{2,0},{3,1},{4,5},{5,4},{6,7},{7,6},{8,10},{9,11},{10,... | collective-permute-start | bytes 393224 | tf_op jit(solution)/shard_map/ppermute | solution.py:41
  12.5 0.0 collective-permute-done
  12.5 1.6 %collective-permute-start.1 = (bf16[2,26,2048]{2,1,0:T(8,128)(2,1)S(1)}, bf16[2,26,2048]{2,1,0:T(8,128)(2,1)S(1)}, u32[]{:S(2)}, u32[]{:S(2)}) collective-permute-start(bf16[2,26,2048]{2,1,0:T(8,128)(2,1)S(1)} %pad_maximum_fusion.2), channel_id=1, source_target_pairs={{0,16},{1,17},{2,18},{3,19},{4,12},{5,13},{6,14},{7,15},{8,24},{9,... | collective-permute-start | bytes 638984 | tf_op jit(solution)/shard_map/ppermute | solution.py:41
  14.1 2.0 %collective-permute-done.7.other = f32[256,128]{1,0:T(8,128)S(1)} collective-permute-done((f32[256,128]{1,0:T(8,128)S(1)}, f32[256,128]{1,0:T(8,128)S(1)}, u32[]{:S(2)}, u32[]{:S(2)}) %collective-permute-start.7) | collective-permute-done | bytes 131104 | tf_op jit(solution)/shard_map/ppermute | solution.py:41
  16.1 0.0 copy-done
  16.1 0.9 %current.1 = bf16[2,64,128]{2,1,0:T(8,128)(2,1)S(1)} custom-call(s32[2]{0:T(128)S(1)} %copy-done, f32[256,128]{1,0:T(8,128)S(1)} %add.11.own, f32[256,128]{1,0:T(8,128)S(1)} %collective-permute-done.7.other), custom_call_target="tpu_custom_call" | custom-call | flops 4194304 | bytes 262144 | tf_op jit(solution)/shard_map/current/pallas_call | solution.py:122
  17.0 2.0 %collective-permute-start.8 = (bf16[1,2,8192]{2,1,0:T(2,128)(2,1)S(1)}, bf16[1,2,8192]{2,1,0:T(2,128)(2,1)S(1)}, u32[]{:S(2)}, u32[]{:S(2)}) collective-permute-start(bf16[1,2,8192]{2,1,0:T(2,128)(2,1)S(1)} %reshape.6), channel_id=1, source_target_pairs={{0,8},{1,9},{2,10},{3,11},{4,20},{5,21},{6,22},{7,23},{8,0},{9,1},... | collective-permute-start | bytes 98312 | tf_op jit(solution)/shard_map/ppermute | solution.py:41
  19.1 0.2 collective-permute-done.1
  19.3 0.1 pad_maximum_fusion.stored
  19.4 0.1 collective-permute-start.3
  19.5 1.5 %collective-permute-done.8 = bf16[1,2,8192]{2,1,0:T(2,128)(2,1)S(1)} collective-permute-done((bf16[1,2,8192]{2,1,0:T(2,128)(2,1)S(1)}, bf16[1,2,8192]{2,1,0:T(2,128)(2,1)S(1)}, u32[]{:S(2)}, u32[]{:S(2)}) %collective-permute-start.8) | collective-permute-done | bytes 32800 | tf_op jit(solution)/shard_map/ppermute | solution.py:41
  21.0 0.1 pad_maximum_fusion.4
  21.1 2.0 %collective-permute-start.9 = (bf16[2,2,8192]{2,1,0:T(2,128)(2,1)S(1)}, bf16[2,2,8192]{2,1,0:T(2,128)(2,1)S(1)}, u32[]{:S(2)}, u32[]{:S(2)}) collective-permute-start(bf16[2,2,8192]{2,1,0:T(2,128)(2,1)S(1)} %pad_maximum_fusion.4), channel_id=1, source_target_pairs={{0,16},{1,17},{2,18},{3,19},{4,12},{5,13},{6,14},{7,15},{8,24},{9,... | collective-permute-start | bytes 196616 | tf_op jit(solution)/shard_map/ppermute | solution.py:41
  23.1 0.0 collective-permute-done.3
  23.2 1.9 %collective-permute-start.4 = (bf16[1,8,26,256]{3,2,1,0:T(8,128)(2,1)S(1)}, bf16[1,8,26,256]{3,2,1,0:T(8,128)(2,1)S(1)}, u32[]{:S(2)}, u32[]{:S(2)}) collective-permute-start(bf16[1,8,26,256]{3,2,1,0:T(8,128)(2,1)S(1)} %maximum_bitcast_fusion), channel_id=1, source_target_pairs={{0,2},{1,3},{2,0},{3,1},{4,5},{5,4},{6,7},{7,6},{8,10},{9,11},{10,... | collective-permute-start | bytes 319496 | tf_op jit(solution)/shard_map/ppermute | solution.py:41
  25.1 0.1 collective-permute-start.2
  25.1 5.4 %collective-permute-done.4 = bf16[1,8,26,256]{3,2,1,0:T(8,128)(2,1)S(1)} collective-permute-done((bf16[1,8,26,256]{3,2,1,0:T(8,128)(2,1)S(1)}, bf16[1,8,26,256]{3,2,1,0:T(8,128)(2,1)S(1)}, u32[]{:S(2)}, u32[]{:S(2)}) %collective-permute-start.4) | collective-permute-done | bytes 106528 | tf_op jit(solution)/shard_map/ppermute | solution.py:41
  30.5 3.7 %collective-permute-start.5 = (bf16[2,8,26,256]{3,2,1,0:T(8,128)(2,1)S(1)}, bf16[2,8,26,256]{3,2,1,0:T(8,128)(2,1)S(1)}, u32[]{:S(2)}, u32[]{:S(2)}) collective-permute-start(bf16[2,8,26,256]{3,2,1,0:T(8,128)(2,1)S(1)} %pad_maximum_fusion.3), channel_id=1, source_target_pairs={{0,1},{1,0},{2,3},{3,2},{4,6},{5,7},{6,4},{7,5},{8,9},{9,8},{10,11... | collective-permute-start | bytes 638984 | tf_op jit(solution)/shard_map/ppermute | solution.py:41
  34.3 0.0 collective-permute-done.9
  34.3 0.1 constant_dynamic-update-slice_fusion.cur
  34.3 0.1 collective-permute-start.10
  34.4 4.5 %collective-permute-done.5 = bf16[2,8,26,256]{3,2,1,0:T(8,128)(2,1)S(1)} collective-permute-done((bf16[2,8,26,256]{3,2,1,0:T(8,128)(2,1)S(1)}, bf16[2,8,26,256]{3,2,1,0:T(8,128)(2,1)S(1)}, u32[]{:S(2)}, u32[]{:S(2)}) %collective-permute-start.5) | collective-permute-done | bytes 213024 | tf_op jit(solution)/shard_map/ppermute | solution.py:41
  38.9 0.1 pad_maximum_fusion.1.cols
  39.0 0.0 collective-permute-done.10.moved
  39.0 0.0 collective-permute-done.2.near
  39.0 2.6 %gram.1 = bf16[2048,1024]{1,0:T(8,128)(2,1)} custom-call(bf16[4,26,2048]{2,1,0:T(8,128)(2,1)S(1)} %pad_maximum_fusion.stored, bf16[4,26,2048]{2,1,0:T(8,128)(2,1)S(1)} %collective-permute-done.2.near, bf16[4,8,26,256]{3,2,1,0:T(8,128)(2,1)S(1)} %pad_maximum_fusion.1.cols, bf16[4,2,8192]{2,1,0:T(2,128)(2,1)S(1)} %constant_dynamic-update-slice_fusion.cur, ...), custom_call_target="tpu_custom_call" | custom-call | flops 1073741824 | bytes 4194304 | tf_op jit(solution)/shard_map/gram/pallas_call | solution.py:203
  (8 shorter events, 0.2 us)
Async XLA Ops:
  0.0 16.1 %copy-start = (s32[2]{0:T(128)S(1)}, s32[2]{0:T(128)}, u32[]{:S(2)}) copy-start(s32[2]{0:T(128)} %lengths.1) | copy-start | bytes 28
  3.0 7.2 %collective-permute-start.6 = (f32[256,128]{1,0:T(8,128)S(1)}, f32[256,128]{1,0:T(8,128)S(1)}, u32[]{:S(2)}, u32[]{:S(2)}) collective-permute-start(f32[256,128]{1,0:T(8,128)S(1)} %get-tuple-element.8), channel_id=1, source_target_pairs={{0,1},{1,0},{2,3},{3,2},{4,6},{5,7},{6,4},{7,5},{8,9},{9,8},{10,11... | collective-permute-start | bytes 393224 | tf_op jit(solution)/shard_map/ppermute | solution.py:41
  6.1 6.4 %collective-permute-start = (bf16[26,2048]{1,0:T(8,128)(2,1)}, bf16[26,2048]{1,0:T(8,128)(2,1)S(1)}, u32[]{:S(2)}, u32[]{:S(2)}) collective-permute-start(bf16[26,2048]{1,0:T(8,128)(2,1)} %stored.1), channel_id=1, source_target_pairs={{0,8},{1,9},{2,10},{3,11},{4,20},{5,21},{6,22},{7,23},{8,0},{9,1},... | collective-permute-start | bytes 319496 | tf_op jit(solution)/shard_map/ppermute | solution.py:41
  10.2 5.9 %collective-permute-start.7 = (f32[256,128]{1,0:T(8,128)S(1)}, f32[256,128]{1,0:T(8,128)S(1)}, u32[]{:S(2)}, u32[]{:S(2)}) collective-permute-start(f32[256,128]{1,0:T(8,128)S(1)} %add.11.own), channel_id=1, source_target_pairs={{0,2},{1,3},{2,0},{3,1},{4,5},{5,4},{6,7},{7,6},{8,10},{9,11},{10,... | collective-permute-start | bytes 393224 | tf_op jit(solution)/shard_map/ppermute | solution.py:41
  12.5 6.8 %collective-permute-start.1 = (bf16[2,26,2048]{2,1,0:T(8,128)(2,1)S(1)}, bf16[2,26,2048]{2,1,0:T(8,128)(2,1)S(1)}, u32[]{:S(2)}, u32[]{:S(2)}) collective-permute-start(bf16[2,26,2048]{2,1,0:T(8,128)(2,1)S(1)} %pad_maximum_fusion.2), channel_id=1, source_target_pairs={{0,16},{1,17},{2,18},{3,19},{4,12},{5,13},{6,14},{7,15},{8,24},{9,... | collective-permute-start | bytes 638984 | tf_op jit(solution)/shard_map/ppermute | solution.py:41
  17.0 4.0 %collective-permute-start.8 = (bf16[1,2,8192]{2,1,0:T(2,128)(2,1)S(1)}, bf16[1,2,8192]{2,1,0:T(2,128)(2,1)S(1)}, u32[]{:S(2)}, u32[]{:S(2)}) collective-permute-start(bf16[1,2,8192]{2,1,0:T(2,128)(2,1)S(1)} %reshape.6), channel_id=1, source_target_pairs={{0,8},{1,9},{2,10},{3,11},{4,20},{5,21},{6,22},{7,23},{8,0},{9,1},... | collective-permute-start | bytes 98312 | tf_op jit(solution)/shard_map/ppermute | solution.py:41
  19.4 3.7 %collective-permute-start.3 = (bf16[4,26,256]{2,1,0:T(8,128)(2,1)S(1)}, bf16[4,26,256]{2,1,0:T(8,128)(2,1)S(1)}, u32[]{:S(2)}, u32[]{:S(2)}) collective-permute-start(bf16[4,26,256]{2,1,0:T(8,128)(2,1)S(1)} %get-tuple-element.10), channel_id=1, source_target_pairs={{0,4},{1,5},{2,6},{3,7},{4,0},{5,1},{6,2},{7,3},{8,12},{9,13},{10,... | collective-permute-start | bytes 159752 | tf_op jit(solution)/shard_map/ppermute | solution.py:41
  21.1 13.2 %collective-permute-start.9 = (bf16[2,2,8192]{2,1,0:T(2,128)(2,1)S(1)}, bf16[2,2,8192]{2,1,0:T(2,128)(2,1)S(1)}, u32[]{:S(2)}, u32[]{:S(2)}) collective-permute-start(bf16[2,2,8192]{2,1,0:T(2,128)(2,1)S(1)} %pad_maximum_fusion.4), channel_id=1, source_target_pairs={{0,16},{1,17},{2,18},{3,19},{4,12},{5,13},{6,14},{7,15},{8,24},{9,... | collective-permute-start | bytes 196616 | tf_op jit(solution)/shard_map/ppermute | solution.py:41
  23.2 7.3 %collective-permute-start.4 = (bf16[1,8,26,256]{3,2,1,0:T(8,128)(2,1)S(1)}, bf16[1,8,26,256]{3,2,1,0:T(8,128)(2,1)S(1)}, u32[]{:S(2)}, u32[]{:S(2)}) collective-permute-start(bf16[1,8,26,256]{3,2,1,0:T(8,128)(2,1)S(1)} %maximum_bitcast_fusion), channel_id=1, source_target_pairs={{0,2},{1,3},{2,0},{3,1},{4,5},{5,4},{6,7},{7,6},{8,10},{9,11},{10,... | collective-permute-start | bytes 319496 | tf_op jit(solution)/shard_map/ppermute | solution.py:41
  25.1 14.0 %collective-permute-start.2 = (bf16[4,26,2048]{2,1,0:T(8,128)(2,1)S(1)}, bf16[4,26,2048]{2,1,0:T(8,128)(2,1)S(1)}, u32[]{:S(2)}, u32[]{:S(2)}) collective-permute-start(bf16[4,26,2048]{2,1,0:T(8,128)(2,1)S(1)} %pad_maximum_fusion.stored), channel_id=1, source_target_pairs={{0,4},{1,5},{2,6},{3,7},{4,0},{5,1},{6,2},{7,3},{8,12},{9,13},{10,... | collective-permute-start | bytes 1277960 | tf_op jit(solution)/shard_map/ppermute | solution.py:41
  30.5 8.4 %collective-permute-start.5 = (bf16[2,8,26,256]{3,2,1,0:T(8,128)(2,1)S(1)}, bf16[2,8,26,256]{3,2,1,0:T(8,128)(2,1)S(1)}, u32[]{:S(2)}, u32[]{:S(2)}) collective-permute-start(bf16[2,8,26,256]{3,2,1,0:T(8,128)(2,1)S(1)} %pad_maximum_fusion.3), channel_id=1, source_target_pairs={{0,1},{1,0},{2,3},{3,2},{4,6},{5,7},{6,4},{7,5},{8,9},{9,8},{10,11... | collective-permute-start | bytes 638984 | tf_op jit(solution)/shard_map/ppermute | solution.py:41
  34.3 4.7 %collective-permute-start.10 = (bf16[4,2,8192]{2,1,0:T(2,128)(2,1)S(1)}, bf16[4,2,8192]{2,1,0:T(2,128)(2,1)S(1)}, u32[]{:S(2)}, u32[]{:S(2)}) collective-permute-start(bf16[4,2,8192]{2,1,0:T(2,128)(2,1)S(1)} %constant_dynamic-update-slice_fusion.cur), channel_id=1, source_target_pairs={{0,4},{1,5},{2,6},{3,7},{4,0},{5,1},{6,2},{7,3},{8,12},{9,13},{10,... | collective-permute-start | bytes 393224 | tf_op jit(solution)/shard_map/ppermute | solution.py:41

commit v6 on v5

--- a/solution.py
+++ b/solution.py
@@ -95,17 +95,16 @@
     )(*args)
 
 
-def current_kernel(lengths, own, other, out):
+def current_kernel(live, own, other, out):
     examples, half, width = out.shape
     total = own[...] + other[...]
     rows = total.shape[0] // 2
     slots = rows // examples
-    position = lax.broadcasted_iota(jnp.int32, (slots, width), 0)
     lane = lax.broadcasted_iota(jnp.int32, (half, width), 1)
     for e in range(examples):
         left = total[rows + e * slots : rows + (e + 1) * slots]
         right = total[e * slots : (e + 1) * slots]
-        left = left * (position < lengths[e]).astype(jnp.float32)
+        left = left * live[e * slots : (e + 1) * slots, :]
         both = lax.dot_general(
             left,
             right,
@@ -119,16 +118,15 @@
 
 def current_rows(lengths, own, other, proj_width):
     examples = lengths.shape[0]
+    rows, width = own.shape[0] // 2, own.shape[1]
+    position = lax.broadcasted_iota(jnp.int32, (examples, rows // examples, width), 1)
+    live = (position < lengths[:, None, None]).astype(jnp.float32).reshape(rows, width)
     return pl.pallas_call(
         current_kernel,
         out_shape=jax.ShapeDtypeStruct(
             (examples, proj_width, LAYERS * proj_width), jnp.bfloat16
         ),
-        in_specs=[
-            pl.BlockSpec(memory_space=pltpu.SMEM),
-            pl.BlockSpec(memory_space=pltpu.VMEM),
-            pl.BlockSpec(memory_space=pltpu.VMEM),
-        ],
+        in_specs=[pl.BlockSpec(memory_space=pltpu.VMEM)] * 3,
         out_specs=pl.BlockSpec(memory_space=pltpu.VMEM),
         cost_estimate=pl.CostEstimate(
             flops=2 * examples * 64 * width_flops(proj_width),
@@ -137,21 +135,60 @@
         ),
         compiler_params=pltpu.CompilerParams(vmem_limit_bytes=4 * MIB),
         name="current",
-    )(lengths, own, other)
+    )(live, own, other)
 
 
 def width_flops(proj_width):
     return (LAYERS * proj_width) ** 2
 
 
-def gram_kernel(
-    scale, offsets, stored, near, cols, cur, moved, out, left, right, buf, sem
-):
+def fill(right, k, pair, cols, cur, moved, old):
+    pieces, sub = cols.shape[0], cols.shape[-1]
+    half, new = cur.shape[:2]
+    slot = right.shape[0] // pieces
+    q, i = lax.axis_index("tensor"), lax.axis_index("dp")
+    quarter = cur.shape[-1] // lax.axis_size("tensor")
+    block = q ^ jnp.where(i % 2 == 0, *pair)
+    source = pl.ds(pl.multiple_of(block * quarter + i * sub, sub), sub)
+    to = slice(k * sub, (k + 1) * sub)
+    for p in range(pieces):
+        base = p * slot
+        fresh = cur if p < half else moved
+        right[base : base + old, to] = cols[p]
+        right[base + old : base + old + new, to] = fresh[p % half, :, source]
+    return pl.ds(pl.multiple_of(block * sub, sub), sub)
+
+
+def multiply(scale, left, right, places, out, buf, sem):
+    chunk = buf.shape[2]
+    copies = []
+    for m in range(buf.shape[1]):
+        product = lax.dot_general(
+            left[:, m * chunk : (m + 1) * chunk],
+            right[...],
+            (((0,), (0,)), ((), ())),
+            preferred_element_type=jnp.float32,
+        )
+        product = (product * scale).astype(buf.dtype)
+        for k, place in enumerate(places):
+            sub = buf.shape[3]
+            buf[k, m] = product[:, k * sub : (k + 1) * sub]
+            copies.append(
+                pltpu.make_async_copy(
+                    buf.at[k, m], out.at[pl.ds(m * chunk, chunk), place], sem.at[k, m]
+                )
+            )
+            copies[-1].start()
+    for copy in copies:
+        copy.wait()
+
+
+def gram_kernel(scale, offsets, stored, near, cur, moved, *refs):
+    cols, (out, left, right, buf, sem) = refs[:-5], refs[-5:]
     half, old, quarter = stored.shape
     pieces, new = 2 * half, cur.shape[1]
-    sub = cols.shape[-1]
     slot = left.shape[0] // pieces
-    q, i = lax.axis_index("tensor"), lax.axis_index("dp")
+    q = lax.axis_index("tensor")
     place = pl.ds(pl.multiple_of(q * quarter, quarter), quarter)
     left[...] = jnp.zeros_like(left)
     right[...] = jnp.zeros_like(right)
@@ -160,65 +197,64 @@
         here, fresh = (stored, cur) if p < half else (near, moved)
         left[base : base + old, :] = here[p % half]
         left[base + old : base + old + new, :] = fresh[p % half, :, place]
-    for block in range(len(offsets)):
-        to = slice(block * sub, (block + 1) * sub)
-        source = pl.ds(pl.multiple_of(block * quarter + i * sub, sub), sub)
-        for p in range(pieces):
-            base = p * slot + old
-            fresh = cur if p < half else moved
-            right[base : base + new, to] = fresh[p % half, :, source]
-    for k, pair in enumerate(offsets):
-        block = q ^ jnp.where(i % 2 == 0, *pair)
-        to = pl.ds(pl.multiple_of(block * sub, sub), sub)
-        for p in range(pieces):
-            right[p * slot : p * slot + old, to] = cols[k, p]
-    chunk = buf.shape[1]
-    copies = []
-    for m in range(buf.shape[0]):
-        product = lax.dot_general(
-            left[:, m * chunk : (m + 1) * chunk],
-            right[...],
-            (((0,), (0,)), ((), ())),
-            preferred_element_type=jnp.float32,
-        )
-        buf[m] = (product * scale).astype(buf.dtype)
-        copies.append(
-            pltpu.make_async_copy(
-                buf.at[m], out.at[pl.ds(m * chunk, chunk)], sem.at[m]
-            )
-        )
-        copies[-1].start()
-    for copy in copies:
-        copy.wait()
+    places = [
+        fill(right, k, pair, cols[k], cur, moved, old) for k, pair in enumerate(offsets)
+    ]
+    multiply(scale, left, right, places, out, buf, sem)
+
+
+def last_kernel(scale, offset, left, cur, moved, cols, begun, out, right, buf, sem):
+    right[...] = jnp.zeros_like(right)
+    place = fill(right, 0, offset, cols, cur, moved, cols.shape[1])
+    multiply(scale, left, right, [place], out, buf, sem)
 
 
 def gram(stored, near, cols, cur, moved, offsets):
     half, old, quarter = stored.shape
-    pieces = 2 * half
-    new = cur.shape[1]
+    pieces, new, sub = 2 * half, cur.shape[1], cols[0].shape[-1]
     slot = -(-(old + new) // SLOT) * SLOT
-    width = cols.shape[0] * cols.shape[-1]
+    depth, count = pieces * slot, len(cols)
     chunk = 256 if quarter % 256 == 0 else quarter
     scale = 1.0 / math.sqrt(pieces * (old + new))
+    product = jax.ShapeDtypeStruct((quarter, count * sub), jnp.bfloat16)
+    vmem, hbm = pl.BlockSpec(memory_space=pltpu.VMEM), pl.BlockSpec(memory_space=pltpu.HBM)
+
+    def scratch(blocks):
+        return [
+            pltpu.VMEM((depth, blocks * sub), jnp.bfloat16),
+            pltpu.VMEM((blocks, quarter // chunk, chunk, sub), jnp.bfloat16),
+            pltpu.SemaphoreType.DMA((blocks, quarter // chunk)),
+        ]
+
+    def cost(blocks):
+        return pl.CostEstimate(
+            flops=2 * depth * quarter * blocks * sub,
+            bytes_accessed=2 * quarter * blocks * sub,
+            transcendentals=0,
+        )
+
+    params = pltpu.CompilerParams(vmem_limit_bytes=24 * MIB)
+    begun, left = pl.pallas_call(
+        functools.partial(gram_kernel, scale, offsets[:-1]),
+        out_shape=(product, jax.ShapeDtypeStruct((depth, quarter), jnp.bfloat16)),
+        in_specs=[vmem] * (3 + count),
+        out_specs=(hbm, vmem),
+        scratch_shapes=scratch(count - 1),
+        cost_estimate=cost(count - 1),
+        compiler_params=params,
+        name="gram",
+    )(stored, near, cur, moved, *cols[:-1])
     return pl.pallas_call(
-        functools.partial(gram_kernel, scale, offsets),
-        out_shape=jax.ShapeDtypeStruct((quarter, width), jnp.bfloat16),
-        in_specs=[pl.BlockSpec(memory_space=pltpu.VMEM)] * 5,
-        out_specs=pl.BlockSpec(memory_space=pltpu.HBM),
-        scratch_shapes=[
-            pltpu.VMEM((pieces * slot, quarter), jnp.bfloat16),
-            pltpu.VMEM((pieces * slot, width), jnp.bfloat16),
-            pltpu.VMEM((quarter // chunk, chunk, width), jnp.bfloat16),
-            pltpu.SemaphoreType.DMA((quarter // chunk,)),
-        ],
-        cost_estimate=pl.CostEstimate(
-            flops=2 * pieces * slot * quarter * width,
-            bytes_accessed=2 * quarter * width,
-            transcendentals=0,
-        ),
-        compiler_params=pltpu.CompilerParams(vmem_limit_bytes=24 * MIB),
-        name="gram",
-    )(stored, near, cols, cur, moved)
+        functools.partial(last_kernel, scale, offsets[-1]),
+        out_shape=product,
+        in_specs=[vmem] * 4 + [hbm],
+        out_specs=hbm,
+        scratch_shapes=scratch(1),
+        input_output_aliases={4: 0},
+        cost_estimate=cost(1),
+        compiler_params=params,
+        name="last",
+    )(left, cur, moved, cols[-1], begun)
 
 
 def local(
@@ -264,13 +300,14 @@
     give = lax.dynamic_slice_in_dim(rows, (i ^ 1) * sub_width, sub_width, 2)
     got = swap(give, "dp", 1, 1)
     cols = lax.dynamic_slice_in_dim(rows, i * sub_width, sub_width, 2)
-    cols = jnp.concatenate([cols, got], axis=0)[None]
+    cols = jnp.concatenate([cols, got], axis=0)
     near = swap(rows, "dp", 1, 1)
-    offsets = [(0, 0)]
-    for bits in reversed(tensor_rounds):
-        moved = swap(cols, "tensor", *bits)
-        cols = jnp.concatenate([cols, moved], axis=0)
-        offsets += [(even ^ bits[0], odd ^ bits[1]) for even, odd in offsets]
+    first, second = reversed(tensor_rounds)
+    beside = swap(cols, "tensor", *first)
+    beyond = swap(cols, "tensor", *second)
+    across = swap(beside, "tensor", *second)
+    offsets = [(0, 0), first, second, (first[0] ^ second[0], first[1] ^ second[1])]
+    cols = (cols, beside, beyond, across)
 
     for n, bits in enumerate(tensor_rounds):
         other = swap(total, "tensor", *bits)
@@ -338,7 +375,7 @@
 
 def paired(dp_count, tensor_count, proj_width, quarter):
     sizes = power_of_two(dp_count) and power_of_two(tensor_count)
-    many = dp_count > 1 and tensor_count > 1
+    many = dp_count > 1 and len(bits_of(tensor_count)) == 2
     lanes = quarter % (dp_count * LANES) == 0 and LAYERS * proj_width == LANES
     return sizes and many and lanes
 

time: 41.7 us -> 41.1 us (0.986); the launches traced: 41.6 us -> 40.5 us
  waiting for transfers between devices: 16.3 us -> 10.7 us
  starting transfers between devices: 18.3 us -> 21.6 us
  other arithmetic: 0.31 us -> 0.94 us
    ppermute x11 -> x12, waiting for transfers between devices: 16.3 us -> 10.7 us  [swap(): return lax.ppermute(value, ('dp', 'tensor'), pairs)]
    ppermute x11 -> x12, starting transfers between devices: 18.3 us -> 21.6 us  [swap(): return lax.ppermute(value, ('dp', 'tensor'), pairs)]
    pallas_call x1 -> x2, Pallas kernels: 2.56 us -> 3.51 us  [the longest x1 2.23 us: gram(): pl.pallas_call(functools.partial(gram_kernel, scale, offsets[:-1]), out_s...]
    convert_element_type x0 -> x1, other arithmetic: none -> 0.72 us  [current_rows(): (position < lengths[:, None, None]).astype(jnp.float32).reshape(rows, width)]
    pallas_call x1, Pallas kernels: 0.86 us -> 0.32 us  [current_rows(): pl.pallas_call(current_kernel, out_shape=jax.ShapeDtypeStruct((examples,...]
  transfers between devices with their start and end apart: 11 -> 12, of which waited for: 6 -> 6; matrix products, arithmetic and copies ran while one was open for 1% -> 3% of each run, Pallas kernels for 2% -> 14%
where the time goes in v6:
time: 41.1 us; the launch traced here: 40.5 us
  starting transfers between devices  21.6 us (53%)
  waiting for transfers between devices  10.7 us (26%)
  Pallas kernels  6.81 us (17%)
  other arithmetic  0.94 us (2%)
    ppermute x12, starting transfers between devices, swap(): return lax.ppermute(value, ('dp', 'tensor'), pairs)  21.6 us
    ppermute x12, waiting for transfers between devices, swap(): return lax.ppermute(value, ('dp', 'tensor'), pairs)  10.7 us
    pallas_call x1, Pallas kernels, project(): pl.pallas_call(project_kernel, out_shape=(jax.ShapeDtypeStruct((2 * rows,...  2.97 us
    pallas_call x1, Pallas kernels, gram(): pl.pallas_call(functools.partial(gram_kernel, scale, offsets[:-1]), out_s...  2.23 us
    pallas_call x1, Pallas kernels, gram(): pl.pallas_call(functools.partial(last_kernel, scale, offsets[-1]), out_sh...  1.28 us
  transfers between devices with their start and end apart: 12, of which 6 were waited for; matrix products, arithmetic and copies ran while one was open for 3% of the time, Pallas kernels for 14%

profile of v6, /device:TPU:0, one launch (start us, length us, event | category | flops | bytes accessed | tf_op | source)
XLA Modules:
  0.0 40.5 jit_solution(8972319063266455858)
XLA Ops:
  0.0 3.0 %collective-permute-start = (bf16[26,2048]{1,0:T(8,128)(2,1)}, bf16[26,2048]{1,0:T(8,128)(2,1)S(1)}, u32[]{:S(2)}, u32[]{:S(2)}) collective-permute-start(bf16[26,2048]{1,0:T(8,128)(2,1)} %stored.1), channel_id=1, source_target_pairs={{0,8},{1,9},{2,10},{3,11},{4,20},{5,21},{6,22},{7,23},{8,0},{9,1},... | collective-permute-start | bytes 319496 | tf_op jit(solution)/shard_map/ppermute | solution.py:41
  3.0 3.0 %project.1 = (f32[256,128]{1,0:T(8,128)S(1)}, bf16[26,2048]{1,0:T(8,128)(2,1)S(1)}) custom-call(bf16[128,1024]{1,0:T(8,128)(2,1)} %x.1, bf16[128,3584]{1,0:T(8,128)(2,1)} %h.1, bf16[128,3584]{1,0:T(8,128)(2,1)} %gu.1, bf16[128,1024]{1,0:T(8,128)(2,1)} %gd.1, bf16[64,1024]{1,0:T(8,128)(2,1)} %bitcast.13, bf16[64,3584]{1,0:T(8,128)(2,1)} %bitcast.11, ...), custom_call_target="tpu_custom_call" | custom-call | flops 150994944 | bytes 3645440 | tf_op jit(solution)/shard_map/project/pallas_call | solution.py:78
  5.9 1.6 %collective-permute-start.3 = (f32[256,128]{1,0:T(8,128)S(1)}, f32[256,128]{1,0:T(8,128)S(1)}, u32[]{:S(2)}, u32[]{:S(2)}) collective-permute-start(f32[256,128]{1,0:T(8,128)S(1)} %get-tuple-element.10), channel_id=1, source_target_pairs={{0,1},{1,0},{2,3},{3,2},{4,6},{5,7},{6,4},{7,5},{8,9},{9,8},{10,11... | collective-permute-start | bytes 393224 | tf_op jit(solution)/shard_map/ppermute | solution.py:41
  7.6 0.7 %compare_convert_fusion = f32[2,64]{1,0:T(2,128)S(1)} fusion(s32[2]{0:T(128)} %param.18), kind=kLoop, calls=%fused_computation.7 | loop fusion | flops 256 | bytes 520 | tf_op jit(solution)/shard_map/convert_element_type | solution.py:123
  8.3 0.1 reshape.15
  8.4 3.2 %collective-permute-done.3 = f32[256,128]{1,0:T(8,128)S(1)} collective-permute-done((f32[256,128]{1,0:T(8,128)S(1)}, f32[256,128]{1,0:T(8,128)S(1)}, u32[]{:S(2)}, u32[]{:S(2)}) %collective-permute-start.3) | collective-permute-done | bytes 131104 | tf_op jit(solution)/shard_map/ppermute | solution.py:41
  11.6 2.4 %collective-permute-start.4 = (f32[256,128]{1,0:T(8,128)S(1)}, f32[256,128]{1,0:T(8,128)S(1)}, u32[]{:S(2)}, u32[]{:S(2)}) collective-permute-start(f32[256,128]{1,0:T(8,128)S(1)} %add.9.own), channel_id=1, source_target_pairs={{0,2},{1,3},{2,0},{3,1},{4,5},{5,4},{6,7},{7,6},{8,10},{9,11},{10,... | collective-permute-start | bytes 393224 | tf_op jit(solution)/shard_map/ppermute | solution.py:41
  14.1 0.0 collective-permute-done
  14.1 1.5 %collective-permute-start.1 = (bf16[2,26,2048]{2,1,0:T(8,128)(2,1)S(1)}, bf16[2,26,2048]{2,1,0:T(8,128)(2,1)S(1)}, u32[]{:S(2)}, u32[]{:S(2)}) collective-permute-start(bf16[2,26,2048]{2,1,0:T(8,128)(2,1)S(1)} %pad_maximum_fusion.1), channel_id=1, source_target_pairs={{0,16},{1,17},{2,18},{3,19},{4,12},{5,13},{6,14},{7,15},{8,24},{9,... | collective-permute-start | bytes 638984 | tf_op jit(solution)/shard_map/ppermute | solution.py:41
  15.6 2.0 %collective-permute-done.4.other = f32[256,128]{1,0:T(8,128)S(1)} collective-permute-done((f32[256,128]{1,0:T(8,128)S(1)}, f32[256,128]{1,0:T(8,128)S(1)}, u32[]{:S(2)}, u32[]{:S(2)}) %collective-permute-start.4) | collective-permute-done | bytes 131104 | tf_op jit(solution)/shard_map/ppermute | solution.py:41
  17.6 0.1 iota.10.live
  17.6 0.3 current.1
  18.0 0.9 %collective-permute-start.5 = (bf16[1,2,8192]{2,1,0:T(2,128)(2,1)S(1)}, bf16[1,2,8192]{2,1,0:T(2,128)(2,1)S(1)}, u32[]{:S(2)}, u32[]{:S(2)}) collective-permute-start(bf16[1,2,8192]{2,1,0:T(2,128)(2,1)S(1)} %reshape.13), channel_id=1, source_target_pairs={{0,8},{1,9},{2,10},{3,11},{4,20},{5,21},{6,22},{7,23},{8,0},{9,1},... | collective-permute-start | bytes 98312 | tf_op jit(solution)/shard_map/ppermute | solution.py:41
  18.9 3.1 %collective-permute-done.5 = bf16[1,2,8192]{2,1,0:T(2,128)(2,1)S(1)} collective-permute-done((bf16[1,2,8192]{2,1,0:T(2,128)(2,1)S(1)}, bf16[1,2,8192]{2,1,0:T(2,128)(2,1)S(1)}, u32[]{:S(2)}, u32[]{:S(2)}) %collective-permute-start.5) | collective-permute-done | bytes 32800 | tf_op jit(solution)/shard_map/ppermute | solution.py:41
  22.0 0.1 pad_maximum_fusion.3
  22.1 1.2 %collective-permute-start.6 = (bf16[2,2,8192]{2,1,0:T(2,128)(2,1)S(1)}, bf16[2,2,8192]{2,1,0:T(2,128)(2,1)S(1)}, u32[]{:S(2)}, u32[]{:S(2)}) collective-permute-start(bf16[2,2,8192]{2,1,0:T(2,128)(2,1)S(1)} %pad_maximum_fusion.3), channel_id=1, source_target_pairs={{0,16},{1,17},{2,18},{3,19},{4,12},{5,13},{6,14},{7,15},{8,24},{9,... | collective-permute-start | bytes 196616 | tf_op jit(solution)/shard_map/ppermute | solution.py:41
  23.3 0.0 collective-permute-done.1
  23.3 0.1 pad_maximum_fusion.stored
  23.4 0.1 collective-permute-start.8
  23.5 0.6 %collective-permute-start.2 = (bf16[4,26,2048]{2,1,0:T(8,128)(2,1)S(1)}, bf16[4,26,2048]{2,1,0:T(8,128)(2,1)S(1)}, u32[]{:S(2)}, u32[]{:S(2)}) collective-permute-start(bf16[4,26,2048]{2,1,0:T(8,128)(2,1)S(1)} %pad_maximum_fusion.stored), channel_id=1, source_target_pairs={{0,4},{1,5},{2,6},{3,7},{4,0},{5,1},{6,2},{7,3},{8,12},{9,13},{10,... | collective-permute-start | bytes 1277960 | tf_op jit(solution)/shard_map/ppermute | solution.py:41
  24.0 0.6 %collective-permute-done.8 = bf16[4,26,256]{2,1,0:T(8,128)(2,1)S(1)} collective-permute-done((bf16[4,26,256]{2,1,0:T(8,128)(2,1)S(1)}, bf16[4,26,256]{2,1,0:T(8,128)(2,1)S(1)}, u32[]{:S(2)}, u32[]{:S(2)}) %collective-permute-start.8) | collective-permute-done | bytes 53280 | tf_op jit(solution)/shard_map/ppermute | solution.py:41
  24.7 3.0 %collective-permute-start.9 = (bf16[8,26,256]{2,1,0:T(8,128)(2,1)S(1)}, bf16[8,26,256]{2,1,0:T(8,128)(2,1)S(1)}, u32[]{:S(2)}, u32[]{:S(2)}) collective-permute-start(bf16[8,26,256]{2,1,0:T(8,128)(2,1)S(1)} %pad_maximum_fusion.2.refs_0_), channel_id=1, source_target_pairs={{0,2},{1,3},{2,0},{3,1},{4,5},{5,4},{6,7},{7,6},{8,10},{9,11},{10,... | collective-permute-start | bytes 319496 | tf_op jit(solution)/shard_map/ppermute | solution.py:41
  27.7 0.0 collective-permute-done.6
  27.7 0.1 constant_dynamic-update-slice_fusion.cur
  27.7 0.1 collective-permute-start.7
  27.8 2.7 %collective-permute-start.10 = (bf16[8,26,256]{2,1,0:T(8,128)(2,1)S(1)}, bf16[8,26,256]{2,1,0:T(8,128)(2,1)S(1)}, u32[]{:S(2)}, u32[]{:S(2)}) collective-permute-start(bf16[8,26,256]{2,1,0:T(8,128)(2,1)S(1)} %pad_maximum_fusion.2.refs_0_), channel_id=1, source_target_pairs={{0,1},{1,0},{2,3},{3,2},{4,6},{5,7},{6,4},{7,5},{8,9},{9,8},{10,11... | collective-permute-start | bytes 319496 | tf_op jit(solution)/shard_map/ppermute | solution.py:41
  30.5 0.3 collective-permute-done.9.refs_1_
  30.7 4.7 %collective-permute-start.11 = (bf16[8,26,256]{2,1,0:T(8,128)(2,1)S(1)}, bf16[8,26,256]{2,1,0:T(8,128)(2,1)S(1)}, u32[]{:S(2)}, u32[]{:S(2)}) collective-permute-start(bf16[8,26,256]{2,1,0:T(8,128)(2,1)S(1)} %collective-permute-done.9.refs_1_), channel_id=1, source_target_pairs={{0,1},{1,0},{2,3},{3,2},{4,6},{5,7},{6,4},{7,5},{8,9},{9,8},{10,11... | collective-permute-start | bytes 319496 | tf_op jit(solution)/shard_map/ppermute | solution.py:41
  35.4 0.0 collective-permute-done.10.refs_2_
  35.4 0.0 collective-permute-done.7.moved
  35.5 0.0 collective-permute-done.2.near
  35.5 2.2 %gram.1 = (bf16[2048,1024]{1,0:T(8,128)(2,1)}, bf16[256,2048]{1,0:T(8,128)(2,1)S(1)}) custom-call(bf16[4,26,2048]{2,1,0:T(8,128)(2,1)S(1)} %pad_maximum_fusion.stored, bf16[4,26,2048]{2,1,0:T(8,128)(2,1)S(1)} %collective-permute-done.2.near, bf16[4,2,8192]{2,1,0:T(2,128)(2,1)S(1)} %constant_dynamic-update-slice_fusion.cur, ...), custom_call_target="tpu_custom_call" | custom-call | flops 805306368 | bytes 3145728 | tf_op jit(solution)/shard_map/gram/pallas_call | solution.py:237
  37.7 1.5 %collective-permute-done.11.cols = bf16[8,26,256]{2,1,0:T(8,128)(2,1)S(1)} collective-permute-done((bf16[8,26,256]{2,1,0:T(8,128)(2,1)S(1)}, bf16[8,26,256]{2,1,0:T(8,128)(2,1)S(1)}, u32[]{:S(2)}, u32[]{:S(2)}) %collective-permute-start.11) | collective-permute-done | bytes 106528 | tf_op jit(solution)/shard_map/ppermute | solution.py:41
  39.2 1.3 %last.1 = bf16[2048,1024]{1,0:T(8,128)(2,1)} custom-call(bf16[256,2048]{1,0:T(8,128)(2,1)S(1)} %get-tuple-element.11.left, bf16[4,2,8192]{2,1,0:T(2,128)(2,1)S(1)} %constant_dynamic-update-slice_fusion.cur, bf16[4,2,8192]{2,1,0:T(2,128)(2,1)S(1)} %collective-permute-done.7.moved, ...), custom_call_target="tpu_custom_call", output_to_operand_aliasing={{}: (4, {})} | custom-call | flops 268435456 | bytes 1048576 | tf_op jit(solution)/shard_map/last/pallas_call | solution.py:247
  (7 shorter events, 0.2 us)
Async XLA Ops:
  0.0 14.1 %collective-permute-start = (bf16[26,2048]{1,0:T(8,128)(2,1)}, bf16[26,2048]{1,0:T(8,128)(2,1)S(1)}, u32[]{:S(2)}, u32[]{:S(2)}) collective-permute-start(bf16[26,2048]{1,0:T(8,128)(2,1)} %stored.1), channel_id=1, source_target_pairs={{0,8},{1,9},{2,10},{3,11},{4,20},{5,21},{6,22},{7,23},{8,0},{9,1},... | collective-permute-start | bytes 319496 | tf_op jit(solution)/shard_map/ppermute | solution.py:41
  5.9 5.7 %collective-permute-start.3 = (f32[256,128]{1,0:T(8,128)S(1)}, f32[256,128]{1,0:T(8,128)S(1)}, u32[]{:S(2)}, u32[]{:S(2)}) collective-permute-start(f32[256,128]{1,0:T(8,128)S(1)} %get-tuple-element.10), channel_id=1, source_target_pairs={{0,1},{1,0},{2,3},{3,2},{4,6},{5,7},{6,4},{7,5},{8,9},{9,8},{10,11... | collective-permute-start | bytes 393224 | tf_op jit(solution)/shard_map/ppermute | solution.py:41
  11.6 5.9 %collective-permute-start.4 = (f32[256,128]{1,0:T(8,128)S(1)}, f32[256,128]{1,0:T(8,128)S(1)}, u32[]{:S(2)}, u32[]{:S(2)}) collective-permute-start(f32[256,128]{1,0:T(8,128)S(1)} %add.9.own), channel_id=1, source_target_pairs={{0,2},{1,3},{2,0},{3,1},{4,5},{5,4},{6,7},{7,6},{8,10},{9,11},{10,... | collective-permute-start | bytes 393224 | tf_op jit(solution)/shard_map/ppermute | solution.py:41
  14.1 9.1 %collective-permute-start.1 = (bf16[2,26,2048]{2,1,0:T(8,128)(2,1)S(1)}, bf16[2,26,2048]{2,1,0:T(8,128)(2,1)S(1)}, u32[]{:S(2)}, u32[]{:S(2)}) collective-permute-start(bf16[2,26,2048]{2,1,0:T(8,128)(2,1)S(1)} %pad_maximum_fusion.1), channel_id=1, source_target_pairs={{0,16},{1,17},{2,18},{3,19},{4,12},{5,13},{6,14},{7,15},{8,24},{9,... | collective-permute-start | bytes 638984 | tf_op jit(solution)/shard_map/ppermute | solution.py:41
  18.0 4.0 %collective-permute-start.5 = (bf16[1,2,8192]{2,1,0:T(2,128)(2,1)S(1)}, bf16[1,2,8192]{2,1,0:T(2,128)(2,1)S(1)}, u32[]{:S(2)}, u32[]{:S(2)}) collective-permute-start(bf16[1,2,8192]{2,1,0:T(2,128)(2,1)S(1)} %reshape.13), channel_id=1, source_target_pairs={{0,8},{1,9},{2,10},{3,11},{4,20},{5,21},{6,22},{7,23},{8,0},{9,1},... | collective-permute-start | bytes 98312 | tf_op jit(solution)/shard_map/ppermute | solution.py:41
  22.1 5.6 %collective-permute-start.6 = (bf16[2,2,8192]{2,1,0:T(2,128)(2,1)S(1)}, bf16[2,2,8192]{2,1,0:T(2,128)(2,1)S(1)}, u32[]{:S(2)}, u32[]{:S(2)}) collective-permute-start(bf16[2,2,8192]{2,1,0:T(2,128)(2,1)S(1)} %pad_maximum_fusion.3), channel_id=1, source_target_pairs={{0,16},{1,17},{2,18},{3,19},{4,12},{5,13},{6,14},{7,15},{8,24},{9,... | collective-permute-start | bytes 196616 | tf_op jit(solution)/shard_map/ppermute | solution.py:41
  23.4 1.3 %collective-permute-start.8 = (bf16[4,26,256]{2,1,0:T(8,128)(2,1)S(1)}, bf16[4,26,256]{2,1,0:T(8,128)(2,1)S(1)}, u32[]{:S(2)}, u32[]{:S(2)}) collective-permute-start(bf16[4,26,256]{2,1,0:T(8,128)(2,1)S(1)} %get-tuple-element.14), channel_id=1, source_target_pairs={{0,4},{1,5},{2,6},{3,7},{4,0},{5,1},{6,2},{7,3},{8,12},{9,13},{10,... | collective-permute-start | bytes 159752 | tf_op jit(solution)/shard_map/ppermute | solution.py:41
  23.5 12.0 %collective-permute-start.2 = (bf16[4,26,2048]{2,1,0:T(8,128)(2,1)S(1)}, bf16[4,26,2048]{2,1,0:T(8,128)(2,1)S(1)}, u32[]{:S(2)}, u32[]{:S(2)}) collective-permute-start(bf16[4,26,2048]{2,1,0:T(8,128)(2,1)S(1)} %pad_maximum_fusion.stored), channel_id=1, source_target_pairs={{0,4},{1,5},{2,6},{3,7},{4,0},{5,1},{6,2},{7,3},{8,12},{9,13},{10,... | collective-permute-start | bytes 1277960 | tf_op jit(solution)/shard_map/ppermute | solution.py:41
  24.7 6.0 %collective-permute-start.9 = (bf16[8,26,256]{2,1,0:T(8,128)(2,1)S(1)}, bf16[8,26,256]{2,1,0:T(8,128)(2,1)S(1)}, u32[]{:S(2)}, u32[]{:S(2)}) collective-permute-start(bf16[8,26,256]{2,1,0:T(8,128)(2,1)S(1)} %pad_maximum_fusion.2.refs_0_), channel_id=1, source_target_pairs={{0,2},{1,3},{2,0},{3,1},{4,5},{5,4},{6,7},{7,6},{8,10},{9,11},{10,... | collective-permute-start | bytes 319496 | tf_op jit(solution)/shard_map/ppermute | solution.py:41
  27.7 7.7 %collective-permute-start.7 = (bf16[4,2,8192]{2,1,0:T(2,128)(2,1)S(1)}, bf16[4,2,8192]{2,1,0:T(2,128)(2,1)S(1)}, u32[]{:S(2)}, u32[]{:S(2)}) collective-permute-start(bf16[4,2,8192]{2,1,0:T(2,128)(2,1)S(1)} %constant_dynamic-update-slice_fusion.cur), channel_id=1, source_target_pairs={{0,4},{1,5},{2,6},{3,7},{4,0},{5,1},{6,2},{7,3},{8,12},{9,13},{10,... | collective-permute-start | bytes 393224 | tf_op jit(solution)/shard_map/ppermute | solution.py:41
  27.8 7.6 %collective-permute-start.10 = (bf16[8,26,256]{2,1,0:T(8,128)(2,1)S(1)}, bf16[8,26,256]{2,1,0:T(8,128)(2,1)S(1)}, u32[]{:S(2)}, u32[]{:S(2)}) collective-permute-start(bf16[8,26,256]{2,1,0:T(8,128)(2,1)S(1)} %pad_maximum_fusion.2.refs_0_), channel_id=1, source_target_pairs={{0,1},{1,0},{2,3},{3,2},{4,6},{5,7},{6,4},{7,5},{8,9},{9,8},{10,11... | collective-permute-start | bytes 319496 | tf_op jit(solution)/shard_map/ppermute | solution.py:41
  30.7 8.5 %collective-permute-start.11 = (bf16[8,26,256]{2,1,0:T(8,128)(2,1)S(1)}, bf16[8,26,256]{2,1,0:T(8,128)(2,1)S(1)}, u32[]{:S(2)}, u32[]{:S(2)}) collective-permute-start(bf16[8,26,256]{2,1,0:T(8,128)(2,1)S(1)} %collective-permute-done.9.refs_1_), channel_id=1, source_target_pairs={{0,1},{1,0},{2,3},{3,2},{4,6},{5,7},{6,4},{7,5},{8,9},{9,8},{10,11... | collective-permute-start | bytes 319496 | tf_op jit(solution)/shard_map/ppermute | solution.py:41

commit v7 on v6

--- a/solution.py
+++ b/solution.py
@@ -142,6 +142,12 @@
     return (LAYERS * proj_width) ** 2
 
 
+def place_of(pair, sub):
+    q, i = lax.axis_index("tensor"), lax.axis_index("dp")
+    block = q ^ jnp.where(i % 2 == 0, *pair)
+    return pl.ds(pl.multiple_of(block * sub, sub), sub)
+
+
 def fill(right, k, pair, cols, cur, moved, old):
     pieces, sub = cols.shape[0], cols.shape[-1]
     half, new = cur.shape[:2]
@@ -159,32 +165,25 @@
     return pl.ds(pl.multiple_of(block * sub, sub), sub)
 
 
-def multiply(scale, left, right, places, out, buf, sem):
-    chunk = buf.shape[2]
-    copies = []
-    for m in range(buf.shape[1]):
-        product = lax.dot_general(
-            left[:, m * chunk : (m + 1) * chunk],
-            right[...],
-            (((0,), (0,)), ((), ())),
-            preferred_element_type=jnp.float32,
-        )
-        product = (product * scale).astype(buf.dtype)
-        for k, place in enumerate(places):
-            sub = buf.shape[3]
-            buf[k, m] = product[:, k * sub : (k + 1) * sub]
-            copies.append(
-                pltpu.make_async_copy(
-                    buf.at[k, m], out.at[pl.ds(m * chunk, chunk), place], sem.at[k, m]
-                )
-            )
-            copies[-1].start()
-    for copy in copies:
-        copy.wait()
+def multiply(scale, left, right, m, chunk, dtype):
+    product = lax.dot_general(
+        left[:, m * chunk : (m + 1) * chunk],
+        right,
+        (((0,), (0,)), ((), ())),
+        preferred_element_type=jnp.float32,
+    )
+    return (product * scale).astype(dtype)
+
+
+def send(source, out, m, place, sem):
+    chunk = source.shape[0]
+    copy = pltpu.make_async_copy(source, out.at[pl.ds(m * chunk, chunk), place], sem)
+    copy.start()
+    return copy
 
 
 def gram_kernel(scale, offsets, stored, near, cur, moved, *refs):
-    cols, (out, left, right, buf, sem) = refs[:-5], refs[-5:]
+    cols, (out, left, held, right, buf, sem) = refs[:-6], refs[-6:]
     half, old, quarter = stored.shape
     pieces, new = 2 * half, cur.shape[1]
     slot = left.shape[0] // pieces
@@ -200,13 +199,33 @@
     places = [
         fill(right, k, pair, cols[k], cur, moved, old) for k, pair in enumerate(offsets)
     ]
-    multiply(scale, left, right, places, out, buf, sem)
-
-
-def last_kernel(scale, offset, left, cur, moved, cols, begun, out, right, buf, sem):
+    count, steps, chunk, sub = buf.shape
+    wide = count * sub
+    copies = []
+    for m in range(steps):
+        product = multiply(scale, left, right[:, :wide], m, chunk, buf.dtype)
+        for k in range(count):
+            buf[k, m] = product[:, k * sub : (k + 1) * sub]
+            copies.append(send(buf.at[k, m], out, m, places[k], sem.at[k, m]))
+    for m in range(steps):
+        held[m] = multiply(scale, left, right[:, wide:], m, chunk, held.dtype)
+    for copy in copies:
+        copy.wait()
+
+
+def last_kernel(
+    scale, offsets, left, held, cur, moved, cols, begun, out, right, buf, sem
+):
+    _, steps, chunk, sub = buf.shape
+    place = place_of(offsets[0], sub)
+    copies = [send(held.at[m], out, m, place, sem.at[0, m]) for m in range(steps)]
     right[...] = jnp.zeros_like(right)
-    place = fill(right, 0, offset, cols, cur, moved, cols.shape[1])
-    multiply(scale, left, right, [place], out, buf, sem)
+    place = fill(right, 0, offsets[1], cols, cur, moved, cols.shape[1])
+    for m in range(steps):
+        buf[0, m] = multiply(scale, left, right[...], m, chunk, buf.dtype)
+        copies.append(send(buf.at[0, m], out, m, place, sem.at[1, m]))
+    for copy in copies:
+        copy.wait()
 
 
 def gram(stored, near, cols, cur, moved, offsets):
@@ -219,11 +238,13 @@
     product = jax.ShapeDtypeStruct((quarter, count * sub), jnp.bfloat16)
     vmem, hbm = pl.BlockSpec(memory_space=pltpu.VMEM), pl.BlockSpec(memory_space=pltpu.HBM)
 
-    def scratch(blocks):
+    steps = quarter // chunk
+
+    def scratch(blocks, kept, copies):
         return [
             pltpu.VMEM((depth, blocks * sub), jnp.bfloat16),
-            pltpu.VMEM((blocks, quarter // chunk, chunk, sub), jnp.bfloat16),
-            pltpu.SemaphoreType.DMA((blocks, quarter // chunk)),
+            pltpu.VMEM((kept, steps, chunk, sub), jnp.bfloat16),
+            pltpu.SemaphoreType.DMA((copies, steps)),
         ]
 
     def cost(blocks):
@@ -234,27 +255,31 @@
         )
 
     params = pltpu.CompilerParams(vmem_limit_bytes=24 * MIB)
-    begun, left = pl.pallas_call(
+    begun, left, held = pl.pallas_call(
         functools.partial(gram_kernel, scale, offsets[:-1]),
-        out_shape=(product, jax.ShapeDtypeStruct((depth, quarter), jnp.bfloat16)),
+        out_shape=(
+            product,
+            jax.ShapeDtypeStruct((depth, quarter), jnp.bfloat16),
+            jax.ShapeDtypeStruct((steps, chunk, sub), jnp.bfloat16),
+        ),
         in_specs=[vmem] * (3 + count),
-        out_specs=(hbm, vmem),
-        scratch_shapes=scratch(count - 1),
+        out_specs=(hbm, vmem, vmem),
+        scratch_shapes=scratch(count - 1, count - 2, count - 2),
         cost_estimate=cost(count - 1),
         compiler_params=params,
         name="gram",
     )(stored, near, cur, moved, *cols[:-1])
     return pl.pallas_call(
-        functools.partial(last_kernel, scale, offsets[-1]),
+        functools.partial(last_kernel, scale, offsets[-2:]),
         out_shape=product,
-        in_specs=[vmem] * 4 + [hbm],
+        in_specs=[vmem] * 5 + [hbm],
         out_specs=hbm,
-        scratch_shapes=scratch(1),
-        input_output_aliases={4: 0},
+        scratch_shapes=scratch(1, 1, 2),
+        input_output_aliases={5: 0},
         cost_estimate=cost(1),
         compiler_params=params,
         name="last",
-    )(left, cur, moved, cols[-1], begun)
+    )(left, held, cur, moved, cols[-1], begun)
 
 
 def local(

time: 41.1 us -> 41.3 us (level)
  transfers between devices with their start and end apart: 12 -> 12, of which waited for: 6 -> 6; matrix products, arithmetic and copies ran while one was open for 3% -> 3% of each run, Pallas kernels for 14% -> 13%
where the time goes in v7:
time: 41.3 us; the launch traced here: 40.7 us
  starting transfers between devices  21.6 us (52%)
  waiting for transfers between devices  11.1 us (27%)
  Pallas kernels  6.62 us (16%)
  other arithmetic  0.94 us (2%)
    ppermute x12, starting transfers between devices, swap(): return lax.ppermute(value, ('dp', 'tensor'), pairs)  21.6 us
    ppermute x12, waiting for transfers between devices, swap(): return lax.ppermute(value, ('dp', 'tensor'), pairs)  11.1 us
    pallas_call x1, Pallas kernels, project(): pl.pallas_call(project_kernel, out_shape=(jax.ShapeDtypeStruct((2 * rows,...  2.97 us
    pallas_call x1, Pallas kernels, gram(): pl.pallas_call(functools.partial(gram_kernel, scale, offsets[:-1]), out_s...  1.85 us
    pallas_call x1, Pallas kernels, gram(): pl.pallas_call(functools.partial(last_kernel, scale, offsets[-2:]), out_s...  1.47 us
  transfers between devices with their start and end apart: 12, of which 6 were waited for; matrix products, arithmetic and copies ran while one was open for 3% of the time, Pallas kernels for 13%

profile of v7, /device:TPU:0, one launch (start us, length us, event | category | flops | bytes accessed | tf_op | source)
XLA Modules:
  0.0 40.7 jit_solution(9650923759148385636)
XLA Ops:
  0.0 3.0 %collective-permute-start = (bf16[26,2048]{1,0:T(8,128)(2,1)}, bf16[26,2048]{1,0:T(8,128)(2,1)S(1)}, u32[]{:S(2)}, u32[]{:S(2)}) collective-permute-start(bf16[26,2048]{1,0:T(8,128)(2,1)} %stored.1), channel_id=1, source_target_pairs={{0,8},{1,9},{2,10},{3,11},{4,20},{5,21},{6,22},{7,23},{8,0},{9,1},... | collective-permute-start | bytes 319496 | tf_op jit(solution)/shard_map/ppermute | solution.py:41
  3.0 3.0 %project.1 = (f32[256,128]{1,0:T(8,128)S(1)}, bf16[26,2048]{1,0:T(8,128)(2,1)S(1)}) custom-call(bf16[128,1024]{1,0:T(8,128)(2,1)} %x.1, bf16[128,3584]{1,0:T(8,128)(2,1)} %h.1, bf16[128,3584]{1,0:T(8,128)(2,1)} %gu.1, bf16[128,1024]{1,0:T(8,128)(2,1)} %gd.1, bf16[64,1024]{1,0:T(8,128)(2,1)} %bitcast.13, bf16[64,3584]{1,0:T(8,128)(2,1)} %bitcast.11, ...), custom_call_target="tpu_custom_call" | custom-call | flops 150994944 | bytes 3645440 | tf_op jit(solution)/shard_map/project/pallas_call | solution.py:78
  5.9 1.6 %collective-permute-start.3 = (f32[256,128]{1,0:T(8,128)S(1)}, f32[256,128]{1,0:T(8,128)S(1)}, u32[]{:S(2)}, u32[]{:S(2)}) collective-permute-start(f32[256,128]{1,0:T(8,128)S(1)} %get-tuple-element.11), channel_id=1, source_target_pairs={{0,1},{1,0},{2,3},{3,2},{4,6},{5,7},{6,4},{7,5},{8,9},{9,8},{10,11... | collective-permute-start | bytes 393224 | tf_op jit(solution)/shard_map/ppermute | solution.py:41
  7.6 0.7 %compare_convert_fusion = f32[2,64]{1,0:T(2,128)S(1)} fusion(s32[2]{0:T(128)} %param.18), kind=kLoop, calls=%fused_computation.7 | loop fusion | flops 256 | bytes 520 | tf_op jit(solution)/shard_map/convert_element_type | solution.py:123
  8.3 0.1 reshape.15
  8.4 3.2 %collective-permute-done.3 = f32[256,128]{1,0:T(8,128)S(1)} collective-permute-done((f32[256,128]{1,0:T(8,128)S(1)}, f32[256,128]{1,0:T(8,128)S(1)}, u32[]{:S(2)}, u32[]{:S(2)}) %collective-permute-start.3) | collective-permute-done | bytes 131104 | tf_op jit(solution)/shard_map/ppermute | solution.py:41
  11.6 2.4 %collective-permute-start.4 = (f32[256,128]{1,0:T(8,128)S(1)}, f32[256,128]{1,0:T(8,128)S(1)}, u32[]{:S(2)}, u32[]{:S(2)}) collective-permute-start(f32[256,128]{1,0:T(8,128)S(1)} %add.9.own), channel_id=1, source_target_pairs={{0,2},{1,3},{2,0},{3,1},{4,5},{5,4},{6,7},{7,6},{8,10},{9,11},{10,... | collective-permute-start | bytes 393224 | tf_op jit(solution)/shard_map/ppermute | solution.py:41
  14.1 0.0 collective-permute-done
  14.1 1.5 %collective-permute-start.1 = (bf16[2,26,2048]{2,1,0:T(8,128)(2,1)S(1)}, bf16[2,26,2048]{2,1,0:T(8,128)(2,1)S(1)}, u32[]{:S(2)}, u32[]{:S(2)}) collective-permute-start(bf16[2,26,2048]{2,1,0:T(8,128)(2,1)S(1)} %pad_maximum_fusion.1), channel_id=1, source_target_pairs={{0,16},{1,17},{2,18},{3,19},{4,12},{5,13},{6,14},{7,15},{8,24},{9,... | collective-permute-start | bytes 638984 | tf_op jit(solution)/shard_map/ppermute | solution.py:41
  15.6 2.0 %collective-permute-done.4.other = f32[256,128]{1,0:T(8,128)S(1)} collective-permute-done((f32[256,128]{1,0:T(8,128)S(1)}, f32[256,128]{1,0:T(8,128)S(1)}, u32[]{:S(2)}, u32[]{:S(2)}) %collective-permute-start.4) | collective-permute-done | bytes 131104 | tf_op jit(solution)/shard_map/ppermute | solution.py:41
  17.6 0.1 iota.10.live
  17.6 0.3 current.1
  18.0 0.9 %collective-permute-start.5 = (bf16[1,2,8192]{2,1,0:T(2,128)(2,1)S(1)}, bf16[1,2,8192]{2,1,0:T(2,128)(2,1)S(1)}, u32[]{:S(2)}, u32[]{:S(2)}) collective-permute-start(bf16[1,2,8192]{2,1,0:T(2,128)(2,1)S(1)} %reshape.13), channel_id=1, source_target_pairs={{0,8},{1,9},{2,10},{3,11},{4,20},{5,21},{6,22},{7,23},{8,0},{9,1},... | collective-permute-start | bytes 98312 | tf_op jit(solution)/shard_map/ppermute | solution.py:41
  18.9 3.1 %collective-permute-done.5 = bf16[1,2,8192]{2,1,0:T(2,128)(2,1)S(1)} collective-permute-done((bf16[1,2,8192]{2,1,0:T(2,128)(2,1)S(1)}, bf16[1,2,8192]{2,1,0:T(2,128)(2,1)S(1)}, u32[]{:S(2)}, u32[]{:S(2)}) %collective-permute-start.5) | collective-permute-done | bytes 32800 | tf_op jit(solution)/shard_map/ppermute | solution.py:41
  22.0 0.1 pad_maximum_fusion.3
  22.1 1.2 %collective-permute-start.6 = (bf16[2,2,8192]{2,1,0:T(2,128)(2,1)S(1)}, bf16[2,2,8192]{2,1,0:T(2,128)(2,1)S(1)}, u32[]{:S(2)}, u32[]{:S(2)}) collective-permute-start(bf16[2,2,8192]{2,1,0:T(2,128)(2,1)S(1)} %pad_maximum_fusion.3), channel_id=1, source_target_pairs={{0,16},{1,17},{2,18},{3,19},{4,12},{5,13},{6,14},{7,15},{8,24},{9,... | collective-permute-start | bytes 196616 | tf_op jit(solution)/shard_map/ppermute | solution.py:41
  23.3 0.0 collective-permute-done.1
  23.3 0.1 pad_maximum_fusion.stored
  23.4 0.1 collective-permute-start.8
  23.5 0.6 %collective-permute-start.2 = (bf16[4,26,2048]{2,1,0:T(8,128)(2,1)S(1)}, bf16[4,26,2048]{2,1,0:T(8,128)(2,1)S(1)}, u32[]{:S(2)}, u32[]{:S(2)}) collective-permute-start(bf16[4,26,2048]{2,1,0:T(8,128)(2,1)S(1)} %pad_maximum_fusion.stored), channel_id=1, source_target_pairs={{0,4},{1,5},{2,6},{3,7},{4,0},{5,1},{6,2},{7,3},{8,12},{9,13},{10,... | collective-permute-start | bytes 1277960 | tf_op jit(solution)/shard_map/ppermute | solution.py:41
  24.0 0.6 %collective-permute-done.8 = bf16[4,26,256]{2,1,0:T(8,128)(2,1)S(1)} collective-permute-done((bf16[4,26,256]{2,1,0:T(8,128)(2,1)S(1)}, bf16[4,26,256]{2,1,0:T(8,128)(2,1)S(1)}, u32[]{:S(2)}, u32[]{:S(2)}) %collective-permute-start.8) | collective-permute-done | bytes 53280 | tf_op jit(solution)/shard_map/ppermute | solution.py:41
  24.7 3.0 %collective-permute-start.9 = (bf16[8,26,256]{2,1,0:T(8,128)(2,1)S(1)}, bf16[8,26,256]{2,1,0:T(8,128)(2,1)S(1)}, u32[]{:S(2)}, u32[]{:S(2)}) collective-permute-start(bf16[8,26,256]{2,1,0:T(8,128)(2,1)S(1)} %pad_maximum_fusion.2.refs_0_), channel_id=1, source_target_pairs={{0,2},{1,3},{2,0},{3,1},{4,5},{5,4},{6,7},{7,6},{8,10},{9,11},{10,... | collective-permute-start | bytes 319496 | tf_op jit(solution)/shard_map/ppermute | solution.py:41
  27.7 0.0 collective-permute-done.6
  27.7 0.1 constant_dynamic-update-slice_fusion.cur
  27.7 0.1 collective-permute-start.7
  27.8 2.7 %collective-permute-start.10 = (bf16[8,26,256]{2,1,0:T(8,128)(2,1)S(1)}, bf16[8,26,256]{2,1,0:T(8,128)(2,1)S(1)}, u32[]{:S(2)}, u32[]{:S(2)}) collective-permute-start(bf16[8,26,256]{2,1,0:T(8,128)(2,1)S(1)} %pad_maximum_fusion.2.refs_0_), channel_id=1, source_target_pairs={{0,1},{1,0},{2,3},{3,2},{4,6},{5,7},{6,4},{7,5},{8,9},{9,8},{10,11... | collective-permute-start | bytes 319496 | tf_op jit(solution)/shard_map/ppermute | solution.py:41
  30.5 0.3 collective-permute-done.9.refs_1_
  30.7 4.7 %collective-permute-start.11 = (bf16[8,26,256]{2,1,0:T(8,128)(2,1)S(1)}, bf16[8,26,256]{2,1,0:T(8,128)(2,1)S(1)}, u32[]{:S(2)}, u32[]{:S(2)}) collective-permute-start(bf16[8,26,256]{2,1,0:T(8,128)(2,1)S(1)} %collective-permute-done.9.refs_1_), channel_id=1, source_target_pairs={{0,1},{1,0},{2,3},{3,2},{4,6},{5,7},{6,4},{7,5},{8,9},{9,8},{10,11... | collective-permute-start | bytes 319496 | tf_op jit(solution)/shard_map/ppermute | solution.py:41
  35.4 0.0 collective-permute-done.10.refs_2_
  35.4 0.0 collective-permute-done.7.moved
  35.5 0.0 collective-permute-done.2.near
  35.5 1.9 %gram.1 = (bf16[2048,1024]{1,0:T(8,128)(2,1)}, bf16[256,2048]{1,0:T(8,128)(2,1)S(1)}, bf16[8,256,256]{2,1,0:T(8,128)(2,1)S(1)}) custom-call(bf16[4,26,2048]{2,1,0:T(8,128)(2,1)S(1)} %pad_maximum_fusion.stored, bf16[4,26,2048]{2,1,0:T(8,128)(2,1)S(1)} %collective-permute-done.2.near, bf16[4,2,8192]{2,1,0:T(2,128)(2,1)S(1)} %constant_dynamic-update-slice_fusion.cur, ...), custom_call_target="tpu_custom_call" | custom-call | flops 805306368 | bytes 3145728 | tf_op jit(solution)/shard_map/gram/pallas_call | solution.py:258
  37.3 1.9 %collective-permute-done.11.cols = bf16[8,26,256]{2,1,0:T(8,128)(2,1)S(1)} collective-permute-done((bf16[8,26,256]{2,1,0:T(8,128)(2,1)S(1)}, bf16[8,26,256]{2,1,0:T(8,128)(2,1)S(1)}, u32[]{:S(2)}, u32[]{:S(2)}) %collective-permute-start.11) | collective-permute-done | bytes 106528 | tf_op jit(solution)/shard_map/ppermute | solution.py:41
  39.2 1.5 %last.1 = bf16[2048,1024]{1,0:T(8,128)(2,1)} custom-call(bf16[256,2048]{1,0:T(8,128)(2,1)S(1)} %get-tuple-element.12.left, bf16[8,256,256]{2,1,0:T(8,128)(2,1)S(1)} %get-tuple-element.13.held, bf16[4,2,8192]{2,1,0:T(2,128)(2,1)S(1)} %constant_dynamic-update-slice_fusion.cur, ...), custom_call_target="tpu_custom_call", output_to_operand_aliasing={{}: (5, {})} | custom-call | flops 268435456 | bytes 1048576 | tf_op jit(solution)/shard_map/last/pallas_call | solution.py:272
  (7 shorter events, 0.2 us)
Async XLA Ops:
  0.0 14.1 %collective-permute-start = (bf16[26,2048]{1,0:T(8,128)(2,1)}, bf16[26,2048]{1,0:T(8,128)(2,1)S(1)}, u32[]{:S(2)}, u32[]{:S(2)}) collective-permute-start(bf16[26,2048]{1,0:T(8,128)(2,1)} %stored.1), channel_id=1, source_target_pairs={{0,8},{1,9},{2,10},{3,11},{4,20},{5,21},{6,22},{7,23},{8,0},{9,1},... | collective-permute-start | bytes 319496 | tf_op jit(solution)/shard_map/ppermute | solution.py:41
  5.9 5.7 %collective-permute-start.3 = (f32[256,128]{1,0:T(8,128)S(1)}, f32[256,128]{1,0:T(8,128)S(1)}, u32[]{:S(2)}, u32[]{:S(2)}) collective-permute-start(f32[256,128]{1,0:T(8,128)S(1)} %get-tuple-element.11), channel_id=1, source_target_pairs={{0,1},{1,0},{2,3},{3,2},{4,6},{5,7},{6,4},{7,5},{8,9},{9,8},{10,11... | collective-permute-start | bytes 393224 | tf_op jit(solution)/shard_map/ppermute | solution.py:41
  11.6 5.9 %collective-permute-start.4 = (f32[256,128]{1,0:T(8,128)S(1)}, f32[256,128]{1,0:T(8,128)S(1)}, u32[]{:S(2)}, u32[]{:S(2)}) collective-permute-start(f32[256,128]{1,0:T(8,128)S(1)} %add.9.own), channel_id=1, source_target_pairs={{0,2},{1,3},{2,0},{3,1},{4,5},{5,4},{6,7},{7,6},{8,10},{9,11},{10,... | collective-permute-start | bytes 393224 | tf_op jit(solution)/shard_map/ppermute | solution.py:41
  14.1 9.1 %collective-permute-start.1 = (bf16[2,26,2048]{2,1,0:T(8,128)(2,1)S(1)}, bf16[2,26,2048]{2,1,0:T(8,128)(2,1)S(1)}, u32[]{:S(2)}, u32[]{:S(2)}) collective-permute-start(bf16[2,26,2048]{2,1,0:T(8,128)(2,1)S(1)} %pad_maximum_fusion.1), channel_id=1, source_target_pairs={{0,16},{1,17},{2,18},{3,19},{4,12},{5,13},{6,14},{7,15},{8,24},{9,... | collective-permute-start | bytes 638984 | tf_op jit(solution)/shard_map/ppermute | solution.py:41
  18.0 4.0 %collective-permute-start.5 = (bf16[1,2,8192]{2,1,0:T(2,128)(2,1)S(1)}, bf16[1,2,8192]{2,1,0:T(2,128)(2,1)S(1)}, u32[]{:S(2)}, u32[]{:S(2)}) collective-permute-start(bf16[1,2,8192]{2,1,0:T(2,128)(2,1)S(1)} %reshape.13), channel_id=1, source_target_pairs={{0,8},{1,9},{2,10},{3,11},{4,20},{5,21},{6,22},{7,23},{8,0},{9,1},... | collective-permute-start | bytes 98312 | tf_op jit(solution)/shard_map/ppermute | solution.py:41
  22.1 5.6 %collective-permute-start.6 = (bf16[2,2,8192]{2,1,0:T(2,128)(2,1)S(1)}, bf16[2,2,8192]{2,1,0:T(2,128)(2,1)S(1)}, u32[]{:S(2)}, u32[]{:S(2)}) collective-permute-start(bf16[2,2,8192]{2,1,0:T(2,128)(2,1)S(1)} %pad_maximum_fusion.3), channel_id=1, source_target_pairs={{0,16},{1,17},{2,18},{3,19},{4,12},{5,13},{6,14},{7,15},{8,24},{9,... | collective-permute-start | bytes 196616 | tf_op jit(solution)/shard_map/ppermute | solution.py:41
  23.4 1.3 %collective-permute-start.8 = (bf16[4,26,256]{2,1,0:T(8,128)(2,1)S(1)}, bf16[4,26,256]{2,1,0:T(8,128)(2,1)S(1)}, u32[]{:S(2)}, u32[]{:S(2)}) collective-permute-start(bf16[4,26,256]{2,1,0:T(8,128)(2,1)S(1)} %get-tuple-element.16), channel_id=1, source_target_pairs={{0,4},{1,5},{2,6},{3,7},{4,0},{5,1},{6,2},{7,3},{8,12},{9,13},{10,... | collective-permute-start | bytes 159752 | tf_op jit(solution)/shard_map/ppermute | solution.py:41
  23.5 12.0 %collective-permute-start.2 = (bf16[4,26,2048]{2,1,0:T(8,128)(2,1)S(1)}, bf16[4,26,2048]{2,1,0:T(8,128)(2,1)S(1)}, u32[]{:S(2)}, u32[]{:S(2)}) collective-permute-start(bf16[4,26,2048]{2,1,0:T(8,128)(2,1)S(1)} %pad_maximum_fusion.stored), channel_id=1, source_target_pairs={{0,4},{1,5},{2,6},{3,7},{4,0},{5,1},{6,2},{7,3},{8,12},{9,13},{10,... | collective-permute-start | bytes 1277960 | tf_op jit(solution)/shard_map/ppermute | solution.py:41
  24.7 6.0 %collective-permute-start.9 = (bf16[8,26,256]{2,1,0:T(8,128)(2,1)S(1)}, bf16[8,26,256]{2,1,0:T(8,128)(2,1)S(1)}, u32[]{:S(2)}, u32[]{:S(2)}) collective-permute-start(bf16[8,26,256]{2,1,0:T(8,128)(2,1)S(1)} %pad_maximum_fusion.2.refs_0_), channel_id=1, source_target_pairs={{0,2},{1,3},{2,0},{3,1},{4,5},{5,4},{6,7},{7,6},{8,10},{9,11},{10,... | collective-permute-start | bytes 319496 | tf_op jit(solution)/shard_map/ppermute | solution.py:41
  27.7 7.7 %collective-permute-start.7 = (bf16[4,2,8192]{2,1,0:T(2,128)(2,1)S(1)}, bf16[4,2,8192]{2,1,0:T(2,128)(2,1)S(1)}, u32[]{:S(2)}, u32[]{:S(2)}) collective-permute-start(bf16[4,2,8192]{2,1,0:T(2,128)(2,1)S(1)} %constant_dynamic-update-slice_fusion.cur), channel_id=1, source_target_pairs={{0,4},{1,5},{2,6},{3,7},{4,0},{5,1},{6,2},{7,3},{8,12},{9,13},{10,... | collective-permute-start | bytes 393224 | tf_op jit(solution)/shard_map/ppermute | solution.py:41
  27.8 7.6 %collective-permute-start.10 = (bf16[8,26,256]{2,1,0:T(8,128)(2,1)S(1)}, bf16[8,26,256]{2,1,0:T(8,128)(2,1)S(1)}, u32[]{:S(2)}, u32[]{:S(2)}) collective-permute-start(bf16[8,26,256]{2,1,0:T(8,128)(2,1)S(1)} %pad_maximum_fusion.2.refs_0_), channel_id=1, source_target_pairs={{0,1},{1,0},{2,3},{3,2},{4,6},{5,7},{6,4},{7,5},{8,9},{9,8},{10,11... | collective-permute-start | bytes 319496 | tf_op jit(solution)/shard_map/ppermute | solution.py:41
  30.7 8.5 %collective-permute-start.11 = (bf16[8,26,256]{2,1,0:T(8,128)(2,1)S(1)}, bf16[8,26,256]{2,1,0:T(8,128)(2,1)S(1)}, u32[]{:S(2)}, u32[]{:S(2)}) collective-permute-start(bf16[8,26,256]{2,1,0:T(8,128)(2,1)S(1)} %collective-permute-done.9.refs_1_), channel_id=1, source_target_pairs={{0,1},{1,0},{2,3},{3,2},{4,6},{5,7},{6,4},{7,5},{8,9},{9,8},{10,11... | collective-permute-start | bytes 319496 | tf_op jit(solution)/shard_map/ppermute | solution.py:41

commit v8 on v7

--- a/solution.py
+++ b/solution.py
@@ -95,12 +95,27 @@
     )(*args)
 
 
-def current_kernel(live, own, other, out):
-    examples, half, width = out.shape
+def current_kernel(rounds, live, own, other, out):
+    examples, picked, width = out.shape
     total = own[...] + other[...]
     rows = total.shape[0] // 2
     slots = rows // examples
+    half = width // LAYERS
     lane = lax.broadcasted_iota(jnp.int32, (half, width), 1)
+    q, i = lax.axis_index("tensor"), lax.axis_index("dp")
+    tensor_count, dp_count = lax.axis_size("tensor"), lax.axis_size("dp")
+    share = half // tensor_count
+    each, per_index = share // dp_count, half // dp_count
+    place = lax.broadcasted_iota(jnp.int32, (picked, half), 0)
+    later = jnp.maximum(place - share, 0)
+    target, within = later // per_index, later % per_index
+    index = jnp.zeros_like(place) + i
+    for n, pair in enumerate(rounds):
+        bit = jnp.where(i % 2 == 0, *pair)
+        index = index ^ (((target >> (len(rounds) - 1 - n)) & 1) * bit)
+    there = within // each * share + index * each + within % each
+    vector = jnp.where(place < share, q * share + place, there)
+    pick = (vector == lax.broadcasted_iota(jnp.int32, (picked, half), 1)).astype(out.dtype)
     for e in range(examples):
         left = total[rows + e * slots : rows + (e + 1) * slots]
         right = total[e * slots : (e + 1) * slots]
@@ -113,19 +128,19 @@
             preferred_element_type=jnp.float32,
         )
         mine = jnp.where(lane < half, both[:half], both[half:])
-        out[e] = (mine * (1.0 / math.sqrt(slots))).astype(out.dtype)
-
-
-def current_rows(lengths, own, other, proj_width):
+        mine = (mine * (1.0 / math.sqrt(slots))).astype(out.dtype)
+        out[e] = matmul(pick, mine).astype(out.dtype)
+
+
+def current_rows(lengths, own, other, proj_width, rounds):
     examples = lengths.shape[0]
     rows, width = own.shape[0] // 2, own.shape[1]
+    picked = proj_width // lax.axis_size("tensor") + proj_width
     position = lax.broadcasted_iota(jnp.int32, (examples, rows // examples, width), 1)
     live = (position < lengths[:, None, None]).astype(jnp.float32).reshape(rows, width)
     return pl.pallas_call(
-        current_kernel,
-        out_shape=jax.ShapeDtypeStruct(
-            (examples, proj_width, LAYERS * proj_width), jnp.bfloat16
-        ),
+        functools.partial(current_kernel, rounds),
+        out_shape=jax.ShapeDtypeStruct((examples, picked, width), jnp.bfloat16),
         in_specs=[pl.BlockSpec(memory_space=pltpu.VMEM)] * 3,
         out_specs=pl.BlockSpec(memory_space=pltpu.VMEM),
         cost_estimate=pl.CostEstimate(
@@ -153,9 +168,9 @@
     half, new = cur.shape[:2]
     slot = right.shape[0] // pieces
     q, i = lax.axis_index("tensor"), lax.axis_index("dp")
-    quarter = cur.shape[-1] // lax.axis_size("tensor")
+    quarter = sub * lax.axis_size("dp")
     block = q ^ jnp.where(i % 2 == 0, *pair)
-    source = pl.ds(pl.multiple_of(block * quarter + i * sub, sub), sub)
+    source = pl.ds(pl.multiple_of(quarter + block * sub, sub), sub)
     to = slice(k * sub, (k + 1) * sub)
     for p in range(pieces):
         base = p * slot
@@ -187,15 +202,13 @@
     half, old, quarter = stored.shape
     pieces, new = 2 * half, cur.shape[1]
     slot = left.shape[0] // pieces
-    q = lax.axis_index("tensor")
-    place = pl.ds(pl.multiple_of(q * quarter, quarter), quarter)
     left[...] = jnp.zeros_like(left)
     right[...] = jnp.zeros_like(right)
     for p in range(pieces):
         base = p * slot
         here, fresh = (stored, cur) if p < half else (near, moved)
         left[base : base + old, :] = here[p % half]
-        left[base + old : base + old + new, :] = fresh[p % half, :, place]
+        left[base + old : base + old + new, :] = fresh[p % half, :, :quarter]
     places = [
         fill(right, k, pair, cols[k], cur, moved, old) for k, pair in enumerate(offsets)
     ]
@@ -282,6 +295,10 @@
     )(left, held, cur, moved, cols[-1], begun)
 
 
+def kept(cur, quarter):
+    return (quarter + cur.shape[2]) // 2
+
+
 def local(
     inputs_x,
     hidden,
@@ -303,6 +320,7 @@
     i = lax.axis_index("dp")
     links = bits_of(dp_count)[1:]
     dp_rounds = [*zip(links, turned(links), strict=True), (1, 1)]
+    fresh_rounds = [(bit, bit) for bit in links] + [(1, 1)]
     tensor_bits = bits_of(tensor_count)
     tensor_rounds = [*zip(tensor_bits, turned(tensor_bits), strict=True)]
 
@@ -338,12 +356,14 @@
         other = swap(total, "tensor", *bits)
         if n < len(tensor_rounds) - 1:
             total = total + other
-    cur = current_rows(lengths, total, other, proj_width)
-    cur = cur.reshape(1, examples, proj_width * LAYERS * proj_width)
-    for n, bits in enumerate(dp_rounds):
-        moved = swap(cur, "dp", *bits)
+    cur = current_rows(lengths, total, other, proj_width, fresh_rounds)
+    cur = cur.reshape(1, examples, cur.shape[1] * cur.shape[2])
+    give = jnp.concatenate([cur[..., :quarter], cur[..., kept(cur, quarter) :]], axis=2)
+    for n, bits in enumerate(fresh_rounds):
+        moved = swap(give, "dp", *bits)
         if n < len(dp_rounds) - 1:
-            cur = jnp.concatenate([cur, moved], axis=0)
+            cur = jnp.concatenate([cur[..., : kept(cur, quarter)], moved], axis=0)
+            give = jnp.concatenate([cur[..., :quarter], cur[..., kept(cur, quarter) :]], axis=2)
     product = gram(rows, near, cols, cur, moved, offsets)
     return product.reshape(quarter, 1, tensor_count * sub_width)
 

time: 41.3 us -> 44.3 us (1.073)
  starting transfers between devices: 21.6 us -> 23.9 us
  waiting for transfers between devices: 11.1 us -> 11.7 us
    ppermute x12, starting transfers between devices: 21.6 us -> 23.9 us  [swap(): return lax.ppermute(value, ('dp', 'tensor'), pairs)]
    ppermute x12, waiting for transfers between devices: 11.1 us -> 11.7 us  [swap(): return lax.ppermute(value, ('dp', 'tensor'), pairs)]
  transfers between devices with their start and end apart: 12 -> 12, of which waited for: 6 -> 7; matrix products, arithmetic and copies ran while one was open for 3% -> 3% of each run, Pallas kernels for 13% -> 6%
where the time goes in v8:
time: 44.3 us; the launch traced here: 44.1 us
  starting transfers between devices  23.9 us (54%)
  waiting for transfers between devices  11.7 us (26%)
  Pallas kernels  6.97 us (16%)
  other arithmetic  1.18 us (3%)
    ppermute x12, starting transfers between devices, swap(): return lax.ppermute(value, ('dp', 'tensor'), pairs)  23.9 us
    ppermute x12, waiting for transfers between devices, swap(): return lax.ppermute(value, ('dp', 'tensor'), pairs)  11.7 us
    pallas_call x1, Pallas kernels, project(): pl.pallas_call(project_kernel, out_shape=(jax.ShapeDtypeStruct((2 * rows,...  2.97 us
    pallas_call x1, Pallas kernels, gram(): pl.pallas_call(functools.partial(gram_kernel, scale, offsets[:-1]), out_s...  1.84 us
    pallas_call x1, Pallas kernels, gram(): pl.pallas_call(functools.partial(last_kernel, scale, offsets[-2:]), out_s...  1.48 us
  transfers between devices with their start and end apart: 12, of which 7 were waited for; matrix products, arithmetic and copies ran while one was open for 3% of the time, Pallas kernels for 6%

profile of v8, /device:TPU:0, one launch (start us, length us, event | category | flops | bytes accessed | tf_op | source)
XLA Modules:
  0.0 44.1 jit_solution(17507589630816701776)
XLA Ops:
  0.0 3.0 %project.1 = (f32[256,128]{1,0:T(8,128)S(1)}, bf16[26,2048]{1,0:T(8,128)(2,1)S(1)}) custom-call(bf16[128,1024]{1,0:T(8,128)(2,1)} %x.1, bf16[128,3584]{1,0:T(8,128)(2,1)} %h.1, bf16[128,3584]{1,0:T(8,128)(2,1)} %gu.1, bf16[128,1024]{1,0:T(8,128)(2,1)} %gd.1, bf16[64,1024]{1,0:T(8,128)(2,1)} %bitcast.13, bf16[64,3584]{1,0:T(8,128)(2,1)} %bitcast.11, ...), custom_call_target="tpu_custom_call" | custom-call | flops 150994944 | bytes 3645440 | tf_op jit(solution)/shard_map/project/pallas_call | solution.py:78
  3.0 3.1 %collective-permute-start.3 = (f32[256,128]{1,0:T(8,128)S(1)}, f32[256,128]{1,0:T(8,128)S(1)}, u32[]{:S(2)}, u32[]{:S(2)}) collective-permute-start(f32[256,128]{1,0:T(8,128)S(1)} %get-tuple-element.11), channel_id=1, source_target_pairs={{0,1},{1,0},{2,3},{3,2},{4,6},{5,7},{6,4},{7,5},{8,9},{9,8},{10,11... | collective-permute-start | bytes 393224 | tf_op jit(solution)/shard_map/ppermute | solution.py:41
  6.1 1.5 %collective-permute-start = (bf16[26,2048]{1,0:T(8,128)(2,1)}, bf16[26,2048]{1,0:T(8,128)(2,1)S(1)}, u32[]{:S(2)}, u32[]{:S(2)}) collective-permute-start(bf16[26,2048]{1,0:T(8,128)(2,1)} %stored.1), channel_id=1, source_target_pairs={{0,8},{1,9},{2,10},{3,11},{4,20},{5,21},{6,22},{7,23},{8,0},{9,1},... | collective-permute-start | bytes 319496 | tf_op jit(solution)/shard_map/ppermute | solution.py:41
  7.6 2.6 %collective-permute-done.3 = f32[256,128]{1,0:T(8,128)S(1)} collective-permute-done((f32[256,128]{1,0:T(8,128)S(1)}, f32[256,128]{1,0:T(8,128)S(1)}, u32[]{:S(2)}, u32[]{:S(2)}) %collective-permute-start.3) | collective-permute-done | bytes 131104 | tf_op jit(solution)/shard_map/ppermute | solution.py:41
  10.2 2.3 %collective-permute-start.4 = (f32[256,128]{1,0:T(8,128)S(1)}, f32[256,128]{1,0:T(8,128)S(1)}, u32[]{:S(2)}, u32[]{:S(2)}) collective-permute-start(f32[256,128]{1,0:T(8,128)S(1)} %add.9.own), channel_id=1, source_target_pairs={{0,2},{1,3},{2,0},{3,1},{4,5},{5,4},{6,7},{7,6},{8,10},{9,11},{10,... | collective-permute-start | bytes 393224 | tf_op jit(solution)/shard_map/ppermute | solution.py:41
  12.5 0.7 %compare_convert_fusion = f32[2,64]{1,0:T(2,128)S(1)} fusion(s32[2]{0:T(128)} %param.18), kind=kLoop, calls=%fused_computation.23 | loop fusion | flops 256 | bytes 520 | tf_op jit(solution)/shard_map/convert_element_type | solution.py:140
  13.2 0.1 reshape.15
  13.3 2.8 %collective-permute-done.4.other = f32[256,128]{1,0:T(8,128)S(1)} collective-permute-done((f32[256,128]{1,0:T(8,128)S(1)}, f32[256,128]{1,0:T(8,128)S(1)}, u32[]{:S(2)}, u32[]{:S(2)}) %collective-permute-start.4) | collective-permute-done | bytes 131104 | tf_op jit(solution)/shard_map/ppermute | solution.py:41
  16.1 0.1 iota.10.live
  16.2 0.7 %current.1 = bf16[2,80,128]{2,1,0:T(8,128)(2,1)S(1)} custom-call(f32[128,128]{1,0:T(8,128)S(1)} %iota.10.live, f32[256,128]{1,0:T(8,128)S(1)} %add.9.own, f32[256,128]{1,0:T(8,128)S(1)} %collective-permute-done.4.other), custom_call_target="tpu_custom_call" | custom-call | flops 4194304 | bytes 262144 | tf_op jit(solution)/shard_map/current/pallas_call | solution.py:141
  17.0 2.0 %collective-permute-start.5 = (bf16[1,2,6144]{2,1,0:T(2,128)(2,1)S(1)}, bf16[1,2,6144]{2,1,0:T(2,128)(2,1)S(1)}, u32[]{:S(2)}, u32[]{:S(2)}) collective-permute-start(bf16[1,2,6144]{2,1,0:T(2,128)(2,1)S(1)} %pad_maximum_fusion.5), channel_id=1, source_target_pairs={{0,8},{1,9},{2,10},{3,11},{4,12},{5,13},{6,14},{7,15},{8,0},{9,1},... | collective-permute-start | bytes 73736 | tf_op jit(solution)/shard_map/ppermute | solution.py:41
  19.0 0.0 collective-permute-done
  19.0 1.6 %collective-permute-start.1 = (bf16[2,26,2048]{2,1,0:T(8,128)(2,1)S(1)}, bf16[2,26,2048]{2,1,0:T(8,128)(2,1)S(1)}, u32[]{:S(2)}, u32[]{:S(2)}) collective-permute-start(bf16[2,26,2048]{2,1,0:T(8,128)(2,1)S(1)} %pad_maximum_fusion.1), channel_id=1, source_target_pairs={{0,16},{1,17},{2,18},{3,19},{4,12},{5,13},{6,14},{7,15},{8,24},{9,... | collective-permute-start | bytes 638984 | tf_op jit(solution)/shard_map/ppermute | solution.py:41
  20.7 0.5 %collective-permute-done.5 = bf16[1,2,6144]{2,1,0:T(2,128)(2,1)S(1)} collective-permute-done((bf16[1,2,6144]{2,1,0:T(2,128)(2,1)S(1)}, bf16[1,2,6144]{2,1,0:T(2,128)(2,1)S(1)}, u32[]{:S(2)}, u32[]{:S(2)}) %collective-permute-start.5) | collective-permute-done | bytes 24608 | tf_op jit(solution)/shard_map/ppermute | solution.py:41
  21.2 0.1 fusion.3
  21.2 2.1 %collective-permute-start.6 = (bf16[2,2,4096]{2,1,0:T(2,128)(2,1)S(1)}, bf16[2,2,4096]{2,1,0:T(2,128)(2,1)S(1)}, u32[]{:S(2)}, u32[]{:S(2)}) collective-permute-start(bf16[2,2,4096]{2,1,0:T(2,128)(2,1)S(1)} %get-tuple-element.18), channel_id=1, source_target_pairs={{0,16},{1,17},{2,18},{3,19},{4,20},{5,21},{6,22},{7,23},{8,24},{9,... | collective-permute-start | bytes 98312 | tf_op jit(solution)/shard_map/ppermute | solution.py:41
  23.3 2.2 %collective-permute-done.1 = bf16[2,26,2048]{2,1,0:T(8,128)(2,1)S(1)} collective-permute-done((bf16[2,26,2048]{2,1,0:T(8,128)(2,1)S(1)}, bf16[2,26,2048]{2,1,0:T(8,128)(2,1)S(1)}, u32[]{:S(2)}, u32[]{:S(2)}) %collective-permute-start.1) | collective-permute-done | bytes 213024 | tf_op jit(solution)/shard_map/ppermute | solution.py:41
  25.5 0.1 pad_maximum_fusion.stored
  25.5 0.1 collective-permute-start.2
  25.7 0.5 %collective-permute-start.8 = (bf16[4,26,256]{2,1,0:T(8,128)(2,1)S(1)}, bf16[4,26,256]{2,1,0:T(8,128)(2,1)S(1)}, u32[]{:S(2)}, u32[]{:S(2)}) collective-permute-start(bf16[4,26,256]{2,1,0:T(8,128)(2,1)S(1)} %get-tuple-element.16), channel_id=1, source_target_pairs={{0,4},{1,5},{2,6},{3,7},{4,0},{5,1},{6,2},{7,3},{8,12},{9,13},{10,... | collective-permute-start | bytes 159752 | tf_op jit(solution)/shard_map/ppermute | solution.py:41
  26.2 0.0 collective-permute-done.6
  26.3 1.3 %collective-permute-done.8 = bf16[4,26,256]{2,1,0:T(8,128)(2,1)S(1)} collective-permute-done((bf16[4,26,256]{2,1,0:T(8,128)(2,1)S(1)}, bf16[4,26,256]{2,1,0:T(8,128)(2,1)S(1)}, u32[]{:S(2)}, u32[]{:S(2)}) %collective-permute-start.8) | collective-permute-done | bytes 53280 | tf_op jit(solution)/shard_map/ppermute | solution.py:41
  27.6 1.8 %collective-permute-start.9 = (bf16[8,26,256]{2,1,0:T(8,128)(2,1)S(1)}, bf16[8,26,256]{2,1,0:T(8,128)(2,1)S(1)}, u32[]{:S(2)}, u32[]{:S(2)}) collective-permute-start(bf16[8,26,256]{2,1,0:T(8,128)(2,1)S(1)} %pad_maximum_fusion.2.refs_0_), channel_id=1, source_target_pairs={{0,2},{1,3},{2,0},{3,1},{4,5},{5,4},{6,7},{7,6},{8,10},{9,11},{10,... | collective-permute-start | bytes 319496 | tf_op jit(solution)/shard_map/ppermute | solution.py:41
  29.5 0.1 collective-permute-start.7
  29.6 2.9 %collective-permute-start.10 = (bf16[8,26,256]{2,1,0:T(8,128)(2,1)S(1)}, bf16[8,26,256]{2,1,0:T(8,128)(2,1)S(1)}, u32[]{:S(2)}, u32[]{:S(2)}) collective-permute-start(bf16[8,26,256]{2,1,0:T(8,128)(2,1)S(1)} %pad_maximum_fusion.2.refs_0_), channel_id=1, source_target_pairs={{0,1},{1,0},{2,3},{3,2},{4,6},{5,7},{6,4},{7,5},{8,9},{9,8},{10,11... | collective-permute-start | bytes 319496 | tf_op jit(solution)/shard_map/ppermute | solution.py:41
  32.5 1.3 %collective-permute-done.9.refs_1_ = bf16[8,26,256]{2,1,0:T(8,128)(2,1)S(1)} collective-permute-done((bf16[8,26,256]{2,1,0:T(8,128)(2,1)S(1)}, bf16[8,26,256]{2,1,0:T(8,128)(2,1)S(1)}, u32[]{:S(2)}, u32[]{:S(2)}) %collective-permute-start.9) | collective-permute-done | bytes 106528 | tf_op jit(solution)/shard_map/ppermute | solution.py:41
  33.8 5.9 %collective-permute-start.11 = (bf16[8,26,256]{2,1,0:T(8,128)(2,1)S(1)}, bf16[8,26,256]{2,1,0:T(8,128)(2,1)S(1)}, u32[]{:S(2)}, u32[]{:S(2)}) collective-permute-start(bf16[8,26,256]{2,1,0:T(8,128)(2,1)S(1)} %collective-permute-done.9.refs_1_), channel_id=1, source_target_pairs={{0,1},{1,0},{2,3},{3,2},{4,6},{5,7},{6,4},{7,5},{8,9},{9,8},{10,11... | collective-permute-start | bytes 319496 | tf_op jit(solution)/shard_map/ppermute | solution.py:41
  39.7 0.1 pad_maximum_fusion.4.cur
  39.8 0.0 collective-permute-done.7.moved
  39.8 0.0 collective-permute-done.10.refs_2_
  39.8 0.0 collective-permute-done.2.near
  39.8 1.8 %gram.1 = (bf16[2048,1024]{1,0:T(8,128)(2,1)}, bf16[256,2048]{1,0:T(8,128)(2,1)S(1)}, bf16[8,256,256]{2,1,0:T(8,128)(2,1)S(1)}) custom-call(bf16[4,26,2048]{2,1,0:T(8,128)(2,1)S(1)} %pad_maximum_fusion.stored, bf16[4,26,2048]{2,1,0:T(8,128)(2,1)S(1)} %collective-permute-done.2.near, bf16[4,2,4096]{2,1,0:T(2,128)(2,1)S(1)} %pad_maximum_fusion.4.cur, ...), custom_call_target="tpu_custom_call" | custom-call | flops 805306368 | bytes 3145728 | tf_op jit(solution)/shard_map/gram/pallas_call | solution.py:271
  41.7 1.0 %collective-permute-done.11.cols = bf16[8,26,256]{2,1,0:T(8,128)(2,1)S(1)} collective-permute-done((bf16[8,26,256]{2,1,0:T(8,128)(2,1)S(1)}, bf16[8,26,256]{2,1,0:T(8,128)(2,1)S(1)}, u32[]{:S(2)}, u32[]{:S(2)}) %collective-permute-start.11) | collective-permute-done | bytes 106528 | tf_op jit(solution)/shard_map/ppermute | solution.py:41
  42.6 1.5 %last.1 = bf16[2048,1024]{1,0:T(8,128)(2,1)} custom-call(bf16[256,2048]{1,0:T(8,128)(2,1)S(1)} %get-tuple-element.12.left, bf16[8,256,256]{2,1,0:T(8,128)(2,1)S(1)} %get-tuple-element.13.held, bf16[4,2,4096]{2,1,0:T(2,128)(2,1)S(1)} %pad_maximum_fusion.4.cur, bf16[4,2,3072]{2,1,0:T(2,128)(2,1)S(1)} %collective-permute-done.7.moved, ...), custom_call_target="tpu_custom_call", output_to_operand_aliasing={{}: (5, {})} | custom-call | flops 268435456 | bytes 1048576 | tf_op jit(solution)/shard_map/last/pallas_call | solution.py:285
  (13 shorter events, 0.3 us)
Async XLA Ops:
  3.0 7.2 %collective-permute-start.3 = (f32[256,128]{1,0:T(8,128)S(1)}, f32[256,128]{1,0:T(8,128)S(1)}, u32[]{:S(2)}, u32[]{:S(2)}) collective-permute-start(f32[256,128]{1,0:T(8,128)S(1)} %get-tuple-element.11), channel_id=1, source_target_pairs={{0,1},{1,0},{2,3},{3,2},{4,6},{5,7},{6,4},{7,5},{8,9},{9,8},{10,11... | collective-permute-start | bytes 393224 | tf_op jit(solution)/shard_map/ppermute | solution.py:41
  6.1 12.9 %collective-permute-start = (bf16[26,2048]{1,0:T(8,128)(2,1)}, bf16[26,2048]{1,0:T(8,128)(2,1)S(1)}, u32[]{:S(2)}, u32[]{:S(2)}) collective-permute-start(bf16[26,2048]{1,0:T(8,128)(2,1)} %stored.1), channel_id=1, source_target_pairs={{0,8},{1,9},{2,10},{3,11},{4,20},{5,21},{6,22},{7,23},{8,0},{9,1},... | collective-permute-start | bytes 319496 | tf_op jit(solution)/shard_map/ppermute | solution.py:41
  10.2 5.9 %collective-permute-start.4 = (f32[256,128]{1,0:T(8,128)S(1)}, f32[256,128]{1,0:T(8,128)S(1)}, u32[]{:S(2)}, u32[]{:S(2)}) collective-permute-start(f32[256,128]{1,0:T(8,128)S(1)} %add.9.own), channel_id=1, source_target_pairs={{0,2},{1,3},{2,0},{3,1},{4,5},{5,4},{6,7},{7,6},{8,10},{9,11},{10,... | collective-permute-start | bytes 393224 | tf_op jit(solution)/shard_map/ppermute | solution.py:41
  17.0 4.2 %collective-permute-start.5 = (bf16[1,2,6144]{2,1,0:T(2,128)(2,1)S(1)}, bf16[1,2,6144]{2,1,0:T(2,128)(2,1)S(1)}, u32[]{:S(2)}, u32[]{:S(2)}) collective-permute-start(bf16[1,2,6144]{2,1,0:T(2,128)(2,1)S(1)} %pad_maximum_fusion.5), channel_id=1, source_target_pairs={{0,8},{1,9},{2,10},{3,11},{4,12},{5,13},{6,14},{7,15},{8,0},{9,1},... | collective-permute-start | bytes 73736 | tf_op jit(solution)/shard_map/ppermute | solution.py:41
  19.0 6.4 %collective-permute-start.1 = (bf16[2,26,2048]{2,1,0:T(8,128)(2,1)S(1)}, bf16[2,26,2048]{2,1,0:T(8,128)(2,1)S(1)}, u32[]{:S(2)}, u32[]{:S(2)}) collective-permute-start(bf16[2,26,2048]{2,1,0:T(8,128)(2,1)S(1)} %pad_maximum_fusion.1), channel_id=1, source_target_pairs={{0,16},{1,17},{2,18},{3,19},{4,12},{5,13},{6,14},{7,15},{8,24},{9,... | collective-permute-start | bytes 638984 | tf_op jit(solution)/shard_map/ppermute | solution.py:41
  21.2 5.0 %collective-permute-start.6 = (bf16[2,2,4096]{2,1,0:T(2,128)(2,1)S(1)}, bf16[2,2,4096]{2,1,0:T(2,128)(2,1)S(1)}, u32[]{:S(2)}, u32[]{:S(2)}) collective-permute-start(bf16[2,2,4096]{2,1,0:T(2,128)(2,1)S(1)} %get-tuple-element.18), channel_id=1, source_target_pairs={{0,16},{1,17},{2,18},{3,19},{4,20},{5,21},{6,22},{7,23},{8,24},{9,... | collective-permute-start | bytes 98312 | tf_op jit(solution)/shard_map/ppermute | solution.py:41
  25.5 14.3 %collective-permute-start.2 = (bf16[4,26,2048]{2,1,0:T(8,128)(2,1)S(1)}, bf16[4,26,2048]{2,1,0:T(8,128)(2,1)S(1)}, u32[]{:S(2)}, u32[]{:S(2)}) collective-permute-start(bf16[4,26,2048]{2,1,0:T(8,128)(2,1)S(1)} %pad_maximum_fusion.stored), channel_id=1, source_target_pairs={{0,4},{1,5},{2,6},{3,7},{4,0},{5,1},{6,2},{7,3},{8,12},{9,13},{10,... | collective-permute-start | bytes 1277960 | tf_op jit(solution)/shard_map/ppermute | solution.py:41
  25.7 2.0 %collective-permute-start.8 = (bf16[4,26,256]{2,1,0:T(8,128)(2,1)S(1)}, bf16[4,26,256]{2,1,0:T(8,128)(2,1)S(1)}, u32[]{:S(2)}, u32[]{:S(2)}) collective-permute-start(bf16[4,26,256]{2,1,0:T(8,128)(2,1)S(1)} %get-tuple-element.16), channel_id=1, source_target_pairs={{0,4},{1,5},{2,6},{3,7},{4,0},{5,1},{6,2},{7,3},{8,12},{9,13},{10,... | collective-permute-start | bytes 159752 | tf_op jit(solution)/shard_map/ppermute | solution.py:41
  27.6 6.2 %collective-permute-start.9 = (bf16[8,26,256]{2,1,0:T(8,128)(2,1)S(1)}, bf16[8,26,256]{2,1,0:T(8,128)(2,1)S(1)}, u32[]{:S(2)}, u32[]{:S(2)}) collective-permute-start(bf16[8,26,256]{2,1,0:T(8,128)(2,1)S(1)} %pad_maximum_fusion.2.refs_0_), channel_id=1, source_target_pairs={{0,2},{1,3},{2,0},{3,1},{4,5},{5,4},{6,7},{7,6},{8,10},{9,11},{10,... | collective-permute-start | bytes 319496 | tf_op jit(solution)/shard_map/ppermute | solution.py:41
  29.5 10.3 %collective-permute-start.7 = (bf16[4,2,3072]{2,1,0:T(2,128)(2,1)S(1)}, bf16[4,2,3072]{2,1,0:T(2,128)(2,1)S(1)}, u32[]{:S(2)}, u32[]{:S(2)}) collective-permute-start(bf16[4,2,3072]{2,1,0:T(2,128)(2,1)S(1)} %pad_maximum_fusion.3), channel_id=1, source_target_pairs={{0,4},{1,5},{2,6},{3,7},{4,0},{5,1},{6,2},{7,3},{8,12},{9,13},{10,... | collective-permute-start | bytes 147464 | tf_op jit(solution)/shard_map/ppermute | solution.py:41
  29.6 10.2 %collective-permute-start.10 = (bf16[8,26,256]{2,1,0:T(8,128)(2,1)S(1)}, bf16[8,26,256]{2,1,0:T(8,128)(2,1)S(1)}, u32[]{:S(2)}, u32[]{:S(2)}) collective-permute-start(bf16[8,26,256]{2,1,0:T(8,128)(2,1)S(1)} %pad_maximum_fusion.2.refs_0_), channel_id=1, source_target_pairs={{0,1},{1,0},{2,3},{3,2},{4,6},{5,7},{6,4},{7,5},{8,9},{9,8},{10,11... | collective-permute-start | bytes 319496 | tf_op jit(solution)/shard_map/ppermute | solution.py:41
  33.8 8.8 %collective-permute-start.11 = (bf16[8,26,256]{2,1,0:T(8,128)(2,1)S(1)}, bf16[8,26,256]{2,1,0:T(8,128)(2,1)S(1)}, u32[]{:S(2)}, u32[]{:S(2)}) collective-permute-start(bf16[8,26,256]{2,1,0:T(8,128)(2,1)S(1)} %collective-permute-done.9.refs_1_), channel_id=1, source_target_pairs={{0,1},{1,0},{2,3},{3,2},{4,6},{5,7},{6,4},{7,5},{8,9},{9,8},{10,11... | collective-permute-start | bytes 319496 | tf_op jit(solution)/shard_map/ppermute | solution.py:41
